TPU v7x, 32 devices: a whole 2x2x4 slice. The times are simulated.
32 devices in a mesh: seg: 8 (over y, x, core), head: 4 (over z).
Axes of the slice: x: 2, y: 2, z: 4, core: 2. Of those that a mesh axis runs over, the one named last changes fastest.
Arguments:
- layer_input: bfloat16 [1, 4096, 2048], P(None, 'seg', 'head'), may hold values from -160 to 160, as said below
- w_qkv: bfloat16 [2048, 3, 1024], P(None, None, 'head'), may hold values from -3 to 3
- comp_weight: bfloat16 [3, 2, 1024], P(None, None, 'head'), may hold values from -2.5 to 2.5
- w_out: bfloat16 [1024, 2048], P('seg', 'head'), may hold values from -1.5 to 1.5
Outputs:
- attn_out: bfloat16 [1, 4096, 2048], P(None, 'seg', 'head')
Inputs may be any that keep to these rules, and one draw needn't show every extreme that they name: layer_input varies in scale from feature to feature and from token to token.
All inputs are finite; a program needn't handle non-finite values.
Results may differ from a plain program's by a relative error of at most 0.0089.
Values may be sent and summed in bfloat16 or wider, within the bound.
No kernel may reach another device: no remote copies, remote signals or barrier semaphores. Data moves between devices by JAX's collectives and lax.ppermute only.
A program may use at most 64 MiB of HBM per device.

v0:
```python
import math

import jax
import jax.numpy as jnp
from jax import lax
from jax.experimental import pallas as pl
from jax.experimental.pallas import tpu as pltpu
from jax.sharding import PartitionSpec as P


DH = 128
RATE = 3
BACK = 4
BF16 = jnp.bfloat16
F32 = jnp.float32
NEG = -1e30
VMEM_LIMIT = 14 * 1024 * 1024


def params():
    return pltpu.CompilerParams(vmem_limit_bytes=VMEM_LIMIT)


def vmem():
    return pl.BlockSpec(memory_space=pltpu.VMEM)


def ring_order(size):
    return list(range(size))


def around(block):
    order = ring_order(lax.axis_size("head"))
    route = [(a, b) for a, b in zip(order, order[1:] + order[:1])]
    return lax.ppermute(block, "head", route)


def passed_along(block, distance):
    size = lax.axis_size("seg")
    route = [(i, (i + distance) % size) for i in range(size)]
    return lax.ppermute(block, "seg", route)


def source_of(step, size):
    order = ring_order(size)
    z = lax.axis_index("head")
    found = jnp.int32(0)
    for here in range(size):
        found = jnp.where(z == here, order[(order.index(here) - step) % size], found)
    return found


def hbm():
    return pl.BlockSpec(memory_space=pltpu.HBM)


def call(body, outs, args, scratch=(), in_specs=None):
    return pl.pallas_call(
        body,
        out_shape=tuple(jax.ShapeDtypeStruct(s, d) for s, d in outs),
        in_specs=in_specs or [vmem()] * len(args),
        out_specs=tuple(vmem() for _ in outs),
        scratch_shapes=list(scratch),
        compiler_params=params(),
    )(*args)


def split(rows, starts, piece):
    def body(src, *refs):
        sems = refs[-1]
        copies = [
            pltpu.make_async_copy(src.at[pl.ds(at, piece), :], out, sems.at[i])
            for i, (at, out) in enumerate(zip(starts, refs))
        ]
        for copy in copies:
            copy.start()
        for copy in copies:
            copy.wait()

    outs = [((piece, rows.shape[1]), rows.dtype)] * len(starts)
    scratch = [pltpu.SemaphoreType.DMA((len(starts),))]
    return call(body, outs, [rows], scratch, [hbm()])


def join(one, two):
    n = one.shape[0]

    def body(one_ref, two_ref, out_ref):
        out_ref[:n, :] = one_ref[...]
        out_ref[n:, :] = two_ref[...]

    return call(body, [((2 * n, one.shape[1]), one.dtype)], [one, two])[0]


def weight_rows(w_ref, i, source, feats):
    start = pl.multiple_of(source * feats, feats)
    return w_ref[i, pl.ds(start, feats), :]


def moments(block):
    x = block.astype(F32)
    total = jnp.sum(x, axis=1, keepdims=True)
    off = x - total / x.shape[1]
    return total, jnp.sum(off * off, axis=1, keepdims=True)


def joined_moments(parts, feats):
    count = feats * len(parts)
    mean = sum(t for t, _ in parts) / count
    square = sum(q + feats * jnp.square(t / feats - mean) for t, q in parts)
    return mean, lax.rsqrt(square / count + 1e-05)


def project_sum(blocks, steps, w_ref, i):
    feats = blocks[0].shape[1]
    size = w_ref.shape[1] // feats
    acc = None
    for t, block in zip(steps, blocks):
        part = jnp.dot(
            block[...], weight_rows(w_ref, i, source_of(t, size), feats), preferred_element_type=F32
        )
        acc = part if acc is None else acc + part
    return acc


def fetch_weights(w3):
    n_kind, _, width = w3.shape

    def body(src, w_ref, sum_ref, sems):
        copies = [
            pltpu.make_async_copy(src.at[i], w_ref.at[i], sems.at[i]) for i in range(n_kind)
        ]
        for copy in copies:
            copy.start()
        for i, copy in enumerate(copies):
            copy.wait()
            total = jnp.sum(w_ref[i].astype(F32), axis=0, keepdims=True)
            sum_ref[:, i * width : (i + 1) * width] = jnp.broadcast_to(total, (8, width))

    return pl.pallas_call(
        body,
        out_shape=(
            jax.ShapeDtypeStruct(w3.shape, w3.dtype),
            jax.ShapeDtypeStruct((8, n_kind * width), F32),
        ),
        in_specs=[hbm()],
        out_specs=(vmem(), vmem()),
        scratch_shapes=[pltpu.SemaphoreType.DMA((n_kind,))],
        compiler_params=params(),
        name="fetch",
    )(w3)


def project(chunks, w3, col_sums):
    n_head, n_chunk = len(chunks[0]), len(chunks)
    piece, feats = chunks[0][0].shape
    width = w3.shape[2]
    rows = piece * n_chunk

    def body(*refs):
        w_ref, sum_ref, q_ref, kv_ref = refs[n_head * n_chunk :]
        for c in range(n_chunk):
            blocks = refs[c * n_head : (c + 1) * n_head]
            mean, inv = joined_moments([moments(b[...]) for b in blocks], feats)
            at = pl.ds(c * piece, piece)
            for i in range(3):
                acc = project_sum(blocks, range(n_head), w_ref, i)
                cols = slice(i * width, (i + 1) * width)
                acc = ((acc - mean * sum_ref[0:1, cols]) * inv).astype(BF16)
                if i == 0:
                    q_ref[at, :] = acc
                else:
                    kv_ref[at, (i - 1) * width : i * width] = acc

    flat = [b for chunk in chunks for b in chunk]
    outs = [((rows, width), BF16), ((rows, 2 * width), BF16)]
    return call(body, outs, [*flat, w3, col_sums])


def project_begin(chunks, w3):
    n_here, n_chunk = len(chunks[0]), len(chunks)
    piece, _ = chunks[0][0].shape
    width = w3.shape[2]

    def body(*refs):
        w_ref, acc_ref, mom_ref = refs[n_here * n_chunk :]
        lane = lax.broadcasted_iota(jnp.int32, (piece, 128), 1)
        for c in range(n_chunk):
            blocks = refs[c * n_here : (c + 1) * n_here]
            at = pl.ds(c * piece, piece)
            for i in range(3):
                acc_ref[at, i * width : (i + 1) * width] = project_sum(
                    blocks, range(n_here), w_ref, i
                )
            held = jnp.zeros((piece, 128), F32)
            for t, block in enumerate(blocks):
                for k, value in enumerate(moments(block[...])):
                    held = jnp.where(lane == 2 * t + k, value, held)
            mom_ref[at, :] = held

    flat = [b for chunk in chunks for b in chunk]
    outs = [((piece * n_chunk, 3 * width), F32), ((piece * n_chunk, 128), F32)]
    return call(body, outs, [*flat, w3])


def project_end(slots, lasts, begun, w3, col_sums, before, weight):
    n_chunk = len(lasts)
    piece, feats = lasts[0].shape
    width = w3.shape[2]
    rows = piece * n_chunk
    n_head = w3.shape[1] // feats
    last = n_head - 1

    def body(*refs):
        w_ref, acc_ref, mom_ref, sum_ref, before_ref, cw_ref = refs[n_chunk : n_chunk + 6]
        q_ref, kv_ref, *outs = refs[n_chunk + 6 :]
        for c in range(n_chunk):
            at = pl.ds(c * piece, piece)
            held = mom_ref[at, :]
            parts = [(held[:, 2 * t : 2 * t + 1], held[:, 2 * t + 1 : 2 * t + 2]) for t in range(last)]
            parts.append(moments(refs[c][...]))
            mean, inv = joined_moments(parts, feats)
            for i in range(3):
                cols = slice(i * width, (i + 1) * width)
                acc = acc_ref[at, cols] + project_sum([refs[c]], [last], w_ref, i)
                acc = ((acc - mean * sum_ref[0:1, cols]) * inv).astype(BF16)
                if i == 0:
                    q_ref[at, :] = acc
                else:
                    kv_ref[at, (i - 1) * width : i * width] = acc
        write_slots(slots, True, [before_ref, kv_ref], cw_ref, outs)

    outs = [((rows, width), BF16), ((rows, 2 * width), BF16)]
    outs += [((slots.rows, 2 * width), BF16)] * RATE
    args = [*lasts, w3, *begun, col_sums, before, weight]
    return call(body, outs, args)


class Slots:
    def __init__(self, seg_len, early_rows):
        self.seg_len, self.early_rows = seg_len, early_rows
        self.offset = [(-a * seg_len) % RATE for a in range(RATE)]
        self.count = [(seg_len - o) // RATE for o in self.offset]
        self.tail = [seg_len - o - RATE * n for o, n in zip(self.offset, self.count)]
        self.early = [max(0, (early_rows - o) // RATE) for o in self.offset]
        self.late = [n - e for n, e in zip(self.count, self.early)]
        most = max(
            max(e + o for e, o in zip(self.early, self.offset)),
            max(l + t for l, t in zip(self.late, self.tail)),
        )
        self.rows = -(-most // 16) * 16
        self.joints = [b for b in range(RATE - 1) if self.tail[b] > 0]


def filter_rows(w_ref):
    return [
        jnp.concatenate([w_ref[r, k : k + 1, :].astype(F32) for k in range(2)], axis=1)
        for r in range(RATE)
    ]


def write_slots(slots, late, sources, w_ref, outs):
    weight = filter_rows(w_ref)
    n = slots.rows
    main = sources[-1]
    base = slots.early_rows if late else 0
    counts = slots.late if late else slots.early
    begins = slots.early if late else [0] * RATE
    firsts = [slots.offset[a] + RATE * begins[a] for a in range(RATE)]
    wanted = sorted({f + r for f in firsts for r in range(RATE)})

    def hits(first, rows, at):
        row = lax.broadcasted_iota(jnp.int32, (n, rows), 0)
        col = lax.broadcasted_iota(jnp.int32, (n, rows), 1) + at
        return jnp.where(col == first + RATE * row, 1.0, 0.0).astype(BF16)

    chosen = jnp.concatenate([hits(f, main.shape[0], base) for f in wanted], axis=0)
    picks = jnp.dot(chosen, main[...], preferred_element_type=F32)
    row = lax.broadcasted_iota(jnp.int32, (n, 1), 0)
    picked = {}
    for k, f in enumerate(wanted):
        got = picks[k * n : (k + 1) * n]
        if f < base:
            back = base - f
            got = jnp.where(row == 0, sources[0][-16:, :].astype(F32)[16 - back : 17 - back], got)
        picked[f] = got
    raw = main[...].astype(F32)
    for a in range(RATE):
        acc = None
        for r in range(RATE):
            term = picked[firsts[a] + r] * weight[r]
            acc = term if acc is None else acc + term
        n_raw = slots.tail[a] if late else slots.offset[a]
        for i in range(n_raw):
            at = main.shape[0] - n_raw + i if late else i
            acc = jnp.where(row == counts[a] + i, raw[at : at + 1, :], acc)
        outs[a][...] = acc.astype(BF16)


def compress_early(slots, source, weight):
    def body(source_ref, w_ref, *outs):
        write_slots(slots, False, [source_ref], w_ref, outs)

    outs = [((slots.rows, 2 * weight.shape[2]), BF16)] * RATE
    return call(body, outs, [source, weight])


SCALE = math.log2(math.e) / math.sqrt(DH)


def score(q, keys):
    return lax.dot_general(q, keys, (((1,), (1,)), ((), ())), preferred_element_type=F32)


def slot_bias(seg, n_cols, spans):
    col = lax.broadcasted_iota(jnp.int32, (1, n_cols), 1)
    valid = col < 0
    for begin, count in spans:
        valid |= (col >= begin) & (col < begin + count)
    return jnp.where(valid & (seg >= BACK), 0.0, NEG).astype(F32)


def attend_begin(slots, q, own, memory, early):
    rows, width = q.shape
    n = slots.rows
    n_comp = -(-RATE * n // 128) * 128
    heads = width // DH

    def body(q_ref, *refs):
        own_refs = refs[: len(own)]
        mem_ref = refs[len(own)]
        early_refs = refs[len(own) + 1 : len(own) + 1 + RATE]
        mix_ref, stat_ref, comp_ref = refs[len(own) + 1 + RATE :]
        seg = lax.axis_index("seg")
        for a in range(RATE):
            comp_ref[a * n : (a + 1) * n, :] = early_refs[a][...]
        if n_comp > RATE * n:
            comp_ref[RATE * n :, :] = jnp.zeros((n_comp - RATE * n, 2 * width), BF16)
        comp_bias = slot_bias(seg, n_comp, [(a * n, slots.early[a]) for a in range(RATE)])
        mem_bias = jnp.where(seg >= 1, 0.0, NEG).astype(F32)
        q_row = lax.broadcasted_iota(jnp.int32, (rows, rows), 0)
        k_row = lax.broadcasted_iota(jnp.int32, (rows, rows), 1)
        causal = k_row <= q_row
        lane = lax.broadcasted_iota(jnp.int32, (rows, 128), 1)
        stats = jnp.zeros((rows, 128), F32)
        for h in range(heads):
            kc = slice(h * DH, (h + 1) * DH)
            vc = slice(width + h * DH, width + (h + 1) * DH)
            q = q_ref[:, kc]
            pieces = [
                (score(q, comp_ref[:, kc]) + comp_bias, comp_ref, vc),
                (score(q, mem_ref[:, kc]) + mem_bias, mem_ref, vc),
            ]
            for o in own_refs[:-1]:
                pieces.append((score(q, o[:, kc]), o, vc))
            o = own_refs[-1]
            pieces.append((jnp.where(causal, score(q, o[:, kc]), NEG), o, vc))
            top, norm, mixed = gathered(pieces, None)
            mix_ref[:, kc] = mixed
            stats = jnp.where(lane == 2 * h, top, stats)
            stats = jnp.where(lane == 2 * h + 1, norm, stats)
        stat_ref[...] = stats

    outs = [((rows, width), F32), ((rows, 128), F32)]
    scratch = [pltpu.VMEM((n_comp, 2 * width), BF16)]
    return call(body, outs, [q, *own, memory, *early], scratch)


def gathered(pieces, so_far):
    top = None if so_far is None else so_far[0]
    for s, _, _ in pieces:
        m = jnp.max(s, axis=1, keepdims=True)
        top = m if top is None else jnp.maximum(top, m)
    norm = mixed = None
    if so_far is not None:
        shrink = jnp.exp2((so_far[0] - top) * SCALE)
        norm, mixed = so_far[1] * shrink, so_far[2] * shrink
    for s, v, cols in pieces:
        p = jnp.exp2((s - top) * SCALE)
        total = jnp.sum(p, axis=1, keepdims=True)
        part = jnp.dot(p.astype(BF16), v[:, cols], preferred_element_type=F32)
        norm = total if norm is None else norm + total
        mixed = part if mixed is None else mixed + part
    return top, norm, mixed


def attend_end(slots, q, begun, memory, heads_of, late, weight):
    rows, width = q.shape
    n = slots.rows
    n_comp = -(-(RATE * n + 16) // 128) * 128
    heads = width // DH

    def body(q_ref, mix_ref, stat_ref, mem_ref, *refs):
        early_refs = refs[:RATE]
        late_refs = refs[RATE : 2 * RATE]
        w_ref, out_ref, comp_ref = refs[2 * RATE :]
        seg = lax.axis_index("seg")
        weight = filter_rows(w_ref)
        for a in range(RATE):
            comp_ref[a * n : (a + 1) * n, :] = late_refs[a][...]
        pad = n_comp - RATE * n
        row = lax.broadcasted_iota(jnp.int32, (pad, 1), 0)
        extra = jnp.zeros((pad, 2 * width), F32)
        for k, b in enumerate(slots.joints):
            at = slots.late[b]
            tail = late_refs[b][...].astype(F32)
            parts = [tail[at + i : at + i + 1] for i in range(slots.tail[b])]
            at = slots.early[b + 1]
            head = early_refs[b + 1][...].astype(F32)
            parts += [head[at + i : at + i + 1] for i in range(slots.offset[b + 1])]
            slot = sum(p * weight[r] for r, p in enumerate(parts))
            extra = jnp.where(row == k, slot, extra)
        comp_ref[RATE * n :, :] = extra.astype(BF16)
        spans = [(a * n, slots.late[a]) for a in range(RATE)] + [(RATE * n, len(slots.joints))]
        comp_bias = slot_bias(seg, n_comp, spans)
        mem_bias = jnp.where(seg >= 1, 0.0, NEG).astype(F32)
        for h in range(heads):
            kc = slice(h * DH, (h + 1) * DH)
            vc = slice(width + h * DH, width + (h + 1) * DH)
            q = q_ref[:, kc]
            pieces = [
                (score(q, comp_ref[:, kc]) + comp_bias, comp_ref, vc),
                (score(q, mem_ref[:, kc]) + mem_bias, mem_ref, vc),
            ]
            so_far = (
                stat_ref[:, 2 * h : 2 * h + 1],
                stat_ref[:, 2 * h + 1 : 2 * h + 2],
                mix_ref[:, kc],
            )
            _, norm, mixed = gathered(pieces, so_far)
            out_ref[:, kc] = (mixed / norm).astype(BF16)

    outs = [((rows, width), BF16)]
    scratch = [pltpu.VMEM((n_comp, 2 * width), BF16)]
    args = [q, *begun, memory, *heads_of, *late, weight]
    return call(body, outs, args, scratch)[0]


def output_begin(ctx, w_full, xored):
    rows = ctx[0].shape[0]

    def body(*refs):
        w_ref, acc_ref = refs[len(ctx) :]
        acc_ref[...] = output_sum(refs[: len(ctx)], range(len(ctx)), w_ref, xored)

    outs = [((rows, w_full.shape[1]), F32)]
    return call(body, outs, [*ctx, w_full])[0]


def output_sum(ctx, steps, w_ref, xored):
    width = ctx[0].shape[1]
    unit = xored or width
    size = w_ref.shape[0] // width
    acc = None
    for t, c in zip(steps, ctx):
        for k in range(width // unit):
            block = source_of(t, size) * (width // unit) + k
            if xored:
                block = lax.bitwise_xor(block, lax.axis_index("seg"))
            start = pl.multiple_of(block * unit, unit)
            part = jnp.dot(
                c[:, k * unit : (k + 1) * unit],
                w_ref[pl.ds(start, unit), :],
                preferred_element_type=F32,
            )
            acc = part if acc is None else acc + part
    return acc


def output_end(half, n_half, last_step, ctx, begun, w_full, xored, result):
    rows = ctx.shape[0]
    columns = w_full.shape[1]
    n_extra = 1 if result is not None else 0

    def body(ctx_ref, acc_ref, w_ref, *refs):
        out_ref, held, sem = refs[n_extra:]
        acc = acc_ref[...] + output_sum([ctx_ref], [last_step], w_ref, xored)
        held[...] = acc.astype(BF16)
        copy = pltpu.make_async_copy(held, out_ref.at[pl.ds(half * rows, rows), :], sem)
        copy.start()
        copy.wait()

    args = [ctx, begun, w_full]
    in_specs = [vmem(), vmem(), vmem()]
    aliases = {}
    if result is not None:
        args.append(result)
        in_specs.append(hbm())
        aliases = {3: 0}
    return pl.pallas_call(
        body,
        out_shape=jax.ShapeDtypeStruct((rows * n_half, columns), BF16),
        in_specs=in_specs,
        out_specs=hbm(),
        scratch_shapes=[pltpu.VMEM((rows, columns), BF16), pltpu.SemaphoreType.DMA],
        input_output_aliases=aliases,
        compiler_params=params(),
    )(*args)


def gather_rows(block, by_xor):
    size = lax.axis_size("seg")
    if size & (size - 1):
        return lax.all_gather(block, "seg", axis=0, tiled=True)
    seg = lax.axis_index("seg")
    step = 1
    while step < size:
        other = lax.ppermute(block, "seg", [(i, i ^ step) for i in range(size)])
        if by_xor:
            block = join(block, other)
        else:
            upper = (seg // step) % 2 == 1
            low = jnp.where(upper, other, block)
            high = jnp.where(upper, block, other)
            block = jnp.concatenate([low, high], axis=0)
        step *= 2
    return block


def local(layer_input, w_qkv, comp_weight, w_out):
    n_head = lax.axis_size("head")
    seg_len = layer_input.shape[1]
    rows = pltpu.with_memory_space_constraint(layer_input[0], pltpu.HBM)
    w3 = pltpu.with_memory_space_constraint(jnp.transpose(w_qkv, (1, 0, 2)), pltpu.HBM)
    width = w_qkv.shape[2]
    weight = comp_weight

    n_chunk, n_half = 4, 2
    per_half = n_chunk // n_half
    piece = seg_len // n_chunk
    half_rows = seg_len // n_half
    slots = Slots(seg_len, half_rows)

    starts = [c * piece for c in range(n_chunk)]
    first = [[chunk] for chunk in split(rows, starts[:per_half], piece)]
    n_seg = lax.axis_size("seg")
    own_rows = w_out.shape[0]
    power = n_seg & (n_seg - 1) == 0
    xored = own_rows if power and own_rows % DH == 0 and width % own_rows == 0 else 0

    w_vmem, col_sums = fetch_weights(w3)
    for _ in range(1, n_head):
        for chunk in first:
            chunk.append(around(chunk[-1]))
    w_full = gather_rows(w_out, xored)
    q0, kv0 = project(first, w_vmem, col_sums)
    early_parts = compress_early(slots, kv0, weight)
    mem0 = passed_along(kv0, 1)
    early = [passed_along(p, BACK - a) for a, p in enumerate(early_parts)]

    second = [[chunk] for chunk in split(rows, starts[per_half:], piece)]
    for _ in range(1, n_head):
        for chunk in second:
            chunk.append(around(chunk[-1]))
    begun = project_begin([chunk[:-1] for chunk in second], w_vmem)
    lasts = [chunk[-1] for chunk in second]
    q1, kv1, *late = project_end(slots, lasts, begun, w_vmem, col_sums, kv0, weight)
    mem1 = passed_along(kv1, 1)
    late = [passed_along(p, BACK - a) for a, p in enumerate(late)]

    rings = []
    for q, own in ((q0, [kv0]), (q1, [kv0, kv1])):
        part = attend_begin(slots, q, own, mem0, early)
        ctx = attend_end(slots, q, part, mem1, early, late, weight)
        rings.append([ctx])
    for _ in range(1, n_head):
        for ring in rings:
            ring.append(around(ring[-1]))
    result = None
    for h, ring in enumerate(rings):
        part = output_begin(ring[:-1], w_full, xored)
        result = output_end(h, n_half, n_head - 1, ring[-1], part, w_full, xored, result)
    return result[None]


def solution(mesh):
    return jax.shard_map(
        local,
        mesh=mesh,
        in_specs=(
            P(None, "seg", "head"),
            P(None, None, "head"),
            P(None, None, "head"),
            P("seg", "head"),
        ),
        out_specs=P(None, "seg", "head"),
        check_vma=False,
    )
```

profile of v0, /device:TPU:0, one launch (start us, length us, event | category | flops | bytes accessed | tf_op | source)
XLA Modules:
  0.0 101.6 jit_solution(11085460918375544606)
XLA Ops:
  1.0 3.1 %collective-permute-start.6 = (bf16[128,512]{1,0:T(8,128)(2,1)S(1)}, bf16[128,512]{1,0:T(8,128)(2,1)S(1)}, u32[]{:S(2)}, u32[]{:S(2)}) collective-permute-start(bf16[128,512]{1,0:T(8,128)(2,1)S(1)} %get-tuple-element.33.refs_0_), channel_id=1, source_target_pairs={{0,1},{1,2},{2,3},{3,0},{4,5},{5,6},{6,7},{7,4},{8,9},{9,10},{10,1... | collective-permute-start | bytes 393224 | tf_op jit(solution)/shard_map/ppermute | solution.py:35
  4.1 1.6 %collective-permute-start.9 = (bf16[128,512]{1,0:T(8,128)(2,1)S(1)}, bf16[128,512]{1,0:T(8,128)(2,1)S(1)}, u32[]{:S(2)}, u32[]{:S(2)}) collective-permute-start(bf16[128,512]{1,0:T(8,128)(2,1)S(1)} %get-tuple-element.34.refs_4_), channel_id=1, source_target_pairs={{0,1},{1,2},{2,3},{3,0},{4,5},{5,6},{6,7},{7,4},{8,9},{9,10},{10,1... | collective-permute-start | bytes 393224 | tf_op jit(solution)/shard_map/ppermute | solution.py:35
  6.7 1.6 %collective-permute-start = (bf16[128,512]{1,0:T(8,128)(2,1)S(1)}, bf16[128,512]{1,0:T(8,128)(2,1)S(1)}, u32[]{:S(2)}, u32[]{:S(2)}) collective-permute-start(bf16[128,512]{1,0:T(8,128)(2,1)S(1)} %get-tuple-element.27.refs_0_), channel_id=1, source_target_pairs={{0,1},{1,2},{2,3},{3,0},{4,5},{5,6},{6,7},{7,4},{8,9},{9,10},{10,1... | collective-permute-start | bytes 393224 | tf_op jit(solution)/shard_map/ppermute | solution.py:35
  8.4 2.1 %collective-permute-done.6.refs_1_ = bf16[128,512]{1,0:T(8,128)(2,1)S(1)} collective-permute-done((bf16[128,512]{1,0:T(8,128)(2,1)S(1)}, bf16[128,512]{1,0:T(8,128)(2,1)S(1)}, u32[]{:S(2)}, u32[]{:S(2)}) %collective-permute-start.6) | collective-permute-done | bytes 131104 | tf_op jit(solution)/shard_map/ppermute | solution.py:35
  10.5 2.8 %collective-permute-done.9.refs_5_ = bf16[128,512]{1,0:T(8,128)(2,1)S(1)} collective-permute-done((bf16[128,512]{1,0:T(8,128)(2,1)S(1)}, bf16[128,512]{1,0:T(8,128)(2,1)S(1)}, u32[]{:S(2)}, u32[]{:S(2)}) %collective-permute-start.9) | collective-permute-done | bytes 131104 | tf_op jit(solution)/shard_map/ppermute | solution.py:35
  13.3 2.8 %collective-permute-done.refs_1_ = bf16[128,512]{1,0:T(8,128)(2,1)S(1)} collective-permute-done((bf16[128,512]{1,0:T(8,128)(2,1)S(1)}, bf16[128,512]{1,0:T(8,128)(2,1)S(1)}, u32[]{:S(2)}, u32[]{:S(2)}) %collective-permute-start) | collective-permute-done | bytes 131104 | tf_op jit(solution)/shard_map/ppermute | solution.py:35
  16.1 2.8 %collective-permute-done.3.refs_4_ = bf16[128,512]{1,0:T(8,128)(2,1)S(1)} collective-permute-done((bf16[128,512]{1,0:T(8,128)(2,1)S(1)}, bf16[128,512]{1,0:T(8,128)(2,1)S(1)}, u32[]{:S(2)}, u32[]{:S(2)}) %collective-permute-start.3) | collective-permute-done | bytes 131104 | tf_op jit(solution)/shard_map/ppermute | solution.py:35
  18.9 2.8 %collective-permute-done.7.refs_2_ = bf16[128,512]{1,0:T(8,128)(2,1)S(1)} collective-permute-done((bf16[128,512]{1,0:T(8,128)(2,1)S(1)}, bf16[128,512]{1,0:T(8,128)(2,1)S(1)}, u32[]{:S(2)}, u32[]{:S(2)}) %collective-permute-start.7) | collective-permute-done | bytes 131104 | tf_op jit(solution)/shard_map/ppermute | solution.py:35
  21.7 2.8 %collective-permute-done.10.refs_6_ = bf16[128,512]{1,0:T(8,128)(2,1)S(1)} collective-permute-done((bf16[128,512]{1,0:T(8,128)(2,1)S(1)}, bf16[128,512]{1,0:T(8,128)(2,1)S(1)}, u32[]{:S(2)}, u32[]{:S(2)}) %collective-permute-start.10) | collective-permute-done | bytes 131104 | tf_op jit(solution)/shard_map/ppermute | solution.py:35
  25.4 1.8 %collective-permute-start.24 = (bf16[256,512]{1,0:T(8,128)(2,1)S(1)}, bf16[256,512]{1,0:T(8,128)(2,1)S(1)}, u32[]{:S(2)}, u32[]{:S(2)}) collective-permute-start(bf16[256,512]{1,0:T(8,128)(2,1)S(1)} %shard_map.54.one_ref), channel_id=1, source_target_pairs={{0,8},{4,12},{8,0},{12,4},{16,24},{20,28},{24,16},{28,20},{1,9},{5... | collective-permute-start | bytes 786440 | tf_op jit(solution)/shard_map/ppermute | solution.py:508
  28.6 1.6 %collective-permute-done.4.refs_5_ = bf16[128,512]{1,0:T(8,128)(2,1)S(1)} collective-permute-done((bf16[128,512]{1,0:T(8,128)(2,1)S(1)}, bf16[128,512]{1,0:T(8,128)(2,1)S(1)}, u32[]{:S(2)}, u32[]{:S(2)}) %collective-permute-start.4) | collective-permute-done | bytes 131104 | tf_op jit(solution)/shard_map/ppermute | solution.py:35
  30.2 2.3 %fetch.1 = (bf16[3,2048,256]{2,1,0:T(8,128)(2,1)S(1)}, f32[8,768]{1,0:T(8,128)S(1)}) custom-call(bf16[3,2048,256]{2,1,0:T(8,128)(2,1)} %bitcast.3), custom_call_target="tpu_custom_call" | custom-call | tf_op jit(solution)/shard_map/fetch/pallas_call | solution.py:140
  32.9 2.8 %collective-permute-done.11.refs_7_ = bf16[128,512]{1,0:T(8,128)(2,1)S(1)} collective-permute-done((bf16[128,512]{1,0:T(8,128)(2,1)S(1)}, bf16[128,512]{1,0:T(8,128)(2,1)S(1)}, u32[]{:S(2)}, u32[]{:S(2)}) %collective-permute-start.11) | collective-permute-done | bytes 131104 | tf_op jit(solution)/shard_map/ppermute | solution.py:35
  38.6 2.0 %collective-permute-done.5.refs_1_ = bf16[128,512]{1,0:T(8,128)(2,1)S(1)} collective-permute-done((bf16[128,512]{1,0:T(8,128)(2,1)S(1)}, bf16[128,512]{1,0:T(8,128)(2,1)S(1)}, u32[]{:S(2)}, u32[]{:S(2)}) %collective-permute-start.5) | collective-permute-done | bytes 131104 | tf_op jit(solution)/shard_map/ppermute | solution.py:35
  42.4 1.6 %collective-permute-start.13 = (bf16[96,512]{1,0:T(8,128)(2,1)S(1)}, bf16[96,512]{1,0:T(8,128)(2,1)S(1)}, u32[]{:S(2)}, u32[]{:S(2)}) collective-permute-start(bf16[96,512]{1,0:T(8,128)(2,1)S(1)} %get-tuple-element.38), channel_id=1, source_target_pairs={{0,16},{4,20},{8,24},{12,28},{16,0},{20,4},{24,8},{28,12},{1,17},{... | collective-permute-start | bytes 294920 | tf_op jit(solution)/shard_map/ppermute | solution.py:41
  46.9 7.1 %collective-permute-done.13.refs_3_.refs_0_.refs_2_ = bf16[96,512]{1,0:T(8,128)(2,1)S(1)} collective-permute-done((bf16[96,512]{1,0:T(8,128)(2,1)S(1)}, bf16[96,512]{1,0:T(8,128)(2,1)S(1)}, u32[]{:S(2)}, u32[]{:S(2)}) %collective-permute-start.13) | collective-permute-done | bytes 98336 | tf_op jit(solution)/shard_map/ppermute | solution.py:41
  53.9 1.5 %collective-permute-start.25 = (bf16[512,512]{1,0:T(8,128)(2,1)S(1)}, bf16[512,512]{1,0:T(8,128)(2,1)S(1)}, u32[]{:S(2)}, u32[]{:S(2)}) collective-permute-start(bf16[512,512]{1,0:T(8,128)(2,1)S(1)} %shard_map.55.one_ref), channel_id=1, source_target_pairs={{0,16},{4,20},{8,24},{12,28},{16,0},{20,4},{24,8},{28,12},{1,17},{... | collective-permute-start | bytes 1572872 | tf_op jit(solution)/shard_map/ppermute | solution.py:508
  56.6 1.5 %collective-permute-start.19 = (bf16[96,512]{1,0:T(8,128)(2,1)S(1)}, bf16[96,512]{1,0:T(8,128)(2,1)S(1)}, u32[]{:S(2)}, u32[]{:S(2)}) collective-permute-start(bf16[96,512]{1,0:T(8,128)(2,1)S(1)} %get-tuple-element.45), channel_id=1, source_target_pairs={{0,8},{4,12},{8,16},{12,20},{16,24},{20,28},{24,0},{28,4},{1,9},{5... | collective-permute-start | bytes 294920 | tf_op jit(solution)/shard_map/ppermute | solution.py:41
  59.2 14.8 %collective-permute-done.17.refs_3_ = bf16[96,512]{1,0:T(8,128)(2,1)S(1)} collective-permute-done((bf16[96,512]{1,0:T(8,128)(2,1)S(1)}, bf16[96,512]{1,0:T(8,128)(2,1)S(1)}, u32[]{:S(2)}, u32[]{:S(2)}) %collective-permute-start.17) | collective-permute-done | bytes 98336 | tf_op jit(solution)/shard_map/ppermute | solution.py:41
  79.4 3.5 %collective-permute-done.26.refs_1_ = bf16[256,256]{1,0:T(8,128)(2,1)S(1)} collective-permute-done((bf16[256,256]{1,0:T(8,128)(2,1)S(1)}, bf16[256,256]{1,0:T(8,128)(2,1)S(1)}, u32[]{:S(2)}, u32[]{:S(2)}) %collective-permute-start.26) | collective-permute-done | bytes 131104 | tf_op jit(solution)/shard_map/ppermute | solution.py:35
  83.0 2.6 %collective-permute-done.20.refs_1_ = bf16[256,256]{1,0:T(8,128)(2,1)S(1)} collective-permute-done((bf16[256,256]{1,0:T(8,128)(2,1)S(1)}, bf16[256,256]{1,0:T(8,128)(2,1)S(1)}, u32[]{:S(2)}, u32[]{:S(2)}) %collective-permute-start.20) | collective-permute-done | bytes 131104 | tf_op jit(solution)/shard_map/ppermute | solution.py:35
  85.5 5.4 %collective-permute-done.27.refs_2_ = bf16[256,256]{1,0:T(8,128)(2,1)S(1)} collective-permute-done((bf16[256,256]{1,0:T(8,128)(2,1)S(1)}, bf16[256,256]{1,0:T(8,128)(2,1)S(1)}, u32[]{:S(2)}, u32[]{:S(2)}) %collective-permute-start.27) | collective-permute-done | bytes 131104 | tf_op jit(solution)/shard_map/ppermute | solution.py:35
  91.0 2.8 %collective-permute-done.21.refs_2_ = bf16[256,256]{1,0:T(8,128)(2,1)S(1)} collective-permute-done((bf16[256,256]{1,0:T(8,128)(2,1)S(1)}, bf16[256,256]{1,0:T(8,128)(2,1)S(1)}, u32[]{:S(2)}, u32[]{:S(2)}) %collective-permute-start.21) | collective-permute-done | bytes 131104 | tf_op jit(solution)/shard_map/ppermute | solution.py:35
  95.0 3.6 %collective-permute-done.28.ctx_ref = bf16[256,256]{1,0:T(8,128)(2,1)S(1)} collective-permute-done((bf16[256,256]{1,0:T(8,128)(2,1)S(1)}, bf16[256,256]{1,0:T(8,128)(2,1)S(1)}, u32[]{:S(2)}, u32[]{:S(2)}) %collective-permute-start.28) | collective-permute-done | bytes 131104 | tf_op jit(solution)/shard_map/ppermute | solution.py:35
  (56 shorter events, 24.1 us)
Async XLA Ops:
  1.0 9.5 %collective-permute-start.6 = (bf16[128,512]{1,0:T(8,128)(2,1)S(1)}, bf16[128,512]{1,0:T(8,128)(2,1)S(1)}, u32[]{:S(2)}, u32[]{:S(2)}) collective-permute-start(bf16[128,512]{1,0:T(8,128)(2,1)S(1)} %get-tuple-element.33.refs_0_), channel_id=1, source_target_pairs={{0,1},{1,2},{2,3},{3,0},{4,5},{5,6},{6,7},{7,4},{8,9},{9,10},{10,1... | collective-permute-start | bytes 393224 | tf_op jit(solution)/shard_map/ppermute | solution.py:35
  4.1 9.2 %collective-permute-start.9 = (bf16[128,512]{1,0:T(8,128)(2,1)S(1)}, bf16[128,512]{1,0:T(8,128)(2,1)S(1)}, u32[]{:S(2)}, u32[]{:S(2)}) collective-permute-start(bf16[128,512]{1,0:T(8,128)(2,1)S(1)} %get-tuple-element.34.refs_4_), channel_id=1, source_target_pairs={{0,1},{1,2},{2,3},{3,0},{4,5},{5,6},{6,7},{7,4},{8,9},{9,10},{10,1... | collective-permute-start | bytes 393224 | tf_op jit(solution)/shard_map/ppermute | solution.py:35
  6.7 9.4 %collective-permute-start = (bf16[128,512]{1,0:T(8,128)(2,1)S(1)}, bf16[128,512]{1,0:T(8,128)(2,1)S(1)}, u32[]{:S(2)}, u32[]{:S(2)}) collective-permute-start(bf16[128,512]{1,0:T(8,128)(2,1)S(1)} %get-tuple-element.27.refs_0_), channel_id=1, source_target_pairs={{0,1},{1,2},{2,3},{3,0},{4,5},{5,6},{6,7},{7,4},{8,9},{9,10},{10,1... | collective-permute-start | bytes 393224 | tf_op jit(solution)/shard_map/ppermute | solution.py:35
  8.3 10.6 %collective-permute-start.3 = (bf16[128,512]{1,0:T(8,128)(2,1)S(1)}, bf16[128,512]{1,0:T(8,128)(2,1)S(1)}, u32[]{:S(2)}, u32[]{:S(2)}) collective-permute-start(bf16[128,512]{1,0:T(8,128)(2,1)S(1)} %get-tuple-element.28.refs_3_), channel_id=1, source_target_pairs={{0,1},{1,2},{2,3},{3,0},{4,5},{5,6},{6,7},{7,4},{8,9},{9,10},{10,1... | collective-permute-start | bytes 393224 | tf_op jit(solution)/shard_map/ppermute | solution.py:35
  10.5 11.2 %collective-permute-start.7 = (bf16[128,512]{1,0:T(8,128)(2,1)S(1)}, bf16[128,512]{1,0:T(8,128)(2,1)S(1)}, u32[]{:S(2)}, u32[]{:S(2)}) collective-permute-start(bf16[128,512]{1,0:T(8,128)(2,1)S(1)} %collective-permute-done.6.refs_1_), channel_id=1, source_target_pairs={{0,1},{1,2},{2,3},{3,0},{4,5},{5,6},{6,7},{7,4},{8,9},{9,10},{10,1... | collective-permute-start | bytes 393224 | tf_op jit(solution)/shard_map/ppermute | solution.py:35
  13.3 11.2 %collective-permute-start.10 = (bf16[128,512]{1,0:T(8,128)(2,1)S(1)}, bf16[128,512]{1,0:T(8,128)(2,1)S(1)}, u32[]{:S(2)}, u32[]{:S(2)}) collective-permute-start(bf16[128,512]{1,0:T(8,128)(2,1)S(1)} %collective-permute-done.9.refs_5_), channel_id=1, source_target_pairs={{0,1},{1,2},{2,3},{3,0},{4,5},{5,6},{6,7},{7,4},{8,9},{9,10},{10,1... | collective-permute-start | bytes 393224 | tf_op jit(solution)/shard_map/ppermute | solution.py:35
  13.3 11.2 %collective-permute-start.23 = (bf16[128,512]{1,0:T(8,128)(2,1)}, bf16[128,512]{1,0:T(8,128)(2,1)S(1)}, u32[]{:S(2)}, u32[]{:S(2)}) collective-permute-start(bf16[128,512]{1,0:T(8,128)(2,1)} %one_ref.1), channel_id=1, source_target_pairs={{0,4},{4,0},{8,12},{12,8},{16,20},{20,16},{24,28},{28,24},{1,5},{5... | collective-permute-start | bytes 393224 | tf_op jit(solution)/shard_map/ppermute | solution.py:508
  16.1 11.2 %collective-permute-start.1 = (bf16[128,512]{1,0:T(8,128)(2,1)S(1)}, bf16[128,512]{1,0:T(8,128)(2,1)S(1)}, u32[]{:S(2)}, u32[]{:S(2)}) collective-permute-start(bf16[128,512]{1,0:T(8,128)(2,1)S(1)} %collective-permute-done.refs_1_), channel_id=1, source_target_pairs={{0,1},{1,2},{2,3},{3,0},{4,5},{5,6},{6,7},{7,4},{8,9},{9,10},{10,1... | collective-permute-start | bytes 393224 | tf_op jit(solution)/shard_map/ppermute | solution.py:35
  18.9 11.2 %collective-permute-start.4 = (bf16[128,512]{1,0:T(8,128)(2,1)S(1)}, bf16[128,512]{1,0:T(8,128)(2,1)S(1)}, u32[]{:S(2)}, u32[]{:S(2)}) collective-permute-start(bf16[128,512]{1,0:T(8,128)(2,1)S(1)} %collective-permute-done.3.refs_4_), channel_id=1, source_target_pairs={{0,1},{1,2},{2,3},{3,0},{4,5},{5,6},{6,7},{7,4},{8,9},{9,10},{10,1... | collective-permute-start | bytes 393224 | tf_op jit(solution)/shard_map/ppermute | solution.py:35
  21.7 11.2 %collective-permute-start.8 = (bf16[128,512]{1,0:T(8,128)(2,1)S(1)}, bf16[128,512]{1,0:T(8,128)(2,1)S(1)}, u32[]{:S(2)}, u32[]{:S(2)}) collective-permute-start(bf16[128,512]{1,0:T(8,128)(2,1)S(1)} %collective-permute-done.7.refs_2_), channel_id=1, source_target_pairs={{0,1},{1,2},{2,3},{3,0},{4,5},{5,6},{6,7},{7,4},{8,9},{9,10},{10,1... | collective-permute-start | bytes 393224 | tf_op jit(solution)/shard_map/ppermute | solution.py:35
  24.5 11.2 %collective-permute-start.11 = (bf16[128,512]{1,0:T(8,128)(2,1)S(1)}, bf16[128,512]{1,0:T(8,128)(2,1)S(1)}, u32[]{:S(2)}, u32[]{:S(2)}) collective-permute-start(bf16[128,512]{1,0:T(8,128)(2,1)S(1)} %collective-permute-done.10.refs_6_), channel_id=1, source_target_pairs={{0,1},{1,2},{2,3},{3,0},{4,5},{5,6},{6,7},{7,4},{8,9},{9,10},{10,1... | collective-permute-start | bytes 393224 | tf_op jit(solution)/shard_map/ppermute | solution.py:35
  25.4 19.9 %collective-permute-start.24 = (bf16[256,512]{1,0:T(8,128)(2,1)S(1)}, bf16[256,512]{1,0:T(8,128)(2,1)S(1)}, u32[]{:S(2)}, u32[]{:S(2)}) collective-permute-start(bf16[256,512]{1,0:T(8,128)(2,1)S(1)} %shard_map.54.one_ref), channel_id=1, source_target_pairs={{0,8},{4,12},{8,0},{12,4},{16,24},{20,28},{24,16},{28,20},{1,9},{5... | collective-permute-start | bytes 786440 | tf_op jit(solution)/shard_map/ppermute | solution.py:508
  27.3 11.2 %collective-permute-start.2 = (bf16[128,512]{1,0:T(8,128)(2,1)S(1)}, bf16[128,512]{1,0:T(8,128)(2,1)S(1)}, u32[]{:S(2)}, u32[]{:S(2)}) collective-permute-start(bf16[128,512]{1,0:T(8,128)(2,1)S(1)} %collective-permute-done.1.refs_2_), channel_id=1, source_target_pairs={{0,1},{1,2},{2,3},{3,0},{4,5},{5,6},{6,7},{7,4},{8,9},{9,10},{10,1... | collective-permute-start | bytes 393224 | tf_op jit(solution)/shard_map/ppermute | solution.py:35
  30.1 10.4 %collective-permute-start.5 = (bf16[128,512]{1,0:T(8,128)(2,1)S(1)}, bf16[128,512]{1,0:T(8,128)(2,1)S(1)}, u32[]{:S(2)}, u32[]{:S(2)}) collective-permute-start(bf16[128,512]{1,0:T(8,128)(2,1)S(1)} %collective-permute-done.4.refs_5_), channel_id=1, source_target_pairs={{0,1},{1,2},{2,3},{3,0},{4,5},{5,6},{6,7},{7,4},{8,9},{9,10},{10,1... | collective-permute-start | bytes 393224 | tf_op jit(solution)/shard_map/ppermute | solution.py:35
  37.0 19.5 %collective-permute-start.12 = (bf16[256,512]{1,0:T(8,128)(2,1)S(1)}, bf16[256,512]{1,0:T(8,128)(2,1)S(1)}, u32[]{:S(2)}, u32[]{:S(2)}) collective-permute-start(bf16[256,512]{1,0:T(8,128)(2,1)S(1)} %get-tuple-element.35.refs_6_.source_ref.refs_0_), channel_id=1, source_target_pairs={{0,4},{4,8},{8,12},{12,16},{16,20},{20,24},{24,28},{28,0},{1,5},{5... | collective-permute-start | bytes 786440 | tf_op jit(solution)/shard_map/ppermute | solution.py:41
  42.0 32.2 %collective-permute-start.16 = (bf16[256,512]{1,0:T(8,128)(2,1)S(1)}, bf16[256,512]{1,0:T(8,128)(2,1)S(1)}, u32[]{:S(2)}, u32[]{:S(2)}) collective-permute-start(bf16[256,512]{1,0:T(8,128)(2,1)S(1)} %get-tuple-element.37.refs_1_), channel_id=1, source_target_pairs={{0,4},{4,8},{8,12},{12,16},{16,20},{20,24},{24,28},{28,0},{1,5},{5... | collective-permute-start | bytes 786440 | tf_op jit(solution)/shard_map/ppermute | solution.py:41
  42.4 11.6 %collective-permute-start.13 = (bf16[96,512]{1,0:T(8,128)(2,1)S(1)}, bf16[96,512]{1,0:T(8,128)(2,1)S(1)}, u32[]{:S(2)}, u32[]{:S(2)}) collective-permute-start(bf16[96,512]{1,0:T(8,128)(2,1)S(1)} %get-tuple-element.38), channel_id=1, source_target_pairs={{0,16},{4,20},{8,24},{12,28},{16,0},{20,4},{24,8},{28,12},{1,17},{... | collective-permute-start | bytes 294920 | tf_op jit(solution)/shard_map/ppermute | solution.py:41
  43.9 11.5 %collective-permute-start.14 = (bf16[96,512]{1,0:T(8,128)(2,1)S(1)}, bf16[96,512]{1,0:T(8,128)(2,1)S(1)}, u32[]{:S(2)}, u32[]{:S(2)}) collective-permute-start(bf16[96,512]{1,0:T(8,128)(2,1)S(1)} %get-tuple-element.39), channel_id=1, source_target_pairs={{0,12},{4,16},{8,20},{12,24},{16,28},{20,0},{24,4},{28,8},{1,13},{... | collective-permute-start | bytes 294920 | tf_op jit(solution)/shard_map/ppermute | solution.py:41
  45.3 11.2 %collective-permute-start.15 = (bf16[96,512]{1,0:T(8,128)(2,1)S(1)}, bf16[96,512]{1,0:T(8,128)(2,1)S(1)}, u32[]{:S(2)}, u32[]{:S(2)}) collective-permute-start(bf16[96,512]{1,0:T(8,128)(2,1)S(1)} %get-tuple-element.40), channel_id=1, source_target_pairs={{0,8},{4,12},{8,16},{12,20},{16,24},{20,28},{24,0},{28,4},{1,9},{5... | collective-permute-start | bytes 294920 | tf_op jit(solution)/shard_map/ppermute | solution.py:41
  53.9 39.9 %collective-permute-start.25 = (bf16[512,512]{1,0:T(8,128)(2,1)S(1)}, bf16[512,512]{1,0:T(8,128)(2,1)S(1)}, u32[]{:S(2)}, u32[]{:S(2)}) collective-permute-start(bf16[512,512]{1,0:T(8,128)(2,1)S(1)} %shard_map.55.one_ref), channel_id=1, source_target_pairs={{0,16},{4,20},{8,24},{12,28},{16,0},{20,4},{24,8},{28,12},{1,17},{... | collective-permute-start | bytes 1572872 | tf_op jit(solution)/shard_map/ppermute | solution.py:508
  55.5 18.5 %collective-permute-start.17 = (bf16[96,512]{1,0:T(8,128)(2,1)S(1)}, bf16[96,512]{1,0:T(8,128)(2,1)S(1)}, u32[]{:S(2)}, u32[]{:S(2)}) collective-permute-start(bf16[96,512]{1,0:T(8,128)(2,1)S(1)} %get-tuple-element.43), channel_id=1, source_target_pairs={{0,16},{4,20},{8,24},{12,28},{16,0},{20,4},{24,8},{28,12},{1,17},{... | collective-permute-start | bytes 294920 | tf_op jit(solution)/shard_map/ppermute | solution.py:41
  56.6 17.6 %collective-permute-start.18 = (bf16[96,512]{1,0:T(8,128)(2,1)S(1)}, bf16[96,512]{1,0:T(8,128)(2,1)S(1)}, u32[]{:S(2)}, u32[]{:S(2)}) collective-permute-start(bf16[96,512]{1,0:T(8,128)(2,1)S(1)} %get-tuple-element.44), channel_id=1, source_target_pairs={{0,12},{4,16},{8,20},{12,24},{16,28},{20,0},{24,4},{28,8},{1,13},{... | collective-permute-start | bytes 294920 | tf_op jit(solution)/shard_map/ppermute | solution.py:41
  56.6 17.6 %collective-permute-start.19 = (bf16[96,512]{1,0:T(8,128)(2,1)S(1)}, bf16[96,512]{1,0:T(8,128)(2,1)S(1)}, u32[]{:S(2)}, u32[]{:S(2)}) collective-permute-start(bf16[96,512]{1,0:T(8,128)(2,1)S(1)} %get-tuple-element.45), channel_id=1, source_target_pairs={{0,8},{4,12},{8,16},{12,20},{16,24},{20,28},{24,0},{28,4},{1,9},{5... | collective-permute-start | bytes 294920 | tf_op jit(solution)/shard_map/ppermute | solution.py:41
  85.5 8.3 %collective-permute-start.21 = (bf16[256,256]{1,0:T(8,128)(2,1)S(1)}, bf16[256,256]{1,0:T(8,128)(2,1)S(1)}, u32[]{:S(2)}, u32[]{:S(2)}) collective-permute-start(bf16[256,256]{1,0:T(8,128)(2,1)S(1)} %collective-permute-done.20.refs_1_), channel_id=1, source_target_pairs={{0,1},{1,2},{2,3},{3,0},{4,5},{5,6},{6,7},{7,4},{8,9},{9,10},{10,1... | collective-permute-start | bytes 393224 | tf_op jit(solution)/shard_map/ppermute | solution.py:35
  (7 other events, 43.0 us)
where the time goes:
time: 102 us
  waiting for transfers between devices  64.7 us (63%)
  starting transfers between devices  19.6 us (19%)
  Pallas kernels  16.2 us (16%)
    ppermute x18, waiting for transfers between devices, around(): return lax.ppermute(block, 'head', route)  42.6 us
    ppermute x8, waiting for transfers between devices, passed_along(): return lax.ppermute(block, 'seg', route)  22.1 us
    pallas_call x15, Pallas kernels, call(): pl.pallas_call(body, out_shape=tuple((jax.ShapeDtypeStruct(s, d) for s, d...  11.9 us
    ppermute x18, starting transfers between devices, around(): return lax.ppermute(block, 'head', route)  9.08 us
    ppermute x8, starting transfers between devices, passed_along(): return lax.ppermute(block, 'seg', route)  7.23 us
    ppermute x3, starting transfers between devices, gather_rows(): other = lax.ppermute(block, 'seg', [(i, i ^ step) for i in range(size)])  3.3 us
    pallas_call x1, Pallas kernels, fetch_weights(): pl.pallas_call(body, out_shape=(jax.ShapeDtypeStruct(w3.shape, w3.dtype),...  2.25 us
  transfers between devices with their start and end apart: 29, of which 21 were waited for; matrix products, arithmetic and copies ran while one was open for 0% of the time, Pallas kernels for 14%

commit v1 on v0

--- a/solution.py
+++ b/solution.py
@@ -26,7 +26,9 @@
 
 
 def ring_order(size):
-    return list(range(size))
+    ups = [i for i in range(size) if i % 2 == 1]
+    downs = [i for i in range(size) if i % 2 == 0 and i > 0]
+    return [0] + ups + downs[::-1]
 
 
 def around(block):
@@ -203,37 +205,29 @@
     return call(body, outs, [*flat, w3])
 
 
-def project_end(slots, lasts, begun, w3, col_sums, before, weight):
+def project_end(lasts, begun, w3, col_sums, kinds):
     n_chunk = len(lasts)
     piece, feats = lasts[0].shape
     width = w3.shape[2]
     rows = piece * n_chunk
-    n_head = w3.shape[1] // feats
-    last = n_head - 1
+    last = w3.shape[1] // feats - 1
 
     def body(*refs):
-        w_ref, acc_ref, mom_ref, sum_ref, before_ref, cw_ref = refs[n_chunk : n_chunk + 6]
-        q_ref, kv_ref, *outs = refs[n_chunk + 6 :]
+        w_ref, acc_ref, mom_ref, sum_ref, out_ref = refs[n_chunk:]
         for c in range(n_chunk):
             at = pl.ds(c * piece, piece)
             held = mom_ref[at, :]
             parts = [(held[:, 2 * t : 2 * t + 1], held[:, 2 * t + 1 : 2 * t + 2]) for t in range(last)]
             parts.append(moments(refs[c][...]))
             mean, inv = joined_moments(parts, feats)
-            for i in range(3):
+            for k, i in enumerate(kinds):
                 cols = slice(i * width, (i + 1) * width)
                 acc = acc_ref[at, cols] + project_sum([refs[c]], [last], w_ref, i)
-                acc = ((acc - mean * sum_ref[0:1, cols]) * inv).astype(BF16)
-                if i == 0:
-                    q_ref[at, :] = acc
-                else:
-                    kv_ref[at, (i - 1) * width : i * width] = acc
-        write_slots(slots, True, [before_ref, kv_ref], cw_ref, outs)
-
-    outs = [((rows, width), BF16), ((rows, 2 * width), BF16)]
-    outs += [((slots.rows, 2 * width), BF16)] * RATE
-    args = [*lasts, w3, *begun, col_sums, before, weight]
-    return call(body, outs, args)
+                acc = (acc - mean * sum_ref[0:1, cols]) * inv
+                out_ref[at, k * width : (k + 1) * width] = acc.astype(BF16)
+
+    outs = [((rows, len(kinds) * width), BF16)]
+    return call(body, outs, [*lasts, w3, *begun, col_sums])[0]
 
 
 class Slots:
@@ -297,12 +291,14 @@
         outs[a][...] = acc.astype(BF16)
 
 
-def compress_early(slots, source, weight):
-    def body(source_ref, w_ref, *outs):
-        write_slots(slots, False, [source_ref], w_ref, outs)
+def compress(slots, sources, weight):
+    n_in = len(sources)
+
+    def body(*refs):
+        write_slots(slots, n_in == 2, refs[:n_in], refs[n_in], refs[n_in + 1 :])
 
     outs = [((slots.rows, 2 * weight.shape[2]), BF16)] * RATE
-    return call(body, outs, [source, weight])
+    return call(body, outs, [*sources, weight])
 
 
 SCALE = math.log2(math.e) / math.sqrt(DH)
@@ -471,14 +467,21 @@
     rows = ctx.shape[0]
     columns = w_full.shape[1]
     n_extra = 1 if result is not None else 0
+    n_copy = 4 if rows % 64 == 0 else 1
+    part = rows // n_copy
 
     def body(ctx_ref, acc_ref, w_ref, *refs):
-        out_ref, held, sem = refs[n_extra:]
-        acc = acc_ref[...] + output_sum([ctx_ref], [last_step], w_ref, xored)
-        held[...] = acc.astype(BF16)
-        copy = pltpu.make_async_copy(held, out_ref.at[pl.ds(half * rows, rows), :], sem)
-        copy.start()
-        copy.wait()
+        out_ref, held, sems = refs[n_extra:]
+        acc = output_sum([ctx_ref], [last_step], w_ref, xored)
+        copies = []
+        for k in range(n_copy):
+            at = pl.ds(k * part, part)
+            held[at, :] = (acc_ref[at, :] + acc[k * part : (k + 1) * part]).astype(BF16)
+            to = out_ref.at[pl.ds(half * rows + k * part, part), :]
+            copies.append(pltpu.make_async_copy(held.at[at, :], to, sems.at[k]))
+            copies[-1].start()
+        for copy in copies:
+            copy.wait()
 
     args = [ctx, begun, w_full]
     in_specs = [vmem(), vmem(), vmem()]
@@ -492,7 +495,7 @@
         out_shape=jax.ShapeDtypeStruct((rows * n_half, columns), BF16),
         in_specs=in_specs,
         out_specs=hbm(),
-        scratch_shapes=[pltpu.VMEM((rows, columns), BF16), pltpu.SemaphoreType.DMA],
+        scratch_shapes=[pltpu.VMEM((rows, columns), BF16), pltpu.SemaphoreType.DMA((n_copy,))],
         input_output_aliases=aliases,
         compiler_params=params(),
     )(*args)
@@ -544,7 +547,7 @@
             chunk.append(around(chunk[-1]))
     w_full = gather_rows(w_out, xored)
     q0, kv0 = project(first, w_vmem, col_sums)
-    early_parts = compress_early(slots, kv0, weight)
+    early_parts = compress(slots, [kv0], weight)
     mem0 = passed_along(kv0, 1)
     early = [passed_along(p, BACK - a) for a, p in enumerate(early_parts)]
 
@@ -554,9 +557,11 @@
             chunk.append(around(chunk[-1]))
     begun = project_begin([chunk[:-1] for chunk in second], w_vmem)
     lasts = [chunk[-1] for chunk in second]
-    q1, kv1, *late = project_end(slots, lasts, begun, w_vmem, col_sums, kv0, weight)
+    kv1 = project_end(lasts, begun, w_vmem, col_sums, (1, 2))
     mem1 = passed_along(kv1, 1)
-    late = [passed_along(p, BACK - a) for a, p in enumerate(late)]
+    late_parts = compress(slots, [kv0, kv1], weight)
+    late = [passed_along(p, BACK - a) for a, p in enumerate(late_parts)]
+    q1 = project_end(lasts, begun, w_vmem, col_sums, (0,))
 
     rings = []
     for q, own in ((q0, [kv0]), (q1, [kv0, kv1])):

time: 102 us -> 98 us (0.961)
  waiting for transfers between devices: 64.7 us -> 39 us
  starting transfers between devices: 19.6 us -> 40.6 us
    ppermute x18, waiting for transfers between devices: 42.6 us -> 18.5 us  [around(): return lax.ppermute(block, 'head', route)]
    ppermute x18, starting transfers between devices: 9.08 us -> 30.1 us  [around(): return lax.ppermute(block, 'head', route)]
    ppermute x8, waiting for transfers between devices: 22.1 us -> 20.5 us  [passed_along(): return lax.ppermute(block, 'seg', route)]
    pallas_call x15 -> x17, Pallas kernels: 11.9 us -> 12.9 us  [call(): pl.pallas_call(body, out_shape=tuple((jax.ShapeDtypeStruct(s, d) for s, d...]
  transfers between devices with their start and end apart: 29 -> 29, of which waited for: 21 -> 16; matrix products, arithmetic and copies ran while one was open for 0% -> 0% of each run, Pallas kernels for 14% -> 16%
where the time goes in v1:
time: 98 us; the launch traced here: 97.8 us
  starting transfers between devices  40.6 us (41%)
  waiting for transfers between devices  39 us (40%)
  Pallas kernels  17.1 us (17%)
    ppermute x18, starting transfers between devices, around(): return lax.ppermute(block, 'head', route)  30.1 us
    ppermute x8, waiting for transfers between devices, passed_along(): return lax.ppermute(block, 'seg', route)  20.5 us
    ppermute x18, waiting for transfers between devices, around(): return lax.ppermute(block, 'head', route)  18.5 us
    pallas_call x17, Pallas kernels, call(): pl.pallas_call(body, out_shape=tuple((jax.ShapeDtypeStruct(s, d) for s, d...  12.9 us
    ppermute x8, starting transfers between devices, passed_along(): return lax.ppermute(block, 'seg', route)  7.34 us
    ppermute x3, starting transfers between devices, gather_rows(): other = lax.ppermute(block, 'seg', [(i, i ^ step) for i in range(size)])  3.13 us
    pallas_call x1, Pallas kernels, fetch_weights(): pl.pallas_call(body, out_shape=(jax.ShapeDtypeStruct(w3.shape, w3.dtype),...  2.24 us
  transfers between devices with their start and end apart: 29, of which 16 were waited for; matrix products, arithmetic and copies ran while one was open for 0% of the time, Pallas kernels for 16%

profile of v1, /device:TPU:0, one launch (start us, length us, event | category | flops | bytes accessed | tf_op | source)
XLA Modules:
  0.0 97.8 jit_solution(10320466975285366731)
XLA Ops:
  1.0 3.1 %collective-permute-start.6 = (bf16[128,512]{1,0:T(8,128)(2,1)S(1)}, bf16[128,512]{1,0:T(8,128)(2,1)S(1)}, u32[]{:S(2)}, u32[]{:S(2)}) collective-permute-start(bf16[128,512]{1,0:T(8,128)(2,1)S(1)} %get-tuple-element.31.refs_0_), channel_id=1, source_target_pairs={{0,1},{1,3},{3,2},{2,0},{4,5},{5,7},{7,6},{6,4},{8,9},{9,11},{11,1... | collective-permute-start | bytes 393224 | tf_op jit(solution)/shard_map/ppermute | solution.py:37
  4.1 2.6 %collective-permute-start.9 = (bf16[128,512]{1,0:T(8,128)(2,1)S(1)}, bf16[128,512]{1,0:T(8,128)(2,1)S(1)}, u32[]{:S(2)}, u32[]{:S(2)}) collective-permute-start(bf16[128,512]{1,0:T(8,128)(2,1)S(1)} %get-tuple-element.32.refs_4_), channel_id=1, source_target_pairs={{0,1},{1,3},{3,2},{2,0},{4,5},{5,7},{7,6},{6,4},{8,9},{9,11},{11,1... | collective-permute-start | bytes 393224 | tf_op jit(solution)/shard_map/ppermute | solution.py:37
  10.6 1.7 %collective-permute-done.9.refs_5_ = bf16[128,512]{1,0:T(8,128)(2,1)S(1)} collective-permute-done((bf16[128,512]{1,0:T(8,128)(2,1)S(1)}, bf16[128,512]{1,0:T(8,128)(2,1)S(1)}, u32[]{:S(2)}, u32[]{:S(2)}) %collective-permute-start.9) | collective-permute-done | bytes 131104 | tf_op jit(solution)/shard_map/ppermute | solution.py:37
  12.3 1.7 %collective-permute-start.10 = (bf16[128,512]{1,0:T(8,128)(2,1)S(1)}, bf16[128,512]{1,0:T(8,128)(2,1)S(1)}, u32[]{:S(2)}, u32[]{:S(2)}) collective-permute-start(bf16[128,512]{1,0:T(8,128)(2,1)S(1)} %collective-permute-done.9.refs_5_), channel_id=1, source_target_pairs={{0,1},{1,3},{3,2},{2,0},{4,5},{5,7},{7,6},{6,4},{8,9},{9,11},{11,1... | collective-permute-start | bytes 393224 | tf_op jit(solution)/shard_map/ppermute | solution.py:37
  15.1 1.7 %collective-permute-start.1 = (bf16[128,512]{1,0:T(8,128)(2,1)S(1)}, bf16[128,512]{1,0:T(8,128)(2,1)S(1)}, u32[]{:S(2)}, u32[]{:S(2)}) collective-permute-start(bf16[128,512]{1,0:T(8,128)(2,1)S(1)} %collective-permute-done.refs_1_), channel_id=1, source_target_pairs={{0,1},{1,3},{3,2},{2,0},{4,5},{5,7},{7,6},{6,4},{8,9},{9,11},{11,1... | collective-permute-start | bytes 393224 | tf_op jit(solution)/shard_map/ppermute | solution.py:37
  17.9 1.7 %collective-permute-start.4 = (bf16[128,512]{1,0:T(8,128)(2,1)S(1)}, bf16[128,512]{1,0:T(8,128)(2,1)S(1)}, u32[]{:S(2)}, u32[]{:S(2)}) collective-permute-start(bf16[128,512]{1,0:T(8,128)(2,1)S(1)} %collective-permute-done.3.refs_4_), channel_id=1, source_target_pairs={{0,1},{1,3},{3,2},{2,0},{4,5},{5,7},{7,6},{6,4},{8,9},{9,11},{11,1... | collective-permute-start | bytes 393224 | tf_op jit(solution)/shard_map/ppermute | solution.py:37
  20.7 1.7 %collective-permute-start.8 = (bf16[128,512]{1,0:T(8,128)(2,1)S(1)}, bf16[128,512]{1,0:T(8,128)(2,1)S(1)}, u32[]{:S(2)}, u32[]{:S(2)}) collective-permute-start(bf16[128,512]{1,0:T(8,128)(2,1)S(1)} %collective-permute-done.7.refs_2_), channel_id=1, source_target_pairs={{0,1},{1,3},{3,2},{2,0},{4,5},{5,7},{7,6},{6,4},{8,9},{9,11},{11,1... | collective-permute-start | bytes 393224 | tf_op jit(solution)/shard_map/ppermute | solution.py:37
  23.5 1.7 %collective-permute-start.11 = (bf16[128,512]{1,0:T(8,128)(2,1)S(1)}, bf16[128,512]{1,0:T(8,128)(2,1)S(1)}, u32[]{:S(2)}, u32[]{:S(2)}) collective-permute-start(bf16[128,512]{1,0:T(8,128)(2,1)S(1)} %collective-permute-done.10.refs_6_), channel_id=1, source_target_pairs={{0,1},{1,3},{3,2},{2,0},{4,5},{5,7},{7,6},{6,4},{8,9},{9,11},{11,1... | collective-permute-start | bytes 393224 | tf_op jit(solution)/shard_map/ppermute | solution.py:37
  26.1 1.6 %collective-permute-start.24 = (bf16[256,512]{1,0:T(8,128)(2,1)S(1)}, bf16[256,512]{1,0:T(8,128)(2,1)S(1)}, u32[]{:S(2)}, u32[]{:S(2)}) collective-permute-start(bf16[256,512]{1,0:T(8,128)(2,1)S(1)} %shard_map.56.one_ref), channel_id=1, source_target_pairs={{0,8},{4,12},{8,0},{12,4},{16,24},{20,28},{24,16},{28,20},{1,9},{5... | collective-permute-start | bytes 786440 | tf_op jit(solution)/shard_map/ppermute | solution.py:511
  27.7 2.8 %collective-permute-start.2 = (bf16[128,512]{1,0:T(8,128)(2,1)S(1)}, bf16[128,512]{1,0:T(8,128)(2,1)S(1)}, u32[]{:S(2)}, u32[]{:S(2)}) collective-permute-start(bf16[128,512]{1,0:T(8,128)(2,1)S(1)} %collective-permute-done.1.refs_2_), channel_id=1, source_target_pairs={{0,1},{1,3},{3,2},{2,0},{4,5},{5,7},{7,6},{6,4},{8,9},{9,11},{11,1... | collective-permute-start | bytes 393224 | tf_op jit(solution)/shard_map/ppermute | solution.py:37
  30.8 2.2 %fetch.1 = (bf16[3,2048,256]{2,1,0:T(8,128)(2,1)S(1)}, f32[8,768]{1,0:T(8,128)S(1)}) custom-call(bf16[3,2048,256]{2,1,0:T(8,128)(2,1)} %bitcast.3), custom_call_target="tpu_custom_call" | custom-call | tf_op jit(solution)/shard_map/fetch/pallas_call | solution.py:142
  33.1 1.7 %collective-permute-done.11.refs_7_ = bf16[128,512]{1,0:T(8,128)(2,1)S(1)} collective-permute-done((bf16[128,512]{1,0:T(8,128)(2,1)S(1)}, bf16[128,512]{1,0:T(8,128)(2,1)S(1)}, u32[]{:S(2)}, u32[]{:S(2)}) %collective-permute-start.11) | collective-permute-done | bytes 131104 | tf_op jit(solution)/shard_map/ppermute | solution.py:37
  37.5 2.0 %collective-permute-done.5.refs_1_ = bf16[128,512]{1,0:T(8,128)(2,1)S(1)} collective-permute-done((bf16[128,512]{1,0:T(8,128)(2,1)S(1)}, bf16[128,512]{1,0:T(8,128)(2,1)S(1)}, u32[]{:S(2)}, u32[]{:S(2)}) %collective-permute-start.5) | collective-permute-done | bytes 131104 | tf_op jit(solution)/shard_map/ppermute | solution.py:37
  41.0 1.6 %collective-permute-start.13 = (bf16[96,512]{1,0:T(8,128)(2,1)S(1)}, bf16[96,512]{1,0:T(8,128)(2,1)S(1)}, u32[]{:S(2)}, u32[]{:S(2)}) collective-permute-start(bf16[96,512]{1,0:T(8,128)(2,1)S(1)} %get-tuple-element.34), channel_id=1, source_target_pairs={{0,16},{4,20},{8,24},{12,28},{16,0},{20,4},{24,8},{28,12},{1,17},{... | collective-permute-start | bytes 294920 | tf_op jit(solution)/shard_map/ppermute | solution.py:43
  45.6 7.0 %collective-permute-done.13.refs_3_.refs_0_.refs_2_ = bf16[96,512]{1,0:T(8,128)(2,1)S(1)} collective-permute-done((bf16[96,512]{1,0:T(8,128)(2,1)S(1)}, bf16[96,512]{1,0:T(8,128)(2,1)S(1)}, u32[]{:S(2)}, u32[]{:S(2)}) %collective-permute-start.13) | collective-permute-done | bytes 98336 | tf_op jit(solution)/shard_map/ppermute | solution.py:43
  52.6 1.6 %collective-permute-start.25 = (bf16[512,512]{1,0:T(8,128)(2,1)S(1)}, bf16[512,512]{1,0:T(8,128)(2,1)S(1)}, u32[]{:S(2)}, u32[]{:S(2)}) collective-permute-start(bf16[512,512]{1,0:T(8,128)(2,1)S(1)} %shard_map.57.one_ref), channel_id=1, source_target_pairs={{0,16},{4,20},{8,24},{12,28},{16,0},{20,4},{24,8},{28,12},{1,17},{... | collective-permute-start | bytes 1572872 | tf_op jit(solution)/shard_map/ppermute | solution.py:511
  55.3 1.9 %collective-permute-start.19 = (bf16[96,512]{1,0:T(8,128)(2,1)S(1)}, bf16[96,512]{1,0:T(8,128)(2,1)S(1)}, u32[]{:S(2)}, u32[]{:S(2)}) collective-permute-start(bf16[96,512]{1,0:T(8,128)(2,1)S(1)} %get-tuple-element.41), channel_id=1, source_target_pairs={{0,8},{4,12},{8,16},{12,20},{16,24},{20,28},{24,0},{28,4},{1,9},{5... | collective-permute-start | bytes 294920 | tf_op jit(solution)/shard_map/ppermute | solution.py:43
  59.3 13.3 %collective-permute-done.17.refs_3_ = bf16[96,512]{1,0:T(8,128)(2,1)S(1)} collective-permute-done((bf16[96,512]{1,0:T(8,128)(2,1)S(1)}, bf16[96,512]{1,0:T(8,128)(2,1)S(1)}, u32[]{:S(2)}, u32[]{:S(2)}) %collective-permute-start.17) | collective-permute-done | bytes 98336 | tf_op jit(solution)/shard_map/ppermute | solution.py:43
  77.6 3.4 %collective-permute-start.20 = (bf16[256,256]{1,0:T(8,128)(2,1)S(1)}, bf16[256,256]{1,0:T(8,128)(2,1)S(1)}, u32[]{:S(2)}, u32[]{:S(2)}) collective-permute-start(bf16[256,256]{1,0:T(8,128)(2,1)S(1)} %shard_map.55.refs_0_), channel_id=1, source_target_pairs={{0,1},{1,3},{3,2},{2,0},{4,5},{5,7},{7,6},{6,4},{8,9},{9,11},{11,1... | collective-permute-start | bytes 393224 | tf_op jit(solution)/shard_map/ppermute | solution.py:37
  81.5 3.0 %collective-permute-done.20.refs_1_ = bf16[256,256]{1,0:T(8,128)(2,1)S(1)} collective-permute-done((bf16[256,256]{1,0:T(8,128)(2,1)S(1)}, bf16[256,256]{1,0:T(8,128)(2,1)S(1)}, u32[]{:S(2)}, u32[]{:S(2)}) %collective-permute-start.20) | collective-permute-done | bytes 131104 | tf_op jit(solution)/shard_map/ppermute | solution.py:37
  84.6 2.5 %collective-permute-start.21 = (bf16[256,256]{1,0:T(8,128)(2,1)S(1)}, bf16[256,256]{1,0:T(8,128)(2,1)S(1)}, u32[]{:S(2)}, u32[]{:S(2)}) collective-permute-start(bf16[256,256]{1,0:T(8,128)(2,1)S(1)} %collective-permute-done.20.refs_1_), channel_id=1, source_target_pairs={{0,1},{1,3},{3,2},{2,0},{4,5},{5,7},{7,6},{6,4},{8,9},{9,11},{11,1... | collective-permute-start | bytes 393224 | tf_op jit(solution)/shard_map/ppermute | solution.py:37
  87.8 2.0 %collective-permute-start.28 = (bf16[256,256]{1,0:T(8,128)(2,1)S(1)}, bf16[256,256]{1,0:T(8,128)(2,1)S(1)}, u32[]{:S(2)}, u32[]{:S(2)}) collective-permute-start(bf16[256,256]{1,0:T(8,128)(2,1)S(1)} %collective-permute-done.27.refs_2_), channel_id=1, source_target_pairs={{0,1},{1,3},{3,2},{2,0},{4,5},{5,7},{7,6},{6,4},{8,9},{9,11},{11,1... | collective-permute-start | bytes 393224 | tf_op jit(solution)/shard_map/ppermute | solution.py:37
  91.0 1.8 %collective-permute-start.22 = (bf16[256,256]{1,0:T(8,128)(2,1)S(1)}, bf16[256,256]{1,0:T(8,128)(2,1)S(1)}, u32[]{:S(2)}, u32[]{:S(2)}) collective-permute-start(bf16[256,256]{1,0:T(8,128)(2,1)S(1)} %collective-permute-done.21.refs_2_), channel_id=1, source_target_pairs={{0,1},{1,3},{3,2},{2,0},{4,5},{5,7},{7,6},{6,4},{8,9},{9,11},{11,1... | collective-permute-start | bytes 393224 | tf_op jit(solution)/shard_map/ppermute | solution.py:37
  95.0 1.9 %collective-permute-done.22.ctx_ref = bf16[256,256]{1,0:T(8,128)(2,1)S(1)} collective-permute-done((bf16[256,256]{1,0:T(8,128)(2,1)S(1)}, bf16[256,256]{1,0:T(8,128)(2,1)S(1)}, u32[]{:S(2)}, u32[]{:S(2)}) %collective-permute-start.22) | collective-permute-done | bytes 131104 | tf_op jit(solution)/shard_map/ppermute | solution.py:37
  (58 shorter events, 31.5 us)
Async XLA Ops:
  1.0 8.5 %collective-permute-start.6 = (bf16[128,512]{1,0:T(8,128)(2,1)S(1)}, bf16[128,512]{1,0:T(8,128)(2,1)S(1)}, u32[]{:S(2)}, u32[]{:S(2)}) collective-permute-start(bf16[128,512]{1,0:T(8,128)(2,1)S(1)} %get-tuple-element.31.refs_0_), channel_id=1, source_target_pairs={{0,1},{1,3},{3,2},{2,0},{4,5},{5,7},{7,6},{6,4},{8,9},{9,11},{11,1... | collective-permute-start | bytes 393224 | tf_op jit(solution)/shard_map/ppermute | solution.py:37
  4.1 8.2 %collective-permute-start.9 = (bf16[128,512]{1,0:T(8,128)(2,1)S(1)}, bf16[128,512]{1,0:T(8,128)(2,1)S(1)}, u32[]{:S(2)}, u32[]{:S(2)}) collective-permute-start(bf16[128,512]{1,0:T(8,128)(2,1)S(1)} %get-tuple-element.32.refs_4_), channel_id=1, source_target_pairs={{0,1},{1,3},{3,2},{2,0},{4,5},{5,7},{7,6},{6,4},{8,9},{9,11},{11,1... | collective-permute-start | bytes 393224 | tf_op jit(solution)/shard_map/ppermute | solution.py:37
  7.7 7.4 %collective-permute-start = (bf16[128,512]{1,0:T(8,128)(2,1)S(1)}, bf16[128,512]{1,0:T(8,128)(2,1)S(1)}, u32[]{:S(2)}, u32[]{:S(2)}) collective-permute-start(bf16[128,512]{1,0:T(8,128)(2,1)S(1)} %get-tuple-element.25.refs_0_), channel_id=1, source_target_pairs={{0,1},{1,3},{3,2},{2,0},{4,5},{5,7},{7,6},{6,4},{8,9},{9,11},{11,1... | collective-permute-start | bytes 393224 | tf_op jit(solution)/shard_map/ppermute | solution.py:37
  8.2 9.7 %collective-permute-start.3 = (bf16[128,512]{1,0:T(8,128)(2,1)S(1)}, bf16[128,512]{1,0:T(8,128)(2,1)S(1)}, u32[]{:S(2)}, u32[]{:S(2)}) collective-permute-start(bf16[128,512]{1,0:T(8,128)(2,1)S(1)} %get-tuple-element.26.refs_3_), channel_id=1, source_target_pairs={{0,1},{1,3},{3,2},{2,0},{4,5},{5,7},{7,6},{6,4},{8,9},{9,11},{11,1... | collective-permute-start | bytes 393224 | tf_op jit(solution)/shard_map/ppermute | solution.py:37
  9.5 11.2 %collective-permute-start.7 = (bf16[128,512]{1,0:T(8,128)(2,1)S(1)}, bf16[128,512]{1,0:T(8,128)(2,1)S(1)}, u32[]{:S(2)}, u32[]{:S(2)}) collective-permute-start(bf16[128,512]{1,0:T(8,128)(2,1)S(1)} %collective-permute-done.6.refs_1_), channel_id=1, source_target_pairs={{0,1},{1,3},{3,2},{2,0},{4,5},{5,7},{7,6},{6,4},{8,9},{9,11},{11,1... | collective-permute-start | bytes 393224 | tf_op jit(solution)/shard_map/ppermute | solution.py:37
  12.3 11.2 %collective-permute-start.10 = (bf16[128,512]{1,0:T(8,128)(2,1)S(1)}, bf16[128,512]{1,0:T(8,128)(2,1)S(1)}, u32[]{:S(2)}, u32[]{:S(2)}) collective-permute-start(bf16[128,512]{1,0:T(8,128)(2,1)S(1)} %collective-permute-done.9.refs_5_), channel_id=1, source_target_pairs={{0,1},{1,3},{3,2},{2,0},{4,5},{5,7},{7,6},{6,4},{8,9},{9,11},{11,1... | collective-permute-start | bytes 393224 | tf_op jit(solution)/shard_map/ppermute | solution.py:37
  14.0 11.2 %collective-permute-start.23 = (bf16[128,512]{1,0:T(8,128)(2,1)}, bf16[128,512]{1,0:T(8,128)(2,1)S(1)}, u32[]{:S(2)}, u32[]{:S(2)}) collective-permute-start(bf16[128,512]{1,0:T(8,128)(2,1)} %one_ref.1), channel_id=1, source_target_pairs={{0,4},{4,0},{8,12},{12,8},{16,20},{20,16},{24,28},{28,24},{1,5},{5... | collective-permute-start | bytes 393224 | tf_op jit(solution)/shard_map/ppermute | solution.py:511
  15.1 12.6 %collective-permute-start.1 = (bf16[128,512]{1,0:T(8,128)(2,1)S(1)}, bf16[128,512]{1,0:T(8,128)(2,1)S(1)}, u32[]{:S(2)}, u32[]{:S(2)}) collective-permute-start(bf16[128,512]{1,0:T(8,128)(2,1)S(1)} %collective-permute-done.refs_1_), channel_id=1, source_target_pairs={{0,1},{1,3},{3,2},{2,0},{4,5},{5,7},{7,6},{6,4},{8,9},{9,11},{11,1... | collective-permute-start | bytes 393224 | tf_op jit(solution)/shard_map/ppermute | solution.py:37
  17.9 12.6 %collective-permute-start.4 = (bf16[128,512]{1,0:T(8,128)(2,1)S(1)}, bf16[128,512]{1,0:T(8,128)(2,1)S(1)}, u32[]{:S(2)}, u32[]{:S(2)}) collective-permute-start(bf16[128,512]{1,0:T(8,128)(2,1)S(1)} %collective-permute-done.3.refs_4_), channel_id=1, source_target_pairs={{0,1},{1,3},{3,2},{2,0},{4,5},{5,7},{7,6},{6,4},{8,9},{9,11},{11,1... | collective-permute-start | bytes 393224 | tf_op jit(solution)/shard_map/ppermute | solution.py:37
  20.7 12.4 %collective-permute-start.8 = (bf16[128,512]{1,0:T(8,128)(2,1)S(1)}, bf16[128,512]{1,0:T(8,128)(2,1)S(1)}, u32[]{:S(2)}, u32[]{:S(2)}) collective-permute-start(bf16[128,512]{1,0:T(8,128)(2,1)S(1)} %collective-permute-done.7.refs_2_), channel_id=1, source_target_pairs={{0,1},{1,3},{3,2},{2,0},{4,5},{5,7},{7,6},{6,4},{8,9},{9,11},{11,1... | collective-permute-start | bytes 393224 | tf_op jit(solution)/shard_map/ppermute | solution.py:37
  23.5 11.2 %collective-permute-start.11 = (bf16[128,512]{1,0:T(8,128)(2,1)S(1)}, bf16[128,512]{1,0:T(8,128)(2,1)S(1)}, u32[]{:S(2)}, u32[]{:S(2)}) collective-permute-start(bf16[128,512]{1,0:T(8,128)(2,1)S(1)} %collective-permute-done.10.refs_6_), channel_id=1, source_target_pairs={{0,1},{1,3},{3,2},{2,0},{4,5},{5,7},{7,6},{6,4},{8,9},{9,11},{11,1... | collective-permute-start | bytes 393224 | tf_op jit(solution)/shard_map/ppermute | solution.py:37
  26.1 17.9 %collective-permute-start.24 = (bf16[256,512]{1,0:T(8,128)(2,1)S(1)}, bf16[256,512]{1,0:T(8,128)(2,1)S(1)}, u32[]{:S(2)}, u32[]{:S(2)}) collective-permute-start(bf16[256,512]{1,0:T(8,128)(2,1)S(1)} %shard_map.56.one_ref), channel_id=1, source_target_pairs={{0,8},{4,12},{8,0},{12,4},{16,24},{20,28},{24,16},{28,20},{1,9},{5... | collective-permute-start | bytes 786440 | tf_op jit(solution)/shard_map/ppermute | solution.py:511
  27.7 9.9 %collective-permute-start.2 = (bf16[128,512]{1,0:T(8,128)(2,1)S(1)}, bf16[128,512]{1,0:T(8,128)(2,1)S(1)}, u32[]{:S(2)}, u32[]{:S(2)}) collective-permute-start(bf16[128,512]{1,0:T(8,128)(2,1)S(1)} %collective-permute-done.1.refs_2_), channel_id=1, source_target_pairs={{0,1},{1,3},{3,2},{2,0},{4,5},{5,7},{7,6},{6,4},{8,9},{9,11},{11,1... | collective-permute-start | bytes 393224 | tf_op jit(solution)/shard_map/ppermute | solution.py:37
  30.5 9.0 %collective-permute-start.5 = (bf16[128,512]{1,0:T(8,128)(2,1)S(1)}, bf16[128,512]{1,0:T(8,128)(2,1)S(1)}, u32[]{:S(2)}, u32[]{:S(2)}) collective-permute-start(bf16[128,512]{1,0:T(8,128)(2,1)S(1)} %collective-permute-done.4.refs_5_), channel_id=1, source_target_pairs={{0,1},{1,3},{3,2},{2,0},{4,5},{5,7},{7,6},{6,4},{8,9},{9,11},{11,1... | collective-permute-start | bytes 393224 | tf_op jit(solution)/shard_map/ppermute | solution.py:37
  36.0 19.3 %collective-permute-start.12 = (bf16[256,512]{1,0:T(8,128)(2,1)S(1)}, bf16[256,512]{1,0:T(8,128)(2,1)S(1)}, u32[]{:S(2)}, u32[]{:S(2)}) collective-permute-start(bf16[256,512]{1,0:T(8,128)(2,1)S(1)} %get-tuple-element.33.refs_0_), channel_id=1, source_target_pairs={{0,4},{4,8},{8,12},{12,16},{16,20},{20,24},{24,28},{28,0},{1,5},{5... | collective-permute-start | bytes 786440 | tf_op jit(solution)/shard_map/ppermute | solution.py:43
  40.6 32.2 %collective-permute-start.16 = (bf16[256,512]{1,0:T(8,128)(2,1)S(1)}, bf16[256,512]{1,0:T(8,128)(2,1)S(1)}, u32[]{:S(2)}, u32[]{:S(2)}) collective-permute-start(bf16[256,512]{1,0:T(8,128)(2,1)S(1)} %shard_map.51.refs_1_), channel_id=1, source_target_pairs={{0,4},{4,8},{8,12},{12,16},{16,20},{20,24},{24,28},{28,0},{1,5},{5... | collective-permute-start | bytes 786440 | tf_op jit(solution)/shard_map/ppermute | solution.py:43
  41.0 11.6 %collective-permute-start.13 = (bf16[96,512]{1,0:T(8,128)(2,1)S(1)}, bf16[96,512]{1,0:T(8,128)(2,1)S(1)}, u32[]{:S(2)}, u32[]{:S(2)}) collective-permute-start(bf16[96,512]{1,0:T(8,128)(2,1)S(1)} %get-tuple-element.34), channel_id=1, source_target_pairs={{0,16},{4,20},{8,24},{12,28},{16,0},{20,4},{24,8},{28,12},{1,17},{... | collective-permute-start | bytes 294920 | tf_op jit(solution)/shard_map/ppermute | solution.py:43
  42.7 11.8 %collective-permute-start.14 = (bf16[96,512]{1,0:T(8,128)(2,1)S(1)}, bf16[96,512]{1,0:T(8,128)(2,1)S(1)}, u32[]{:S(2)}, u32[]{:S(2)}) collective-permute-start(bf16[96,512]{1,0:T(8,128)(2,1)S(1)} %get-tuple-element.35), channel_id=1, source_target_pairs={{0,12},{4,16},{8,20},{12,24},{16,28},{20,0},{24,4},{28,8},{1,13},{... | collective-permute-start | bytes 294920 | tf_op jit(solution)/shard_map/ppermute | solution.py:43
  44.0 11.3 %collective-permute-start.15 = (bf16[96,512]{1,0:T(8,128)(2,1)S(1)}, bf16[96,512]{1,0:T(8,128)(2,1)S(1)}, u32[]{:S(2)}, u32[]{:S(2)}) collective-permute-start(bf16[96,512]{1,0:T(8,128)(2,1)S(1)} %get-tuple-element.36), channel_id=1, source_target_pairs={{0,8},{4,12},{8,16},{12,20},{16,24},{20,28},{24,0},{28,4},{1,9},{5... | collective-permute-start | bytes 294920 | tf_op jit(solution)/shard_map/ppermute | solution.py:43
  52.6 40.2 %collective-permute-start.25 = (bf16[512,512]{1,0:T(8,128)(2,1)S(1)}, bf16[512,512]{1,0:T(8,128)(2,1)S(1)}, u32[]{:S(2)}, u32[]{:S(2)}) collective-permute-start(bf16[512,512]{1,0:T(8,128)(2,1)S(1)} %shard_map.57.one_ref), channel_id=1, source_target_pairs={{0,16},{4,20},{8,24},{12,28},{16,0},{20,4},{24,8},{28,12},{1,17},{... | collective-permute-start | bytes 1572872 | tf_op jit(solution)/shard_map/ppermute | solution.py:511
  54.5 18.2 %collective-permute-start.17 = (bf16[96,512]{1,0:T(8,128)(2,1)S(1)}, bf16[96,512]{1,0:T(8,128)(2,1)S(1)}, u32[]{:S(2)}, u32[]{:S(2)}) collective-permute-start(bf16[96,512]{1,0:T(8,128)(2,1)S(1)} %get-tuple-element.39), channel_id=1, source_target_pairs={{0,16},{4,20},{8,24},{12,28},{16,0},{20,4},{24,8},{28,12},{1,17},{... | collective-permute-start | bytes 294920 | tf_op jit(solution)/shard_map/ppermute | solution.py:43
  55.3 17.6 %collective-permute-start.18 = (bf16[96,512]{1,0:T(8,128)(2,1)S(1)}, bf16[96,512]{1,0:T(8,128)(2,1)S(1)}, u32[]{:S(2)}, u32[]{:S(2)}) collective-permute-start(bf16[96,512]{1,0:T(8,128)(2,1)S(1)} %get-tuple-element.40), channel_id=1, source_target_pairs={{0,12},{4,16},{8,20},{12,24},{16,28},{20,0},{24,4},{28,8},{1,13},{... | collective-permute-start | bytes 294920 | tf_op jit(solution)/shard_map/ppermute | solution.py:43
  55.3 17.6 %collective-permute-start.19 = (bf16[96,512]{1,0:T(8,128)(2,1)S(1)}, bf16[96,512]{1,0:T(8,128)(2,1)S(1)}, u32[]{:S(2)}, u32[]{:S(2)}) collective-permute-start(bf16[96,512]{1,0:T(8,128)(2,1)S(1)} %get-tuple-element.41), channel_id=1, source_target_pairs={{0,8},{4,12},{8,16},{12,20},{16,24},{20,28},{24,0},{28,4},{1,9},{5... | collective-permute-start | bytes 294920 | tf_op jit(solution)/shard_map/ppermute | solution.py:43
  77.6 7.0 %collective-permute-start.20 = (bf16[256,256]{1,0:T(8,128)(2,1)S(1)}, bf16[256,256]{1,0:T(8,128)(2,1)S(1)}, u32[]{:S(2)}, u32[]{:S(2)}) collective-permute-start(bf16[256,256]{1,0:T(8,128)(2,1)S(1)} %shard_map.55.refs_0_), channel_id=1, source_target_pairs={{0,1},{1,3},{3,2},{2,0},{4,5},{5,7},{7,6},{6,4},{8,9},{9,11},{11,1... | collective-permute-start | bytes 393224 | tf_op jit(solution)/shard_map/ppermute | solution.py:37
  (7 other events, 36.8 us)

commit v2 on v1

--- a/solution.py
+++ b/solution.py
@@ -25,14 +25,19 @@
     return pl.BlockSpec(memory_space=pltpu.VMEM)
 
 
-def ring_order(size):
+def folded_ring(size):
     ups = [i for i in range(size) if i % 2 == 1]
     downs = [i for i in range(size) if i % 2 == 0 and i > 0]
     return [0] + ups + downs[::-1]
 
 
-def around(block):
-    order = ring_order(lax.axis_size("head"))
+IN_RING = folded_ring
+OUT_RING = folded_ring
+EARLY = 8
+EARLY_PARTS, LATE_PARTS = 2, 2
+
+
+def around(block, order):
     route = [(a, b) for a, b in zip(order, order[1:] + order[:1])]
     return lax.ppermute(block, "head", route)
 
@@ -43,8 +48,8 @@
     return lax.ppermute(block, "seg", route)
 
 
-def source_of(step, size):
-    order = ring_order(size)
+def source_of(step, order):
+    size = len(order)
     z = lax.axis_index("head")
     found = jnp.int32(0)
     for here in range(size):
@@ -119,7 +124,7 @@
     acc = None
     for t, block in zip(steps, blocks):
         part = jnp.dot(
-            block[...], weight_rows(w_ref, i, source_of(t, size), feats), preferred_element_type=F32
+            block[...], weight_rows(w_ref, i, source_of(t, IN_RING(size)), feats), preferred_element_type=F32
         )
         acc = part if acc is None else acc + part
     return acc
@@ -450,7 +455,7 @@
     acc = None
     for t, c in zip(steps, ctx):
         for k in range(width // unit):
-            block = source_of(t, size) * (width // unit) + k
+            block = source_of(t, OUT_RING(size)) * (width // unit) + k
             if xored:
                 block = lax.bitwise_xor(block, lax.axis_index("seg"))
             start = pl.multiple_of(block * unit, unit)
@@ -463,7 +468,7 @@
     return acc
 
 
-def output_end(half, n_half, last_step, ctx, begun, w_full, xored, result):
+def output_end(offset, n_rows, last_step, ctx, begun, w_full, xored, result):
     rows = ctx.shape[0]
     columns = w_full.shape[1]
     n_extra = 1 if result is not None else 0
@@ -477,7 +482,7 @@
         for k in range(n_copy):
             at = pl.ds(k * part, part)
             held[at, :] = (acc_ref[at, :] + acc[k * part : (k + 1) * part]).astype(BF16)
-            to = out_ref.at[pl.ds(half * rows + k * part, part), :]
+            to = out_ref.at[pl.ds(offset + k * part, part), :]
             copies.append(pltpu.make_async_copy(held.at[at, :], to, sems.at[k]))
             copies[-1].start()
         for copy in copies:
@@ -492,7 +497,7 @@
         aliases = {3: 0}
     return pl.pallas_call(
         body,
-        out_shape=jax.ShapeDtypeStruct((rows * n_half, columns), BF16),
+        out_shape=jax.ShapeDtypeStruct((n_rows, columns), BF16),
         in_specs=in_specs,
         out_specs=hbm(),
         scratch_shapes=[pltpu.VMEM((rows, columns), BF16), pltpu.SemaphoreType.DMA((n_copy,))],
@@ -528,15 +533,15 @@
     width = w_qkv.shape[2]
     weight = comp_weight
 
-    n_chunk, n_half = 4, 2
-    per_half = n_chunk // n_half
-    piece = seg_len // n_chunk
-    half_rows = seg_len // n_half
-    slots = Slots(seg_len, half_rows)
-
-    starts = [c * piece for c in range(n_chunk)]
-    first = [[chunk] for chunk in split(rows, starts[:per_half], piece)]
+    early_rows = seg_len * EARLY // 16
+    early_piece, late_piece = early_rows // EARLY_PARTS, (seg_len - early_rows) // LATE_PARTS
+    slots = Slots(seg_len, early_rows)
+    starts = [c * early_piece for c in range(EARLY_PARTS)]
+    first = [[chunk] for chunk in split(rows, starts, early_piece)]
+    starts = [early_rows + c * late_piece for c in range(LATE_PARTS)]
+    second = [[chunk] for chunk in split(rows, starts, late_piece)]
     n_seg = lax.axis_size("seg")
+    in_ring, out_ring = IN_RING(n_head), OUT_RING(n_head)
     own_rows = w_out.shape[0]
     power = n_seg & (n_seg - 1) == 0
     xored = own_rows if power and own_rows % DH == 0 and width % own_rows == 0 else 0
@@ -544,17 +549,16 @@
     w_vmem, col_sums = fetch_weights(w3)
     for _ in range(1, n_head):
         for chunk in first:
-            chunk.append(around(chunk[-1]))
+            chunk.append(around(chunk[-1], in_ring))
     w_full = gather_rows(w_out, xored)
     q0, kv0 = project(first, w_vmem, col_sums)
     early_parts = compress(slots, [kv0], weight)
     mem0 = passed_along(kv0, 1)
     early = [passed_along(p, BACK - a) for a, p in enumerate(early_parts)]
 
-    second = [[chunk] for chunk in split(rows, starts[per_half:], piece)]
     for _ in range(1, n_head):
         for chunk in second:
-            chunk.append(around(chunk[-1]))
+            chunk.append(around(chunk[-1], in_ring))
     begun = project_begin([chunk[:-1] for chunk in second], w_vmem)
     lasts = [chunk[-1] for chunk in second]
     kv1 = project_end(lasts, begun, w_vmem, col_sums, (1, 2))
@@ -570,11 +574,13 @@
         rings.append([ctx])
     for _ in range(1, n_head):
         for ring in rings:
-            ring.append(around(ring[-1]))
+            ring.append(around(ring[-1], out_ring))
     result = None
     for h, ring in enumerate(rings):
         part = output_begin(ring[:-1], w_full, xored)
-        result = output_end(h, n_half, n_head - 1, ring[-1], part, w_full, xored, result)
+        result = output_end(
+            h * early_rows, seg_len, n_head - 1, ring[-1], part, w_full, xored, result,
+        )
     return result[None]
 
 

time: 98 us -> 98 us (level)
  no operation moved by 1% of the time
where the time goes in v2:
time: 98 us; the launch traced here: 97.8 us
  starting transfers between devices  40.6 us (41%)
  waiting for transfers between devices  39 us (40%)
  Pallas kernels  17.1 us (17%)
    ppermute x18, starting transfers between devices, around(): return lax.ppermute(block, 'head', route)  30.1 us
    ppermute x8, waiting for transfers between devices, passed_along(): return lax.ppermute(block, 'seg', route)  20.5 us
    ppermute x18, waiting for transfers between devices, around(): return lax.ppermute(block, 'head', route)  18.5 us
    pallas_call x17, Pallas kernels, call(): pl.pallas_call(body, out_shape=tuple((jax.ShapeDtypeStruct(s, d) for s, d...  12.9 us
    ppermute x8, starting transfers between devices, passed_along(): return lax.ppermute(block, 'seg', route)  7.34 us
    ppermute x3, starting transfers between devices, gather_rows(): other = lax.ppermute(block, 'seg', [(i, i ^ step) for i in range(size)])  3.13 us
    pallas_call x1, Pallas kernels, fetch_weights(): pl.pallas_call(body, out_shape=(jax.ShapeDtypeStruct(w3.shape, w3.dtype),...  2.24 us
  transfers between devices with their start and end apart: 29, of which 16 were waited for; matrix products, arithmetic and copies ran while one was open for 0% of the time, Pallas kernels for 16%

profile of v2, /device:TPU:0, one launch (start us, length us, event | category | flops | bytes accessed | tf_op | source)
XLA Modules:
  0.0 97.8 jit_solution(10320466975285366731)
XLA Ops:
  1.0 3.1 %collective-permute-start.6 = (bf16[128,512]{1,0:T(8,128)(2,1)S(1)}, bf16[128,512]{1,0:T(8,128)(2,1)S(1)}, u32[]{:S(2)}, u32[]{:S(2)}) collective-permute-start(bf16[128,512]{1,0:T(8,128)(2,1)S(1)} %get-tuple-element.31.refs_0_), channel_id=1, source_target_pairs={{0,1},{1,3},{3,2},{2,0},{4,5},{5,7},{7,6},{6,4},{8,9},{9,11},{11,1... | collective-permute-start | bytes 393224 | tf_op jit(solution)/shard_map/ppermute | solution.py:42
  4.1 2.6 %collective-permute-start.9 = (bf16[128,512]{1,0:T(8,128)(2,1)S(1)}, bf16[128,512]{1,0:T(8,128)(2,1)S(1)}, u32[]{:S(2)}, u32[]{:S(2)}) collective-permute-start(bf16[128,512]{1,0:T(8,128)(2,1)S(1)} %get-tuple-element.32.refs_4_), channel_id=1, source_target_pairs={{0,1},{1,3},{3,2},{2,0},{4,5},{5,7},{7,6},{6,4},{8,9},{9,11},{11,1... | collective-permute-start | bytes 393224 | tf_op jit(solution)/shard_map/ppermute | solution.py:42
  10.6 1.7 %collective-permute-done.9.refs_5_ = bf16[128,512]{1,0:T(8,128)(2,1)S(1)} collective-permute-done((bf16[128,512]{1,0:T(8,128)(2,1)S(1)}, bf16[128,512]{1,0:T(8,128)(2,1)S(1)}, u32[]{:S(2)}, u32[]{:S(2)}) %collective-permute-start.9) | collective-permute-done | bytes 131104 | tf_op jit(solution)/shard_map/ppermute | solution.py:42
  12.3 1.7 %collective-permute-start.10 = (bf16[128,512]{1,0:T(8,128)(2,1)S(1)}, bf16[128,512]{1,0:T(8,128)(2,1)S(1)}, u32[]{:S(2)}, u32[]{:S(2)}) collective-permute-start(bf16[128,512]{1,0:T(8,128)(2,1)S(1)} %collective-permute-done.9.refs_5_), channel_id=1, source_target_pairs={{0,1},{1,3},{3,2},{2,0},{4,5},{5,7},{7,6},{6,4},{8,9},{9,11},{11,1... | collective-permute-start | bytes 393224 | tf_op jit(solution)/shard_map/ppermute | solution.py:42
  15.1 1.7 %collective-permute-start.1 = (bf16[128,512]{1,0:T(8,128)(2,1)S(1)}, bf16[128,512]{1,0:T(8,128)(2,1)S(1)}, u32[]{:S(2)}, u32[]{:S(2)}) collective-permute-start(bf16[128,512]{1,0:T(8,128)(2,1)S(1)} %collective-permute-done.refs_1_), channel_id=1, source_target_pairs={{0,1},{1,3},{3,2},{2,0},{4,5},{5,7},{7,6},{6,4},{8,9},{9,11},{11,1... | collective-permute-start | bytes 393224 | tf_op jit(solution)/shard_map/ppermute | solution.py:42
  17.9 1.7 %collective-permute-start.4 = (bf16[128,512]{1,0:T(8,128)(2,1)S(1)}, bf16[128,512]{1,0:T(8,128)(2,1)S(1)}, u32[]{:S(2)}, u32[]{:S(2)}) collective-permute-start(bf16[128,512]{1,0:T(8,128)(2,1)S(1)} %collective-permute-done.3.refs_4_), channel_id=1, source_target_pairs={{0,1},{1,3},{3,2},{2,0},{4,5},{5,7},{7,6},{6,4},{8,9},{9,11},{11,1... | collective-permute-start | bytes 393224 | tf_op jit(solution)/shard_map/ppermute | solution.py:42
  20.7 1.7 %collective-permute-start.8 = (bf16[128,512]{1,0:T(8,128)(2,1)S(1)}, bf16[128,512]{1,0:T(8,128)(2,1)S(1)}, u32[]{:S(2)}, u32[]{:S(2)}) collective-permute-start(bf16[128,512]{1,0:T(8,128)(2,1)S(1)} %collective-permute-done.7.refs_2_), channel_id=1, source_target_pairs={{0,1},{1,3},{3,2},{2,0},{4,5},{5,7},{7,6},{6,4},{8,9},{9,11},{11,1... | collective-permute-start | bytes 393224 | tf_op jit(solution)/shard_map/ppermute | solution.py:42
  23.5 1.7 %collective-permute-start.11 = (bf16[128,512]{1,0:T(8,128)(2,1)S(1)}, bf16[128,512]{1,0:T(8,128)(2,1)S(1)}, u32[]{:S(2)}, u32[]{:S(2)}) collective-permute-start(bf16[128,512]{1,0:T(8,128)(2,1)S(1)} %collective-permute-done.10.refs_6_), channel_id=1, source_target_pairs={{0,1},{1,3},{3,2},{2,0},{4,5},{5,7},{7,6},{6,4},{8,9},{9,11},{11,1... | collective-permute-start | bytes 393224 | tf_op jit(solution)/shard_map/ppermute | solution.py:42
  26.1 1.6 %collective-permute-start.24 = (bf16[256,512]{1,0:T(8,128)(2,1)S(1)}, bf16[256,512]{1,0:T(8,128)(2,1)S(1)}, u32[]{:S(2)}, u32[]{:S(2)}) collective-permute-start(bf16[256,512]{1,0:T(8,128)(2,1)S(1)} %shard_map.56.one_ref), channel_id=1, source_target_pairs={{0,8},{4,12},{8,0},{12,4},{16,24},{20,28},{24,16},{28,20},{1,9},{5... | collective-permute-start | bytes 786440 | tf_op jit(solution)/shard_map/ppermute | solution.py:516
  27.7 2.8 %collective-permute-start.2 = (bf16[128,512]{1,0:T(8,128)(2,1)S(1)}, bf16[128,512]{1,0:T(8,128)(2,1)S(1)}, u32[]{:S(2)}, u32[]{:S(2)}) collective-permute-start(bf16[128,512]{1,0:T(8,128)(2,1)S(1)} %collective-permute-done.1.refs_2_), channel_id=1, source_target_pairs={{0,1},{1,3},{3,2},{2,0},{4,5},{5,7},{7,6},{6,4},{8,9},{9,11},{11,1... | collective-permute-start | bytes 393224 | tf_op jit(solution)/shard_map/ppermute | solution.py:42
  30.8 2.2 %fetch.1 = (bf16[3,2048,256]{2,1,0:T(8,128)(2,1)S(1)}, f32[8,768]{1,0:T(8,128)S(1)}) custom-call(bf16[3,2048,256]{2,1,0:T(8,128)(2,1)} %bitcast.3), custom_call_target="tpu_custom_call" | custom-call | tf_op jit(solution)/shard_map/fetch/pallas_call | solution.py:147
  33.1 1.7 %collective-permute-done.11.refs_7_ = bf16[128,512]{1,0:T(8,128)(2,1)S(1)} collective-permute-done((bf16[128,512]{1,0:T(8,128)(2,1)S(1)}, bf16[128,512]{1,0:T(8,128)(2,1)S(1)}, u32[]{:S(2)}, u32[]{:S(2)}) %collective-permute-start.11) | collective-permute-done | bytes 131104 | tf_op jit(solution)/shard_map/ppermute | solution.py:42
  37.5 2.0 %collective-permute-done.5.refs_1_ = bf16[128,512]{1,0:T(8,128)(2,1)S(1)} collective-permute-done((bf16[128,512]{1,0:T(8,128)(2,1)S(1)}, bf16[128,512]{1,0:T(8,128)(2,1)S(1)}, u32[]{:S(2)}, u32[]{:S(2)}) %collective-permute-start.5) | collective-permute-done | bytes 131104 | tf_op jit(solution)/shard_map/ppermute | solution.py:42
  41.0 1.6 %collective-permute-start.13 = (bf16[96,512]{1,0:T(8,128)(2,1)S(1)}, bf16[96,512]{1,0:T(8,128)(2,1)S(1)}, u32[]{:S(2)}, u32[]{:S(2)}) collective-permute-start(bf16[96,512]{1,0:T(8,128)(2,1)S(1)} %get-tuple-element.34), channel_id=1, source_target_pairs={{0,16},{4,20},{8,24},{12,28},{16,0},{20,4},{24,8},{28,12},{1,17},{... | collective-permute-start | bytes 294920 | tf_op jit(solution)/shard_map/ppermute | solution.py:48
  45.6 7.0 %collective-permute-done.13.refs_3_.refs_0_.refs_2_ = bf16[96,512]{1,0:T(8,128)(2,1)S(1)} collective-permute-done((bf16[96,512]{1,0:T(8,128)(2,1)S(1)}, bf16[96,512]{1,0:T(8,128)(2,1)S(1)}, u32[]{:S(2)}, u32[]{:S(2)}) %collective-permute-start.13) | collective-permute-done | bytes 98336 | tf_op jit(solution)/shard_map/ppermute | solution.py:48
  52.6 1.6 %collective-permute-start.25 = (bf16[512,512]{1,0:T(8,128)(2,1)S(1)}, bf16[512,512]{1,0:T(8,128)(2,1)S(1)}, u32[]{:S(2)}, u32[]{:S(2)}) collective-permute-start(bf16[512,512]{1,0:T(8,128)(2,1)S(1)} %shard_map.57.one_ref), channel_id=1, source_target_pairs={{0,16},{4,20},{8,24},{12,28},{16,0},{20,4},{24,8},{28,12},{1,17},{... | collective-permute-start | bytes 1572872 | tf_op jit(solution)/shard_map/ppermute | solution.py:516
  55.3 1.9 %collective-permute-start.19 = (bf16[96,512]{1,0:T(8,128)(2,1)S(1)}, bf16[96,512]{1,0:T(8,128)(2,1)S(1)}, u32[]{:S(2)}, u32[]{:S(2)}) collective-permute-start(bf16[96,512]{1,0:T(8,128)(2,1)S(1)} %get-tuple-element.41), channel_id=1, source_target_pairs={{0,8},{4,12},{8,16},{12,20},{16,24},{20,28},{24,0},{28,4},{1,9},{5... | collective-permute-start | bytes 294920 | tf_op jit(solution)/shard_map/ppermute | solution.py:48
  59.3 13.3 %collective-permute-done.17.refs_3_ = bf16[96,512]{1,0:T(8,128)(2,1)S(1)} collective-permute-done((bf16[96,512]{1,0:T(8,128)(2,1)S(1)}, bf16[96,512]{1,0:T(8,128)(2,1)S(1)}, u32[]{:S(2)}, u32[]{:S(2)}) %collective-permute-start.17) | collective-permute-done | bytes 98336 | tf_op jit(solution)/shard_map/ppermute | solution.py:48
  77.6 3.4 %collective-permute-start.20 = (bf16[256,256]{1,0:T(8,128)(2,1)S(1)}, bf16[256,256]{1,0:T(8,128)(2,1)S(1)}, u32[]{:S(2)}, u32[]{:S(2)}) collective-permute-start(bf16[256,256]{1,0:T(8,128)(2,1)S(1)} %shard_map.55.refs_0_), channel_id=1, source_target_pairs={{0,1},{1,3},{3,2},{2,0},{4,5},{5,7},{7,6},{6,4},{8,9},{9,11},{11,1... | collective-permute-start | bytes 393224 | tf_op jit(solution)/shard_map/ppermute | solution.py:42
  81.5 3.0 %collective-permute-done.20.refs_1_ = bf16[256,256]{1,0:T(8,128)(2,1)S(1)} collective-permute-done((bf16[256,256]{1,0:T(8,128)(2,1)S(1)}, bf16[256,256]{1,0:T(8,128)(2,1)S(1)}, u32[]{:S(2)}, u32[]{:S(2)}) %collective-permute-start.20) | collective-permute-done | bytes 131104 | tf_op jit(solution)/shard_map/ppermute | solution.py:42
  84.6 2.5 %collective-permute-start.21 = (bf16[256,256]{1,0:T(8,128)(2,1)S(1)}, bf16[256,256]{1,0:T(8,128)(2,1)S(1)}, u32[]{:S(2)}, u32[]{:S(2)}) collective-permute-start(bf16[256,256]{1,0:T(8,128)(2,1)S(1)} %collective-permute-done.20.refs_1_), channel_id=1, source_target_pairs={{0,1},{1,3},{3,2},{2,0},{4,5},{5,7},{7,6},{6,4},{8,9},{9,11},{11,1... | collective-permute-start | bytes 393224 | tf_op jit(solution)/shard_map/ppermute | solution.py:42
  87.8 2.0 %collective-permute-start.28 = (bf16[256,256]{1,0:T(8,128)(2,1)S(1)}, bf16[256,256]{1,0:T(8,128)(2,1)S(1)}, u32[]{:S(2)}, u32[]{:S(2)}) collective-permute-start(bf16[256,256]{1,0:T(8,128)(2,1)S(1)} %collective-permute-done.27.refs_2_), channel_id=1, source_target_pairs={{0,1},{1,3},{3,2},{2,0},{4,5},{5,7},{7,6},{6,4},{8,9},{9,11},{11,1... | collective-permute-start | bytes 393224 | tf_op jit(solution)/shard_map/ppermute | solution.py:42
  91.0 1.8 %collective-permute-start.22 = (bf16[256,256]{1,0:T(8,128)(2,1)S(1)}, bf16[256,256]{1,0:T(8,128)(2,1)S(1)}, u32[]{:S(2)}, u32[]{:S(2)}) collective-permute-start(bf16[256,256]{1,0:T(8,128)(2,1)S(1)} %collective-permute-done.21.refs_2_), channel_id=1, source_target_pairs={{0,1},{1,3},{3,2},{2,0},{4,5},{5,7},{7,6},{6,4},{8,9},{9,11},{11,1... | collective-permute-start | bytes 393224 | tf_op jit(solution)/shard_map/ppermute | solution.py:42
  95.0 1.9 %collective-permute-done.22.ctx_ref = bf16[256,256]{1,0:T(8,128)(2,1)S(1)} collective-permute-done((bf16[256,256]{1,0:T(8,128)(2,1)S(1)}, bf16[256,256]{1,0:T(8,128)(2,1)S(1)}, u32[]{:S(2)}, u32[]{:S(2)}) %collective-permute-start.22) | collective-permute-done | bytes 131104 | tf_op jit(solution)/shard_map/ppermute | solution.py:42
  (58 shorter events, 31.5 us)
Async XLA Ops:
  1.0 8.5 %collective-permute-start.6 = (bf16[128,512]{1,0:T(8,128)(2,1)S(1)}, bf16[128,512]{1,0:T(8,128)(2,1)S(1)}, u32[]{:S(2)}, u32[]{:S(2)}) collective-permute-start(bf16[128,512]{1,0:T(8,128)(2,1)S(1)} %get-tuple-element.31.refs_0_), channel_id=1, source_target_pairs={{0,1},{1,3},{3,2},{2,0},{4,5},{5,7},{7,6},{6,4},{8,9},{9,11},{11,1... | collective-permute-start | bytes 393224 | tf_op jit(solution)/shard_map/ppermute | solution.py:42
  4.1 8.2 %collective-permute-start.9 = (bf16[128,512]{1,0:T(8,128)(2,1)S(1)}, bf16[128,512]{1,0:T(8,128)(2,1)S(1)}, u32[]{:S(2)}, u32[]{:S(2)}) collective-permute-start(bf16[128,512]{1,0:T(8,128)(2,1)S(1)} %get-tuple-element.32.refs_4_), channel_id=1, source_target_pairs={{0,1},{1,3},{3,2},{2,0},{4,5},{5,7},{7,6},{6,4},{8,9},{9,11},{11,1... | collective-permute-start | bytes 393224 | tf_op jit(solution)/shard_map/ppermute | solution.py:42
  7.7 7.4 %collective-permute-start = (bf16[128,512]{1,0:T(8,128)(2,1)S(1)}, bf16[128,512]{1,0:T(8,128)(2,1)S(1)}, u32[]{:S(2)}, u32[]{:S(2)}) collective-permute-start(bf16[128,512]{1,0:T(8,128)(2,1)S(1)} %get-tuple-element.25.refs_0_), channel_id=1, source_target_pairs={{0,1},{1,3},{3,2},{2,0},{4,5},{5,7},{7,6},{6,4},{8,9},{9,11},{11,1... | collective-permute-start | bytes 393224 | tf_op jit(solution)/shard_map/ppermute | solution.py:42
  8.2 9.7 %collective-permute-start.3 = (bf16[128,512]{1,0:T(8,128)(2,1)S(1)}, bf16[128,512]{1,0:T(8,128)(2,1)S(1)}, u32[]{:S(2)}, u32[]{:S(2)}) collective-permute-start(bf16[128,512]{1,0:T(8,128)(2,1)S(1)} %get-tuple-element.26.refs_3_), channel_id=1, source_target_pairs={{0,1},{1,3},{3,2},{2,0},{4,5},{5,7},{7,6},{6,4},{8,9},{9,11},{11,1... | collective-permute-start | bytes 393224 | tf_op jit(solution)/shard_map/ppermute | solution.py:42
  9.5 11.2 %collective-permute-start.7 = (bf16[128,512]{1,0:T(8,128)(2,1)S(1)}, bf16[128,512]{1,0:T(8,128)(2,1)S(1)}, u32[]{:S(2)}, u32[]{:S(2)}) collective-permute-start(bf16[128,512]{1,0:T(8,128)(2,1)S(1)} %collective-permute-done.6.refs_1_), channel_id=1, source_target_pairs={{0,1},{1,3},{3,2},{2,0},{4,5},{5,7},{7,6},{6,4},{8,9},{9,11},{11,1... | collective-permute-start | bytes 393224 | tf_op jit(solution)/shard_map/ppermute | solution.py:42
  12.3 11.2 %collective-permute-start.10 = (bf16[128,512]{1,0:T(8,128)(2,1)S(1)}, bf16[128,512]{1,0:T(8,128)(2,1)S(1)}, u32[]{:S(2)}, u32[]{:S(2)}) collective-permute-start(bf16[128,512]{1,0:T(8,128)(2,1)S(1)} %collective-permute-done.9.refs_5_), channel_id=1, source_target_pairs={{0,1},{1,3},{3,2},{2,0},{4,5},{5,7},{7,6},{6,4},{8,9},{9,11},{11,1... | collective-permute-start | bytes 393224 | tf_op jit(solution)/shard_map/ppermute | solution.py:42
  14.0 11.2 %collective-permute-start.23 = (bf16[128,512]{1,0:T(8,128)(2,1)}, bf16[128,512]{1,0:T(8,128)(2,1)S(1)}, u32[]{:S(2)}, u32[]{:S(2)}) collective-permute-start(bf16[128,512]{1,0:T(8,128)(2,1)} %one_ref.1), channel_id=1, source_target_pairs={{0,4},{4,0},{8,12},{12,8},{16,20},{20,16},{24,28},{28,24},{1,5},{5... | collective-permute-start | bytes 393224 | tf_op jit(solution)/shard_map/ppermute | solution.py:516
  15.1 12.6 %collective-permute-start.1 = (bf16[128,512]{1,0:T(8,128)(2,1)S(1)}, bf16[128,512]{1,0:T(8,128)(2,1)S(1)}, u32[]{:S(2)}, u32[]{:S(2)}) collective-permute-start(bf16[128,512]{1,0:T(8,128)(2,1)S(1)} %collective-permute-done.refs_1_), channel_id=1, source_target_pairs={{0,1},{1,3},{3,2},{2,0},{4,5},{5,7},{7,6},{6,4},{8,9},{9,11},{11,1... | collective-permute-start | bytes 393224 | tf_op jit(solution)/shard_map/ppermute | solution.py:42
  17.9 12.6 %collective-permute-start.4 = (bf16[128,512]{1,0:T(8,128)(2,1)S(1)}, bf16[128,512]{1,0:T(8,128)(2,1)S(1)}, u32[]{:S(2)}, u32[]{:S(2)}) collective-permute-start(bf16[128,512]{1,0:T(8,128)(2,1)S(1)} %collective-permute-done.3.refs_4_), channel_id=1, source_target_pairs={{0,1},{1,3},{3,2},{2,0},{4,5},{5,7},{7,6},{6,4},{8,9},{9,11},{11,1... | collective-permute-start | bytes 393224 | tf_op jit(solution)/shard_map/ppermute | solution.py:42
  20.7 12.4 %collective-permute-start.8 = (bf16[128,512]{1,0:T(8,128)(2,1)S(1)}, bf16[128,512]{1,0:T(8,128)(2,1)S(1)}, u32[]{:S(2)}, u32[]{:S(2)}) collective-permute-start(bf16[128,512]{1,0:T(8,128)(2,1)S(1)} %collective-permute-done.7.refs_2_), channel_id=1, source_target_pairs={{0,1},{1,3},{3,2},{2,0},{4,5},{5,7},{7,6},{6,4},{8,9},{9,11},{11,1... | collective-permute-start | bytes 393224 | tf_op jit(solution)/shard_map/ppermute | solution.py:42
  23.5 11.2 %collective-permute-start.11 = (bf16[128,512]{1,0:T(8,128)(2,1)S(1)}, bf16[128,512]{1,0:T(8,128)(2,1)S(1)}, u32[]{:S(2)}, u32[]{:S(2)}) collective-permute-start(bf16[128,512]{1,0:T(8,128)(2,1)S(1)} %collective-permute-done.10.refs_6_), channel_id=1, source_target_pairs={{0,1},{1,3},{3,2},{2,0},{4,5},{5,7},{7,6},{6,4},{8,9},{9,11},{11,1... | collective-permute-start | bytes 393224 | tf_op jit(solution)/shard_map/ppermute | solution.py:42
  26.1 17.9 %collective-permute-start.24 = (bf16[256,512]{1,0:T(8,128)(2,1)S(1)}, bf16[256,512]{1,0:T(8,128)(2,1)S(1)}, u32[]{:S(2)}, u32[]{:S(2)}) collective-permute-start(bf16[256,512]{1,0:T(8,128)(2,1)S(1)} %shard_map.56.one_ref), channel_id=1, source_target_pairs={{0,8},{4,12},{8,0},{12,4},{16,24},{20,28},{24,16},{28,20},{1,9},{5... | collective-permute-start | bytes 786440 | tf_op jit(solution)/shard_map/ppermute | solution.py:516
  27.7 9.9 %collective-permute-start.2 = (bf16[128,512]{1,0:T(8,128)(2,1)S(1)}, bf16[128,512]{1,0:T(8,128)(2,1)S(1)}, u32[]{:S(2)}, u32[]{:S(2)}) collective-permute-start(bf16[128,512]{1,0:T(8,128)(2,1)S(1)} %collective-permute-done.1.refs_2_), channel_id=1, source_target_pairs={{0,1},{1,3},{3,2},{2,0},{4,5},{5,7},{7,6},{6,4},{8,9},{9,11},{11,1... | collective-permute-start | bytes 393224 | tf_op jit(solution)/shard_map/ppermute | solution.py:42
  30.5 9.0 %collective-permute-start.5 = (bf16[128,512]{1,0:T(8,128)(2,1)S(1)}, bf16[128,512]{1,0:T(8,128)(2,1)S(1)}, u32[]{:S(2)}, u32[]{:S(2)}) collective-permute-start(bf16[128,512]{1,0:T(8,128)(2,1)S(1)} %collective-permute-done.4.refs_5_), channel_id=1, source_target_pairs={{0,1},{1,3},{3,2},{2,0},{4,5},{5,7},{7,6},{6,4},{8,9},{9,11},{11,1... | collective-permute-start | bytes 393224 | tf_op jit(solution)/shard_map/ppermute | solution.py:42
  36.0 19.3 %collective-permute-start.12 = (bf16[256,512]{1,0:T(8,128)(2,1)S(1)}, bf16[256,512]{1,0:T(8,128)(2,1)S(1)}, u32[]{:S(2)}, u32[]{:S(2)}) collective-permute-start(bf16[256,512]{1,0:T(8,128)(2,1)S(1)} %get-tuple-element.33.refs_0_), channel_id=1, source_target_pairs={{0,4},{4,8},{8,12},{12,16},{16,20},{20,24},{24,28},{28,0},{1,5},{5... | collective-permute-start | bytes 786440 | tf_op jit(solution)/shard_map/ppermute | solution.py:48
  40.6 32.2 %collective-permute-start.16 = (bf16[256,512]{1,0:T(8,128)(2,1)S(1)}, bf16[256,512]{1,0:T(8,128)(2,1)S(1)}, u32[]{:S(2)}, u32[]{:S(2)}) collective-permute-start(bf16[256,512]{1,0:T(8,128)(2,1)S(1)} %shard_map.51.refs_1_), channel_id=1, source_target_pairs={{0,4},{4,8},{8,12},{12,16},{16,20},{20,24},{24,28},{28,0},{1,5},{5... | collective-permute-start | bytes 786440 | tf_op jit(solution)/shard_map/ppermute | solution.py:48
  41.0 11.6 %collective-permute-start.13 = (bf16[96,512]{1,0:T(8,128)(2,1)S(1)}, bf16[96,512]{1,0:T(8,128)(2,1)S(1)}, u32[]{:S(2)}, u32[]{:S(2)}) collective-permute-start(bf16[96,512]{1,0:T(8,128)(2,1)S(1)} %get-tuple-element.34), channel_id=1, source_target_pairs={{0,16},{4,20},{8,24},{12,28},{16,0},{20,4},{24,8},{28,12},{1,17},{... | collective-permute-start | bytes 294920 | tf_op jit(solution)/shard_map/ppermute | solution.py:48
  42.7 11.8 %collective-permute-start.14 = (bf16[96,512]{1,0:T(8,128)(2,1)S(1)}, bf16[96,512]{1,0:T(8,128)(2,1)S(1)}, u32[]{:S(2)}, u32[]{:S(2)}) collective-permute-start(bf16[96,512]{1,0:T(8,128)(2,1)S(1)} %get-tuple-element.35), channel_id=1, source_target_pairs={{0,12},{4,16},{8,20},{12,24},{16,28},{20,0},{24,4},{28,8},{1,13},{... | collective-permute-start | bytes 294920 | tf_op jit(solution)/shard_map/ppermute | solution.py:48
  44.0 11.3 %collective-permute-start.15 = (bf16[96,512]{1,0:T(8,128)(2,1)S(1)}, bf16[96,512]{1,0:T(8,128)(2,1)S(1)}, u32[]{:S(2)}, u32[]{:S(2)}) collective-permute-start(bf16[96,512]{1,0:T(8,128)(2,1)S(1)} %get-tuple-element.36), channel_id=1, source_target_pairs={{0,8},{4,12},{8,16},{12,20},{16,24},{20,28},{24,0},{28,4},{1,9},{5... | collective-permute-start | bytes 294920 | tf_op jit(solution)/shard_map/ppermute | solution.py:48
  52.6 40.2 %collective-permute-start.25 = (bf16[512,512]{1,0:T(8,128)(2,1)S(1)}, bf16[512,512]{1,0:T(8,128)(2,1)S(1)}, u32[]{:S(2)}, u32[]{:S(2)}) collective-permute-start(bf16[512,512]{1,0:T(8,128)(2,1)S(1)} %shard_map.57.one_ref), channel_id=1, source_target_pairs={{0,16},{4,20},{8,24},{12,28},{16,0},{20,4},{24,8},{28,12},{1,17},{... | collective-permute-start | bytes 1572872 | tf_op jit(solution)/shard_map/ppermute | solution.py:516
  54.5 18.2 %collective-permute-start.17 = (bf16[96,512]{1,0:T(8,128)(2,1)S(1)}, bf16[96,512]{1,0:T(8,128)(2,1)S(1)}, u32[]{:S(2)}, u32[]{:S(2)}) collective-permute-start(bf16[96,512]{1,0:T(8,128)(2,1)S(1)} %get-tuple-element.39), channel_id=1, source_target_pairs={{0,16},{4,20},{8,24},{12,28},{16,0},{20,4},{24,8},{28,12},{1,17},{... | collective-permute-start | bytes 294920 | tf_op jit(solution)/shard_map/ppermute | solution.py:48
  55.3 17.6 %collective-permute-start.18 = (bf16[96,512]{1,0:T(8,128)(2,1)S(1)}, bf16[96,512]{1,0:T(8,128)(2,1)S(1)}, u32[]{:S(2)}, u32[]{:S(2)}) collective-permute-start(bf16[96,512]{1,0:T(8,128)(2,1)S(1)} %get-tuple-element.40), channel_id=1, source_target_pairs={{0,12},{4,16},{8,20},{12,24},{16,28},{20,0},{24,4},{28,8},{1,13},{... | collective-permute-start | bytes 294920 | tf_op jit(solution)/shard_map/ppermute | solution.py:48
  55.3 17.6 %collective-permute-start.19 = (bf16[96,512]{1,0:T(8,128)(2,1)S(1)}, bf16[96,512]{1,0:T(8,128)(2,1)S(1)}, u32[]{:S(2)}, u32[]{:S(2)}) collective-permute-start(bf16[96,512]{1,0:T(8,128)(2,1)S(1)} %get-tuple-element.41), channel_id=1, source_target_pairs={{0,8},{4,12},{8,16},{12,20},{16,24},{20,28},{24,0},{28,4},{1,9},{5... | collective-permute-start | bytes 294920 | tf_op jit(solution)/shard_map/ppermute | solution.py:48
  77.6 7.0 %collective-permute-start.20 = (bf16[256,256]{1,0:T(8,128)(2,1)S(1)}, bf16[256,256]{1,0:T(8,128)(2,1)S(1)}, u32[]{:S(2)}, u32[]{:S(2)}) collective-permute-start(bf16[256,256]{1,0:T(8,128)(2,1)S(1)} %shard_map.55.refs_0_), channel_id=1, source_target_pairs={{0,1},{1,3},{3,2},{2,0},{4,5},{5,7},{7,6},{6,4},{8,9},{9,11},{11,1... | collective-permute-start | bytes 393224 | tf_op jit(solution)/shard_map/ppermute | solution.py:42
  (7 other events, 36.8 us)

commit v3 on v2

--- a/solution.py
+++ b/solution.py
@@ -25,21 +25,28 @@
     return pl.BlockSpec(memory_space=pltpu.VMEM)
 
 
-def folded_ring(size):
+def ring_of(size):
     ups = [i for i in range(size) if i % 2 == 1]
     downs = [i for i in range(size) if i % 2 == 0 and i > 0]
     return [0] + ups + downs[::-1]
 
 
-IN_RING = folded_ring
-OUT_RING = folded_ring
+def offset_of(step):
+    return -((step + 1) // 2) if step % 2 else step // 2
+
+
 EARLY = 8
+FINAL = 2
 EARLY_PARTS, LATE_PARTS = 2, 2
 
 
-def around(block, order):
-    route = [(a, b) for a, b in zip(order, order[1:] + order[:1])]
-    return lax.ppermute(block, "head", route)
+def spread(held, step):
+    order = ring_of(lax.axis_size("head"))
+    towards = order[1:] + order[:1]
+    if step % 2 == 0:
+        order, towards = towards, order
+    block = held[0] if step <= 2 else held[step - 2]
+    return lax.ppermute(block, "head", list(zip(order, towards)))
 
 
 def passed_along(block, distance):
@@ -48,12 +55,13 @@
     return lax.ppermute(block, "seg", route)
 
 
-def source_of(step, order):
-    size = len(order)
+def source_of(step, size):
+    order = ring_of(size)
     z = lax.axis_index("head")
     found = jnp.int32(0)
     for here in range(size):
-        found = jnp.where(z == here, order[(order.index(here) - step) % size], found)
+        at = (order.index(here) + offset_of(step)) % size
+        found = jnp.where(z == here, order[at], found)
     return found
 
 
@@ -124,7 +132,7 @@
     acc = None
     for t, block in zip(steps, blocks):
         part = jnp.dot(
-            block[...], weight_rows(w_ref, i, source_of(t, IN_RING(size)), feats), preferred_element_type=F32
+            block[...], weight_rows(w_ref, i, source_of(t, size), feats), preferred_element_type=F32
         )
         acc = part if acc is None else acc + part
     return acc
@@ -184,7 +192,7 @@
     return call(body, outs, [*flat, w3, col_sums])
 
 
-def project_begin(chunks, w3):
+def project_begin(chunks, steps, w3):
     n_here, n_chunk = len(chunks[0]), len(chunks)
     piece, _ = chunks[0][0].shape
     width = w3.shape[2]
@@ -197,7 +205,7 @@
             at = pl.ds(c * piece, piece)
             for i in range(3):
                 acc_ref[at, i * width : (i + 1) * width] = project_sum(
-                    blocks, range(n_here), w_ref, i
+                    blocks, steps, w_ref, i
                 )
             held = jnp.zeros((piece, 128), F32)
             for t, block in enumerate(blocks):
@@ -210,19 +218,19 @@
     return call(body, outs, [*flat, w3])
 
 
-def project_end(lasts, begun, w3, col_sums, kinds):
+def project_end(lasts, last, begun, w3, col_sums, kinds):
     n_chunk = len(lasts)
     piece, feats = lasts[0].shape
     width = w3.shape[2]
     rows = piece * n_chunk
-    last = w3.shape[1] // feats - 1
+    n_begun = w3.shape[1] // feats - 1
 
     def body(*refs):
         w_ref, acc_ref, mom_ref, sum_ref, out_ref = refs[n_chunk:]
         for c in range(n_chunk):
             at = pl.ds(c * piece, piece)
             held = mom_ref[at, :]
-            parts = [(held[:, 2 * t : 2 * t + 1], held[:, 2 * t + 1 : 2 * t + 2]) for t in range(last)]
+            parts = [(held[:, 2 * t : 2 * t + 1], held[:, 2 * t + 1 : 2 * t + 2]) for t in range(n_begun)]
             parts.append(moments(refs[c][...]))
             mean, inv = joined_moments(parts, feats)
             for k, i in enumerate(kinds):
@@ -247,7 +255,8 @@
             max(e + o for e, o in zip(self.early, self.offset)),
             max(l + t for l, t in zip(self.late, self.tail)),
         )
-        self.rows = -(-most // 16) * 16
+        self.rows = -(-most // 8) * 8
+        self.pitch = -(-most // 16) * 16
         self.joints = [b for b in range(RATE - 1) if self.tail[b] > 0]
 
 
@@ -271,9 +280,9 @@
     def hits(first, rows, at):
         row = lax.broadcasted_iota(jnp.int32, (n, rows), 0)
         col = lax.broadcasted_iota(jnp.int32, (n, rows), 1) + at
-        return jnp.where(col == first + RATE * row, 1.0, 0.0).astype(BF16)
-
-    chosen = jnp.concatenate([hits(f, main.shape[0], base) for f in wanted], axis=0)
+        return jnp.where(col == first + RATE * row, 1.0, 0.0)
+
+    chosen = jnp.concatenate([hits(f, main.shape[0], base) for f in wanted], axis=0).astype(BF16)
     picks = jnp.dot(chosen, main[...], preferred_element_type=F32)
     row = lax.broadcasted_iota(jnp.int32, (n, 1), 0)
     picked = {}
@@ -323,8 +332,8 @@
 
 def attend_begin(slots, q, own, memory, early):
     rows, width = q.shape
-    n = slots.rows
-    n_comp = -(-RATE * n // 128) * 128
+    n, pitch = slots.rows, slots.pitch
+    n_comp = -(-RATE * pitch // 128) * 128
     heads = width // DH
 
     def body(q_ref, *refs):
@@ -333,11 +342,10 @@
         early_refs = refs[len(own) + 1 : len(own) + 1 + RATE]
         mix_ref, stat_ref, comp_ref = refs[len(own) + 1 + RATE :]
         seg = lax.axis_index("seg")
+        comp_ref[...] = jnp.zeros((n_comp, 2 * width), BF16)
         for a in range(RATE):
-            comp_ref[a * n : (a + 1) * n, :] = early_refs[a][...]
-        if n_comp > RATE * n:
-            comp_ref[RATE * n :, :] = jnp.zeros((n_comp - RATE * n, 2 * width), BF16)
-        comp_bias = slot_bias(seg, n_comp, [(a * n, slots.early[a]) for a in range(RATE)])
+            comp_ref[a * pitch : a * pitch + n, :] = early_refs[a][...]
+        comp_bias = slot_bias(seg, n_comp, [(a * pitch, slots.early[a]) for a in range(RATE)])
         mem_bias = jnp.where(seg >= 1, 0.0, NEG).astype(F32)
         q_row = lax.broadcasted_iota(jnp.int32, (rows, rows), 0)
         k_row = lax.broadcasted_iota(jnp.int32, (rows, rows), 1)
@@ -385,21 +393,50 @@
     return top, norm, mixed
 
 
-def attend_end(slots, q, begun, memory, heads_of, late, weight):
+def state_of(mix_ref, stat_ref, h):
+    top, norm = (stat_ref[:, 2 * h + k : 2 * h + k + 1] for k in range(2))
+    return top, norm, mix_ref[:, h * DH : (h + 1) * DH]
+
+
+def attend_more(q, begun, memory):
     rows, width = q.shape
-    n = slots.rows
-    n_comp = -(-(RATE * n + 16) // 128) * 128
+
+    def body(q_ref, mix_ref, stat_ref, mem_ref, mix_out, stat_out):
+        seg = lax.axis_index("seg")
+        mem_bias = jnp.where(seg >= 1, 0.0, NEG).astype(F32)
+        lane = lax.broadcasted_iota(jnp.int32, (rows, 128), 1)
+        stats = jnp.zeros((rows, 128), F32)
+        for h in range(width // DH):
+            kc = slice(h * DH, (h + 1) * DH)
+            vc = slice(width + h * DH, width + (h + 1) * DH)
+            pieces = [(score(q_ref[:, kc], mem_ref[:, kc]) + mem_bias, mem_ref, vc)]
+            top, norm, mixed = gathered(pieces, state_of(mix_ref, stat_ref, h))
+            mix_out[:, kc] = mixed
+            stats = jnp.where(lane == 2 * h, top, stats)
+            stats = jnp.where(lane == 2 * h + 1, norm, stats)
+        stat_out[...] = stats
+
+    outs = [((rows, width), F32), ((rows, 128), F32)]
+    return call(body, outs, [q, *begun, memory])
+
+
+def attend_end(slots, q, begun, heads_of, late, weight):
+    rows, width = q.shape
+    n, pitch = slots.rows, slots.pitch
+    n_comp = -(-(RATE * pitch + 16) // 128) * 128
     heads = width // DH
 
-    def body(q_ref, mix_ref, stat_ref, mem_ref, *refs):
+    def body(q_ref, mix_ref, stat_ref, *refs):
         early_refs = refs[:RATE]
         late_refs = refs[RATE : 2 * RATE]
         w_ref, out_ref, comp_ref = refs[2 * RATE :]
         seg = lax.axis_index("seg")
         weight = filter_rows(w_ref)
+        if n < pitch:
+            comp_ref[: RATE * pitch, :] = jnp.zeros((RATE * pitch, 2 * width), BF16)
         for a in range(RATE):
-            comp_ref[a * n : (a + 1) * n, :] = late_refs[a][...]
-        pad = n_comp - RATE * n
+            comp_ref[a * pitch : a * pitch + n, :] = late_refs[a][...]
+        pad = n_comp - RATE * pitch
         row = lax.broadcasted_iota(jnp.int32, (pad, 1), 0)
         extra = jnp.zeros((pad, 2 * width), F32)
         for k, b in enumerate(slots.joints):
@@ -411,38 +448,29 @@
             parts += [head[at + i : at + i + 1] for i in range(slots.offset[b + 1])]
             slot = sum(p * weight[r] for r, p in enumerate(parts))
             extra = jnp.where(row == k, slot, extra)
-        comp_ref[RATE * n :, :] = extra.astype(BF16)
-        spans = [(a * n, slots.late[a]) for a in range(RATE)] + [(RATE * n, len(slots.joints))]
+        comp_ref[RATE * pitch :, :] = extra.astype(BF16)
+        spans = [(a * pitch, slots.late[a]) for a in range(RATE)]
+        spans.append((RATE * pitch, len(slots.joints)))
         comp_bias = slot_bias(seg, n_comp, spans)
-        mem_bias = jnp.where(seg >= 1, 0.0, NEG).astype(F32)
         for h in range(heads):
             kc = slice(h * DH, (h + 1) * DH)
             vc = slice(width + h * DH, width + (h + 1) * DH)
-            q = q_ref[:, kc]
-            pieces = [
-                (score(q, comp_ref[:, kc]) + comp_bias, comp_ref, vc),
-                (score(q, mem_ref[:, kc]) + mem_bias, mem_ref, vc),
-            ]
-            so_far = (
-                stat_ref[:, 2 * h : 2 * h + 1],
-                stat_ref[:, 2 * h + 1 : 2 * h + 2],
-                mix_ref[:, kc],
-            )
-            _, norm, mixed = gathered(pieces, so_far)
+            pieces = [(score(q_ref[:, kc], comp_ref[:, kc]) + comp_bias, comp_ref, vc)]
+            _, norm, mixed = gathered(pieces, state_of(mix_ref, stat_ref, h))
             out_ref[:, kc] = (mixed / norm).astype(BF16)
 
     outs = [((rows, width), BF16)]
     scratch = [pltpu.VMEM((n_comp, 2 * width), BF16)]
-    args = [q, *begun, memory, *heads_of, *late, weight]
+    args = [q, *begun, *heads_of, *late, weight]
     return call(body, outs, args, scratch)[0]
 
 
-def output_begin(ctx, w_full, xored):
+def output_begin(ctx, steps, w_full, xored):
     rows = ctx[0].shape[0]
 
     def body(*refs):
         w_ref, acc_ref = refs[len(ctx) :]
-        acc_ref[...] = output_sum(refs[: len(ctx)], range(len(ctx)), w_ref, xored)
+        acc_ref[...] = output_sum(refs[: len(ctx)], steps, w_ref, xored)
 
     outs = [((rows, w_full.shape[1]), F32)]
     return call(body, outs, [*ctx, w_full])[0]
@@ -455,7 +483,7 @@
     acc = None
     for t, c in zip(steps, ctx):
         for k in range(width // unit):
-            block = source_of(t, OUT_RING(size)) * (width // unit) + k
+            block = source_of(t, size) * (width // unit) + k
             if xored:
                 block = lax.bitwise_xor(block, lax.axis_index("seg"))
             start = pl.multiple_of(block * unit, unit)
@@ -541,45 +569,47 @@
     starts = [early_rows + c * late_piece for c in range(LATE_PARTS)]
     second = [[chunk] for chunk in split(rows, starts, late_piece)]
     n_seg = lax.axis_size("seg")
-    in_ring, out_ring = IN_RING(n_head), OUT_RING(n_head)
     own_rows = w_out.shape[0]
     power = n_seg & (n_seg - 1) == 0
     xored = own_rows if power and own_rows % DH == 0 and width % own_rows == 0 else 0
 
     w_vmem, col_sums = fetch_weights(w3)
-    for _ in range(1, n_head):
+    for t in range(1, n_head):
         for chunk in first:
-            chunk.append(around(chunk[-1], in_ring))
+            chunk.append(spread(chunk, t))
     w_full = gather_rows(w_out, xored)
     q0, kv0 = project(first, w_vmem, col_sums)
     early_parts = compress(slots, [kv0], weight)
     mem0 = passed_along(kv0, 1)
     early = [passed_along(p, BACK - a) for a, p in enumerate(early_parts)]
 
-    for _ in range(1, n_head):
+    for t in range(1, n_head):
         for chunk in second:
-            chunk.append(around(chunk[-1], in_ring))
-    begun = project_begin([chunk[:-1] for chunk in second], w_vmem)
-    lasts = [chunk[-1] for chunk in second]
-    kv1 = project_end(lasts, begun, w_vmem, col_sums, (1, 2))
+            chunk.append(spread(chunk, t))
+    final = min(FINAL, n_head - 1)
+    steps = [t for t in range(n_head) if t != final]
+    begun = project_begin([[chunk[t] for t in steps] for chunk in second], steps, w_vmem)
+    lasts = [chunk[final] for chunk in second]
+    kv1 = project_end(lasts, final, begun, w_vmem, col_sums, (1, 2))
     mem1 = passed_along(kv1, 1)
     late_parts = compress(slots, [kv0, kv1], weight)
     late = [passed_along(p, BACK - a) for a, p in enumerate(late_parts)]
-    q1 = project_end(lasts, begun, w_vmem, col_sums, (0,))
+    q1 = project_end(lasts, final, begun, w_vmem, col_sums, (0,))
 
     rings = []
     for q, own in ((q0, [kv0]), (q1, [kv0, kv1])):
         part = attend_begin(slots, q, own, mem0, early)
-        ctx = attend_end(slots, q, part, mem1, early, late, weight)
+        part = attend_more(q, part, mem1)
+        ctx = attend_end(slots, q, part, early, late, weight)
         rings.append([ctx])
-    for _ in range(1, n_head):
+    for t in range(1, n_head):
         for ring in rings:
-            ring.append(around(ring[-1], out_ring))
+            ring.append(spread(ring, t))
     result = None
     for h, ring in enumerate(rings):
-        part = output_begin(ring[:-1], w_full, xored)
+        part = output_begin([ring[t] for t in steps], steps, w_full, xored)
         result = output_end(
-            h * early_rows, seg_len, n_head - 1, ring[-1], part, w_full, xored, result,
+            h * early_rows, seg_len, final, ring[final], part, w_full, xored, result,
         )
     return result[None]
 

time: 98 us -> 96.8 us (0.988)
  waiting for transfers between devices: 39 us -> 32.5 us
  starting transfers between devices: 40.6 us -> 44.2 us
  Pallas kernels: 17.1 us -> 18.6 us
    ppermute x18, waiting for transfers between devices: 18.5 us -> 12.8 us  [spread(): return lax.ppermute(block, 'head', list(zip(order, towards)))]
    ppermute x18, starting transfers between devices: 30.1 us -> 34.4 us  [spread(): return lax.ppermute(block, 'head', list(zip(order, towards)))]
    pallas_call x17 -> x19, Pallas kernels: 12.9 us -> 14.4 us  [call(): pl.pallas_call(body, out_shape=tuple((jax.ShapeDtypeStruct(s, d) for s, d...]
  transfers between devices with their start and end apart: 29 -> 29, of which waited for: 16 -> 12; matrix products, arithmetic and copies ran while one was open for 0% -> 0% of each run, Pallas kernels for 16% -> 17%
where the time goes in v3:
time: 96.8 us; the launch traced here: 96.7 us
  starting transfers between devices  44.2 us (46%)
  waiting for transfers between devices  32.5 us (34%)
  Pallas kernels  18.6 us (19%)
    ppermute x18, starting transfers between devices, spread(): return lax.ppermute(block, 'head', list(zip(order, towards)))  34.4 us
    ppermute x8, waiting for transfers between devices, passed_along(): return lax.ppermute(block, 'seg', route)  19.7 us
    pallas_call x19, Pallas kernels, call(): pl.pallas_call(body, out_shape=tuple((jax.ShapeDtypeStruct(s, d) for s, d...  14.4 us
    ppermute x18, waiting for transfers between devices, spread(): return lax.ppermute(block, 'head', list(zip(order, towards)))  12.8 us
    ppermute x8, starting transfers between devices, passed_along(): return lax.ppermute(block, 'seg', route)  6.6 us
    ppermute x3, starting transfers between devices, gather_rows(): other = lax.ppermute(block, 'seg', [(i, i ^ step) for i in range(size)])  3.19 us
    pallas_call x1, Pallas kernels, fetch_weights(): pl.pallas_call(body, out_shape=(jax.ShapeDtypeStruct(w3.shape, w3.dtype),...  2.25 us
  transfers between devices with their start and end apart: 29, of which 12 were waited for; matrix products, arithmetic and copies ran while one was open for 0% of the time, Pallas kernels for 17%

profile of v3, /device:TPU:0, one launch (start us, length us, event | category | flops | bytes accessed | tf_op | source)
XLA Modules:
  0.0 96.7 jit_solution(13586040154745602200)
XLA Ops:
  1.0 3.1 %collective-permute-start.2 = (bf16[128,512]{1,0:T(8,128)(2,1)S(1)}, bf16[128,512]{1,0:T(8,128)(2,1)S(1)}, u32[]{:S(2)}, u32[]{:S(2)}) collective-permute-start(bf16[128,512]{1,0:T(8,128)(2,1)S(1)} %get-tuple-element.29.refs_0_), channel_id=1, source_target_pairs={{0,1},{1,3},{3,2},{2,0},{4,5},{5,7},{7,6},{6,4},{8,9},{9,11},{11,1... | collective-permute-start | bytes 393224 | tf_op jit(solution)/shard_map/ppermute | solution.py:49
  5.1 2.6 %collective-permute-start.6 = (bf16[128,512]{1,0:T(8,128)(2,1)S(1)}, bf16[128,512]{1,0:T(8,128)(2,1)S(1)}, u32[]{:S(2)}, u32[]{:S(2)}) collective-permute-start(bf16[128,512]{1,0:T(8,128)(2,1)S(1)} %get-tuple-element.35.refs_0_), channel_id=1, source_target_pairs={{0,1},{1,3},{3,2},{2,0},{4,5},{5,7},{7,6},{6,4},{8,9},{9,11},{11,1... | collective-permute-start | bytes 393224 | tf_op jit(solution)/shard_map/ppermute | solution.py:49
  9.0 2.5 %collective-permute-start.7 = (bf16[128,512]{1,0:T(8,128)(2,1)S(1)}, bf16[128,512]{1,0:T(8,128)(2,1)S(1)}, u32[]{:S(2)}, u32[]{:S(2)}) collective-permute-start(bf16[128,512]{1,0:T(8,128)(2,1)S(1)} %get-tuple-element.35.refs_0_), channel_id=1, source_target_pairs={{1,0},{3,1},{2,3},{0,2},{5,4},{7,5},{6,7},{4,6},{9,8},{11,9},{10,1... | collective-permute-start | bytes 393224 | tf_op jit(solution)/shard_map/ppermute | solution.py:49
  12.4 1.9 %collective-permute-start.10 = (bf16[128,512]{1,0:T(8,128)(2,1)S(1)}, bf16[128,512]{1,0:T(8,128)(2,1)S(1)}, u32[]{:S(2)}, u32[]{:S(2)}) collective-permute-start(bf16[128,512]{1,0:T(8,128)(2,1)S(1)} %get-tuple-element.36.refs_4_), channel_id=1, source_target_pairs={{1,0},{3,1},{2,3},{0,2},{5,4},{7,5},{6,7},{4,6},{9,8},{11,9},{10,1... | collective-permute-start | bytes 393224 | tf_op jit(solution)/shard_map/ppermute | solution.py:49
  15.2 1.7 %collective-permute-start.8 = (bf16[128,512]{1,0:T(8,128)(2,1)S(1)}, bf16[128,512]{1,0:T(8,128)(2,1)S(1)}, u32[]{:S(2)}, u32[]{:S(2)}) collective-permute-start(bf16[128,512]{1,0:T(8,128)(2,1)S(1)} %collective-permute-done.6.refs_1_), channel_id=1, source_target_pairs={{0,1},{1,3},{3,2},{2,0},{4,5},{5,7},{7,6},{6,4},{8,9},{9,11},{11,1... | collective-permute-start | bytes 393224 | tf_op jit(solution)/shard_map/ppermute | solution.py:49
  16.9 3.1 %collective-permute-start.11 = (bf16[128,512]{1,0:T(8,128)(2,1)S(1)}, bf16[128,512]{1,0:T(8,128)(2,1)S(1)}, u32[]{:S(2)}, u32[]{:S(2)}) collective-permute-start(bf16[128,512]{1,0:T(8,128)(2,1)S(1)} %collective-permute-done.9.refs_5_), channel_id=1, source_target_pairs={{0,1},{1,3},{3,2},{2,0},{4,5},{5,7},{7,6},{6,4},{8,9},{9,11},{11,1... | collective-permute-start | bytes 393224 | tf_op jit(solution)/shard_map/ppermute | solution.py:49
  20.9 1.6 %collective-permute-start.24 = (bf16[256,512]{1,0:T(8,128)(2,1)S(1)}, bf16[256,512]{1,0:T(8,128)(2,1)S(1)}, u32[]{:S(2)}, u32[]{:S(2)}) collective-permute-start(bf16[256,512]{1,0:T(8,128)(2,1)S(1)} %shard_map.57.one_ref), channel_id=1, source_target_pairs={{0,8},{4,12},{8,0},{12,4},{16,24},{20,28},{24,16},{28,20},{1,9},{5... | collective-permute-start | bytes 786440 | tf_op jit(solution)/shard_map/ppermute | solution.py:544
  22.5 3.5 %collective-permute-start.3 = (bf16[128,512]{1,0:T(8,128)(2,1)S(1)}, bf16[128,512]{1,0:T(8,128)(2,1)S(1)}, u32[]{:S(2)}, u32[]{:S(2)}) collective-permute-start(bf16[128,512]{1,0:T(8,128)(2,1)S(1)} %collective-permute-done.2.refs_1_), channel_id=1, source_target_pairs={{0,1},{1,3},{3,2},{2,0},{4,5},{5,7},{7,6},{6,4},{8,9},{9,11},{11,1... | collective-permute-start | bytes 393224 | tf_op jit(solution)/shard_map/ppermute | solution.py:49
  26.0 3.6 %collective-permute-start.5 = (bf16[128,512]{1,0:T(8,128)(2,1)S(1)}, bf16[128,512]{1,0:T(8,128)(2,1)S(1)}, u32[]{:S(2)}, u32[]{:S(2)}) collective-permute-start(bf16[128,512]{1,0:T(8,128)(2,1)S(1)} %collective-permute-done.4.refs_4_), channel_id=1, source_target_pairs={{0,1},{1,3},{3,2},{2,0},{4,5},{5,7},{7,6},{6,4},{8,9},{9,11},{11,1... | collective-permute-start | bytes 393224 | tf_op jit(solution)/shard_map/ppermute | solution.py:49
  29.6 1.5 %collective-permute-start.1 = (bf16[128,512]{1,0:T(8,128)(2,1)S(1)}, bf16[128,512]{1,0:T(8,128)(2,1)S(1)}, u32[]{:S(2)}, u32[]{:S(2)}) collective-permute-start(bf16[128,512]{1,0:T(8,128)(2,1)S(1)} %get-tuple-element.30.refs_3_), channel_id=1, source_target_pairs={{1,0},{3,1},{2,3},{0,2},{5,4},{7,5},{6,7},{4,6},{9,8},{11,9},{10,1... | collective-permute-start | bytes 393224 | tf_op jit(solution)/shard_map/ppermute | solution.py:49
  31.2 2.3 %fetch.1 = (bf16[3,2048,256]{2,1,0:T(8,128)(2,1)S(1)}, f32[8,768]{1,0:T(8,128)S(1)}) custom-call(bf16[3,2048,256]{2,1,0:T(8,128)(2,1)} %bitcast.3), custom_call_target="tpu_custom_call" | custom-call | tf_op jit(solution)/shard_map/fetch/pallas_call | solution.py:155
  35.1 1.6 %collective-permute-start.13 = (bf16[88,512]{1,0:T(8,128)(2,1)S(1)}, bf16[88,512]{1,0:T(8,128)(2,1)S(1)}, u32[]{:S(2)}, u32[]{:S(2)}) collective-permute-start(bf16[88,512]{1,0:T(8,128)(2,1)S(1)} %get-tuple-element.38), channel_id=1, source_target_pairs={{0,16},{4,20},{8,24},{12,28},{16,0},{20,4},{24,8},{28,12},{1,17},{... | collective-permute-start | bytes 270344 | tf_op jit(solution)/shard_map/ppermute | solution.py:55
  37.5 2.0 %collective-permute-done.1.refs_1_ = bf16[128,512]{1,0:T(8,128)(2,1)S(1)} collective-permute-done((bf16[128,512]{1,0:T(8,128)(2,1)S(1)}, bf16[128,512]{1,0:T(8,128)(2,1)S(1)}, u32[]{:S(2)}, u32[]{:S(2)}) %collective-permute-start.1) | collective-permute-done | bytes 131104 | tf_op jit(solution)/shard_map/ppermute | solution.py:49
  40.8 1.6 %collective-permute-start.25 = (bf16[512,512]{1,0:T(8,128)(2,1)S(1)}, bf16[512,512]{1,0:T(8,128)(2,1)S(1)}, u32[]{:S(2)}, u32[]{:S(2)}) collective-permute-start(bf16[512,512]{1,0:T(8,128)(2,1)S(1)} %shard_map.58.one_ref), channel_id=1, source_target_pairs={{0,16},{4,20},{8,24},{12,28},{16,0},{20,4},{24,8},{28,12},{1,17},{... | collective-permute-start | bytes 1572872 | tf_op jit(solution)/shard_map/ppermute | solution.py:544
  42.4 1.3 %collective-permute-start.14 = (bf16[88,512]{1,0:T(8,128)(2,1)S(1)}, bf16[88,512]{1,0:T(8,128)(2,1)S(1)}, u32[]{:S(2)}, u32[]{:S(2)}) collective-permute-start(bf16[88,512]{1,0:T(8,128)(2,1)S(1)} %get-tuple-element.39), channel_id=1, source_target_pairs={{0,12},{4,16},{8,20},{12,24},{16,28},{20,0},{24,4},{28,8},{1,13},{... | collective-permute-start | bytes 270344 | tf_op jit(solution)/shard_map/ppermute | solution.py:55
  43.8 1.5 %collective-permute-start.15 = (bf16[88,512]{1,0:T(8,128)(2,1)S(1)}, bf16[88,512]{1,0:T(8,128)(2,1)S(1)}, u32[]{:S(2)}, u32[]{:S(2)}) collective-permute-start(bf16[88,512]{1,0:T(8,128)(2,1)S(1)} %get-tuple-element.40), channel_id=1, source_target_pairs={{0,8},{4,12},{8,16},{12,20},{16,24},{20,28},{24,0},{28,4},{1,9},{5... | collective-permute-start | bytes 270344 | tf_op jit(solution)/shard_map/ppermute | solution.py:55
  45.6 16.7 %collective-permute-done.14.refs_4_.refs_1_.refs_3_ = bf16[88,512]{1,0:T(8,128)(2,1)S(1)} collective-permute-done((bf16[88,512]{1,0:T(8,128)(2,1)S(1)}, bf16[88,512]{1,0:T(8,128)(2,1)S(1)}, u32[]{:S(2)}, u32[]{:S(2)}) %collective-permute-start.14) | collective-permute-done | bytes 90144 | tf_op jit(solution)/shard_map/ppermute | solution.py:55
  62.3 1.6 %collective-permute-start.17 = (bf16[88,512]{1,0:T(8,128)(2,1)S(1)}, bf16[88,512]{1,0:T(8,128)(2,1)S(1)}, u32[]{:S(2)}, u32[]{:S(2)}) collective-permute-start(bf16[88,512]{1,0:T(8,128)(2,1)S(1)} %get-tuple-element.45), channel_id=1, source_target_pairs={{0,16},{4,20},{8,24},{12,28},{16,0},{20,4},{24,8},{28,12},{1,17},{... | collective-permute-start | bytes 270344 | tf_op jit(solution)/shard_map/ppermute | solution.py:55
  67.7 2.8 %collective-permute-done.17.refs_3_ = bf16[88,512]{1,0:T(8,128)(2,1)S(1)} collective-permute-done((bf16[88,512]{1,0:T(8,128)(2,1)S(1)}, bf16[88,512]{1,0:T(8,128)(2,1)S(1)}, u32[]{:S(2)}, u32[]{:S(2)}) %collective-permute-start.17) | collective-permute-done | bytes 90144 | tf_op jit(solution)/shard_map/ppermute | solution.py:55
  71.7 3.5 %collective-permute-start.21 = (bf16[256,256]{1,0:T(8,128)(2,1)S(1)}, bf16[256,256]{1,0:T(8,128)(2,1)S(1)}, u32[]{:S(2)}, u32[]{:S(2)}) collective-permute-start(bf16[256,256]{1,0:T(8,128)(2,1)S(1)} %shard_map.56.refs_0_), channel_id=1, source_target_pairs={{0,1},{1,3},{3,2},{2,0},{4,5},{5,7},{7,6},{6,4},{8,9},{9,11},{11,1... | collective-permute-start | bytes 393224 | tf_op jit(solution)/shard_map/ppermute | solution.py:49
  78.4 3.4 %collective-permute-start.27 = (bf16[256,256]{1,0:T(8,128)(2,1)S(1)}, bf16[256,256]{1,0:T(8,128)(2,1)S(1)}, u32[]{:S(2)}, u32[]{:S(2)}) collective-permute-start(bf16[256,256]{1,0:T(8,128)(2,1)S(1)} %shard_map.63.refs_0_), channel_id=1, source_target_pairs={{0,1},{1,3},{3,2},{2,0},{4,5},{5,7},{7,6},{6,4},{8,9},{9,11},{11,1... | collective-permute-start | bytes 393224 | tf_op jit(solution)/shard_map/ppermute | solution.py:49
  81.9 3.4 %collective-permute-done.27.refs_1_ = bf16[256,256]{1,0:T(8,128)(2,1)S(1)} collective-permute-done((bf16[256,256]{1,0:T(8,128)(2,1)S(1)}, bf16[256,256]{1,0:T(8,128)(2,1)S(1)}, u32[]{:S(2)}, u32[]{:S(2)}) %collective-permute-start.27) | collective-permute-done | bytes 131104 | tf_op jit(solution)/shard_map/ppermute | solution.py:49
  85.3 2.0 %collective-permute-start.28 = (bf16[256,256]{1,0:T(8,128)(2,1)S(1)}, bf16[256,256]{1,0:T(8,128)(2,1)S(1)}, u32[]{:S(2)}, u32[]{:S(2)}) collective-permute-start(bf16[256,256]{1,0:T(8,128)(2,1)S(1)} %collective-permute-done.27.refs_1_), channel_id=1, source_target_pairs={{0,1},{1,3},{3,2},{2,0},{4,5},{5,7},{7,6},{6,4},{8,9},{9,11},{11,1... | collective-permute-start | bytes 393224 | tf_op jit(solution)/shard_map/ppermute | solution.py:49
  89.4 3.3 %collective-permute-done.28.refs_2_ = bf16[256,256]{1,0:T(8,128)(2,1)S(1)} collective-permute-done((bf16[256,256]{1,0:T(8,128)(2,1)S(1)}, bf16[256,256]{1,0:T(8,128)(2,1)S(1)}, u32[]{:S(2)}, u32[]{:S(2)}) %collective-permute-start.28) | collective-permute-done | bytes 131104 | tf_op jit(solution)/shard_map/ppermute | solution.py:49
  (60 shorter events, 24.2 us)
Async XLA Ops:
  1.0 8.0 %collective-permute-start.2 = (bf16[128,512]{1,0:T(8,128)(2,1)S(1)}, bf16[128,512]{1,0:T(8,128)(2,1)S(1)}, u32[]{:S(2)}, u32[]{:S(2)}) collective-permute-start(bf16[128,512]{1,0:T(8,128)(2,1)S(1)} %get-tuple-element.29.refs_0_), channel_id=1, source_target_pairs={{0,1},{1,3},{3,2},{2,0},{4,5},{5,7},{7,6},{6,4},{8,9},{9,11},{11,1... | collective-permute-start | bytes 393224 | tf_op jit(solution)/shard_map/ppermute | solution.py:49
  5.1 7.3 %collective-permute-start.6 = (bf16[128,512]{1,0:T(8,128)(2,1)S(1)}, bf16[128,512]{1,0:T(8,128)(2,1)S(1)}, u32[]{:S(2)}, u32[]{:S(2)}) collective-permute-start(bf16[128,512]{1,0:T(8,128)(2,1)S(1)} %get-tuple-element.35.refs_0_), channel_id=1, source_target_pairs={{0,1},{1,3},{3,2},{2,0},{4,5},{5,7},{7,6},{6,4},{8,9},{9,11},{11,1... | collective-permute-start | bytes 393224 | tf_op jit(solution)/shard_map/ppermute | solution.py:49
  7.7 7.5 %collective-permute-start.9 = (bf16[128,512]{1,0:T(8,128)(2,1)S(1)}, bf16[128,512]{1,0:T(8,128)(2,1)S(1)}, u32[]{:S(2)}, u32[]{:S(2)}) collective-permute-start(bf16[128,512]{1,0:T(8,128)(2,1)S(1)} %get-tuple-element.36.refs_4_), channel_id=1, source_target_pairs={{0,1},{1,3},{3,2},{2,0},{4,5},{5,7},{7,6},{6,4},{8,9},{9,11},{11,1... | collective-permute-start | bytes 393224 | tf_op jit(solution)/shard_map/ppermute | solution.py:49
  8.2 8.7 %collective-permute-start.23 = (bf16[128,512]{1,0:T(8,128)(2,1)}, bf16[128,512]{1,0:T(8,128)(2,1)S(1)}, u32[]{:S(2)}, u32[]{:S(2)}) collective-permute-start(bf16[128,512]{1,0:T(8,128)(2,1)} %one_ref.1), channel_id=1, source_target_pairs={{0,4},{4,0},{8,12},{12,8},{16,20},{20,16},{24,28},{28,24},{1,5},{5... | collective-permute-start | bytes 393224 | tf_op jit(solution)/shard_map/ppermute | solution.py:544
  8.2 12.7 %collective-permute-start.4 = (bf16[128,512]{1,0:T(8,128)(2,1)S(1)}, bf16[128,512]{1,0:T(8,128)(2,1)S(1)}, u32[]{:S(2)}, u32[]{:S(2)}) collective-permute-start(bf16[128,512]{1,0:T(8,128)(2,1)S(1)} %get-tuple-element.30.refs_3_), channel_id=1, source_target_pairs={{0,1},{1,3},{3,2},{2,0},{4,5},{5,7},{7,6},{6,4},{8,9},{9,11},{11,1... | collective-permute-start | bytes 393224 | tf_op jit(solution)/shard_map/ppermute | solution.py:49
  9.0 13.4 %collective-permute-start.7 = (bf16[128,512]{1,0:T(8,128)(2,1)S(1)}, bf16[128,512]{1,0:T(8,128)(2,1)S(1)}, u32[]{:S(2)}, u32[]{:S(2)}) collective-permute-start(bf16[128,512]{1,0:T(8,128)(2,1)S(1)} %get-tuple-element.35.refs_0_), channel_id=1, source_target_pairs={{1,0},{3,1},{2,3},{0,2},{5,4},{7,5},{6,7},{4,6},{9,8},{11,9},{10,1... | collective-permute-start | bytes 393224 | tf_op jit(solution)/shard_map/ppermute | solution.py:49
  12.4 13.5 %collective-permute-start.10 = (bf16[128,512]{1,0:T(8,128)(2,1)S(1)}, bf16[128,512]{1,0:T(8,128)(2,1)S(1)}, u32[]{:S(2)}, u32[]{:S(2)}) collective-permute-start(bf16[128,512]{1,0:T(8,128)(2,1)S(1)} %get-tuple-element.36.refs_4_), channel_id=1, source_target_pairs={{1,0},{3,1},{2,3},{0,2},{5,4},{7,5},{6,7},{4,6},{9,8},{11,9},{10,1... | collective-permute-start | bytes 393224 | tf_op jit(solution)/shard_map/ppermute | solution.py:49
  15.2 14.3 %collective-permute-start.8 = (bf16[128,512]{1,0:T(8,128)(2,1)S(1)}, bf16[128,512]{1,0:T(8,128)(2,1)S(1)}, u32[]{:S(2)}, u32[]{:S(2)}) collective-permute-start(bf16[128,512]{1,0:T(8,128)(2,1)S(1)} %collective-permute-done.6.refs_1_), channel_id=1, source_target_pairs={{0,1},{1,3},{3,2},{2,0},{4,5},{5,7},{7,6},{6,4},{8,9},{9,11},{11,1... | collective-permute-start | bytes 393224 | tf_op jit(solution)/shard_map/ppermute | solution.py:49
  16.9 12.7 %collective-permute-start.11 = (bf16[128,512]{1,0:T(8,128)(2,1)S(1)}, bf16[128,512]{1,0:T(8,128)(2,1)S(1)}, u32[]{:S(2)}, u32[]{:S(2)}) collective-permute-start(bf16[128,512]{1,0:T(8,128)(2,1)S(1)} %collective-permute-done.9.refs_5_), channel_id=1, source_target_pairs={{0,1},{1,3},{3,2},{2,0},{4,5},{5,7},{7,6},{6,4},{8,9},{9,11},{11,1... | collective-permute-start | bytes 393224 | tf_op jit(solution)/shard_map/ppermute | solution.py:49
  20.9 19.9 %collective-permute-start.24 = (bf16[256,512]{1,0:T(8,128)(2,1)S(1)}, bf16[256,512]{1,0:T(8,128)(2,1)S(1)}, u32[]{:S(2)}, u32[]{:S(2)}) collective-permute-start(bf16[256,512]{1,0:T(8,128)(2,1)S(1)} %shard_map.57.one_ref), channel_id=1, source_target_pairs={{0,8},{4,12},{8,0},{12,4},{16,24},{20,28},{24,16},{28,20},{1,9},{5... | collective-permute-start | bytes 786440 | tf_op jit(solution)/shard_map/ppermute | solution.py:544
  22.5 12.2 %collective-permute-start.3 = (bf16[128,512]{1,0:T(8,128)(2,1)S(1)}, bf16[128,512]{1,0:T(8,128)(2,1)S(1)}, u32[]{:S(2)}, u32[]{:S(2)}) collective-permute-start(bf16[128,512]{1,0:T(8,128)(2,1)S(1)} %collective-permute-done.2.refs_1_), channel_id=1, source_target_pairs={{0,1},{1,3},{3,2},{2,0},{4,5},{5,7},{7,6},{6,4},{8,9},{9,11},{11,1... | collective-permute-start | bytes 393224 | tf_op jit(solution)/shard_map/ppermute | solution.py:49
  26.0 9.1 %collective-permute-start.5 = (bf16[128,512]{1,0:T(8,128)(2,1)S(1)}, bf16[128,512]{1,0:T(8,128)(2,1)S(1)}, u32[]{:S(2)}, u32[]{:S(2)}) collective-permute-start(bf16[128,512]{1,0:T(8,128)(2,1)S(1)} %collective-permute-done.4.refs_4_), channel_id=1, source_target_pairs={{0,1},{1,3},{3,2},{2,0},{4,5},{5,7},{7,6},{6,4},{8,9},{9,11},{11,1... | collective-permute-start | bytes 393224 | tf_op jit(solution)/shard_map/ppermute | solution.py:49
  29.5 8.0 %collective-permute-start = (bf16[128,512]{1,0:T(8,128)(2,1)S(1)}, bf16[128,512]{1,0:T(8,128)(2,1)S(1)}, u32[]{:S(2)}, u32[]{:S(2)}) collective-permute-start(bf16[128,512]{1,0:T(8,128)(2,1)S(1)} %get-tuple-element.29.refs_0_), channel_id=1, source_target_pairs={{1,0},{3,1},{2,3},{0,2},{5,4},{7,5},{6,7},{4,6},{9,8},{11,9},{10,1... | collective-permute-start | bytes 393224 | tf_op jit(solution)/shard_map/ppermute | solution.py:49
  29.6 9.9 %collective-permute-start.1 = (bf16[128,512]{1,0:T(8,128)(2,1)S(1)}, bf16[128,512]{1,0:T(8,128)(2,1)S(1)}, u32[]{:S(2)}, u32[]{:S(2)}) collective-permute-start(bf16[128,512]{1,0:T(8,128)(2,1)S(1)} %get-tuple-element.30.refs_3_), channel_id=1, source_target_pairs={{1,0},{3,1},{2,3},{0,2},{5,4},{7,5},{6,7},{4,6},{9,8},{11,9},{10,1... | collective-permute-start | bytes 393224 | tf_op jit(solution)/shard_map/ppermute | solution.py:49
  34.7 29.2 %collective-permute-start.12 = (bf16[256,512]{1,0:T(8,128)(2,1)S(1)}, bf16[256,512]{1,0:T(8,128)(2,1)S(1)}, u32[]{:S(2)}, u32[]{:S(2)}) collective-permute-start(bf16[256,512]{1,0:T(8,128)(2,1)S(1)} %get-tuple-element.37.refs_0_), channel_id=1, source_target_pairs={{0,4},{4,8},{8,12},{12,16},{16,20},{20,24},{24,28},{28,0},{1,5},{5... | collective-permute-start | bytes 786440 | tf_op jit(solution)/shard_map/ppermute | solution.py:55
  35.1 8.7 %collective-permute-start.13 = (bf16[88,512]{1,0:T(8,128)(2,1)S(1)}, bf16[88,512]{1,0:T(8,128)(2,1)S(1)}, u32[]{:S(2)}, u32[]{:S(2)}) collective-permute-start(bf16[88,512]{1,0:T(8,128)(2,1)S(1)} %get-tuple-element.38), channel_id=1, source_target_pairs={{0,16},{4,20},{8,24},{12,28},{16,0},{20,4},{24,8},{28,12},{1,17},{... | collective-permute-start | bytes 270344 | tf_op jit(solution)/shard_map/ppermute | solution.py:55
  40.7 26.0 %collective-permute-start.16 = (bf16[256,512]{1,0:T(8,128)(2,1)S(1)}, bf16[256,512]{1,0:T(8,128)(2,1)S(1)}, u32[]{:S(2)}, u32[]{:S(2)}) collective-permute-start(bf16[256,512]{1,0:T(8,128)(2,1)S(1)} %shard_map.51.refs_1_), channel_id=1, source_target_pairs={{0,4},{4,8},{8,12},{12,16},{16,20},{20,24},{24,28},{28,0},{1,5},{5... | collective-permute-start | bytes 786440 | tf_op jit(solution)/shard_map/ppermute | solution.py:55
  40.8 47.9 %collective-permute-start.25 = (bf16[512,512]{1,0:T(8,128)(2,1)S(1)}, bf16[512,512]{1,0:T(8,128)(2,1)S(1)}, u32[]{:S(2)}, u32[]{:S(2)}) collective-permute-start(bf16[512,512]{1,0:T(8,128)(2,1)S(1)} %shard_map.58.one_ref), channel_id=1, source_target_pairs={{0,16},{4,20},{8,24},{12,28},{16,0},{20,4},{24,8},{28,12},{1,17},{... | collective-permute-start | bytes 1572872 | tf_op jit(solution)/shard_map/ppermute | solution.py:544
  42.4 19.9 %collective-permute-start.14 = (bf16[88,512]{1,0:T(8,128)(2,1)S(1)}, bf16[88,512]{1,0:T(8,128)(2,1)S(1)}, u32[]{:S(2)}, u32[]{:S(2)}) collective-permute-start(bf16[88,512]{1,0:T(8,128)(2,1)S(1)} %get-tuple-element.39), channel_id=1, source_target_pairs={{0,12},{4,16},{8,20},{12,24},{16,28},{20,0},{24,4},{28,8},{1,13},{... | collective-permute-start | bytes 270344 | tf_op jit(solution)/shard_map/ppermute | solution.py:55
  43.8 20.1 %collective-permute-start.15 = (bf16[88,512]{1,0:T(8,128)(2,1)S(1)}, bf16[88,512]{1,0:T(8,128)(2,1)S(1)}, u32[]{:S(2)}, u32[]{:S(2)}) collective-permute-start(bf16[88,512]{1,0:T(8,128)(2,1)S(1)} %get-tuple-element.40), channel_id=1, source_target_pairs={{0,8},{4,12},{8,16},{12,20},{16,24},{20,28},{24,0},{28,4},{1,9},{5... | collective-permute-start | bytes 270344 | tf_op jit(solution)/shard_map/ppermute | solution.py:55
  62.3 8.1 %collective-permute-start.17 = (bf16[88,512]{1,0:T(8,128)(2,1)S(1)}, bf16[88,512]{1,0:T(8,128)(2,1)S(1)}, u32[]{:S(2)}, u32[]{:S(2)}) collective-permute-start(bf16[88,512]{1,0:T(8,128)(2,1)S(1)} %get-tuple-element.45), channel_id=1, source_target_pairs={{0,16},{4,20},{8,24},{12,28},{16,0},{20,4},{24,8},{28,12},{1,17},{... | collective-permute-start | bytes 270344 | tf_op jit(solution)/shard_map/ppermute | solution.py:55
  71.7 10.1 %collective-permute-start.21 = (bf16[256,256]{1,0:T(8,128)(2,1)S(1)}, bf16[256,256]{1,0:T(8,128)(2,1)S(1)}, u32[]{:S(2)}, u32[]{:S(2)}) collective-permute-start(bf16[256,256]{1,0:T(8,128)(2,1)S(1)} %shard_map.56.refs_0_), channel_id=1, source_target_pairs={{0,1},{1,3},{3,2},{2,0},{4,5},{5,7},{7,6},{6,4},{8,9},{9,11},{11,1... | collective-permute-start | bytes 393224 | tf_op jit(solution)/shard_map/ppermute | solution.py:49
  85.3 7.4 %collective-permute-start.28 = (bf16[256,256]{1,0:T(8,128)(2,1)S(1)}, bf16[256,256]{1,0:T(8,128)(2,1)S(1)}, u32[]{:S(2)}, u32[]{:S(2)}) collective-permute-start(bf16[256,256]{1,0:T(8,128)(2,1)S(1)} %collective-permute-done.27.refs_1_), channel_id=1, source_target_pairs={{0,1},{1,3},{3,2},{2,0},{4,5},{5,7},{7,6},{6,4},{8,9},{9,11},{11,1... | collective-permute-start | bytes 393224 | tf_op jit(solution)/shard_map/ppermute | solution.py:49
  88.2 7.3 %collective-permute-start.20 = (bf16[256,256]{1,0:T(8,128)(2,1)S(1)}, bf16[256,256]{1,0:T(8,128)(2,1)S(1)}, u32[]{:S(2)}, u32[]{:S(2)}) collective-permute-start(bf16[256,256]{1,0:T(8,128)(2,1)S(1)} %shard_map.56.refs_0_), channel_id=1, source_target_pairs={{1,0},{3,1},{2,3},{0,2},{5,4},{7,5},{6,7},{4,6},{9,8},{11,9},{10,1... | collective-permute-start | bytes 393224 | tf_op jit(solution)/shard_map/ppermute | solution.py:49
  (7 other events, 38.6 us)

commit v4 on v3

--- a/solution.py
+++ b/solution.py
@@ -35,7 +35,7 @@
     return -((step + 1) // 2) if step % 2 else step // 2
 
 
-EARLY = 8
+EARLY = 10
 FINAL = 2
 EARLY_PARTS, LATE_PARTS = 2, 2
 
@@ -166,30 +166,37 @@
     )(w3)
 
 
-def project(chunks, w3, col_sums):
+def project(chunks, w3, col_sums, q_rows):
     n_head, n_chunk = len(chunks[0]), len(chunks)
     piece, feats = chunks[0][0].shape
     width = w3.shape[2]
     rows = piece * n_chunk
+    n_q = 2 if rows > q_rows else 1
 
     def body(*refs):
-        w_ref, sum_ref, q_ref, kv_ref = refs[n_head * n_chunk :]
+        w_ref, sum_ref, *q_refs, kv_ref = refs[n_head * n_chunk :]
         for c in range(n_chunk):
             blocks = refs[c * n_head : (c + 1) * n_head]
             mean, inv = joined_moments([moments(b[...]) for b in blocks], feats)
-            at = pl.ds(c * piece, piece)
+            begin, end = c * piece, (c + 1) * piece
             for i in range(3):
                 acc = project_sum(blocks, range(n_head), w_ref, i)
                 cols = slice(i * width, (i + 1) * width)
                 acc = ((acc - mean * sum_ref[0:1, cols]) * inv).astype(BF16)
-                if i == 0:
-                    q_ref[at, :] = acc
-                else:
-                    kv_ref[at, (i - 1) * width : i * width] = acc
+                if i > 0:
+                    kv_ref[begin:end, (i - 1) * width : i * width] = acc
+                    continue
+                cut = min(max(q_rows - begin, 0), piece)
+                if cut:
+                    q_refs[0][begin : begin + cut, :] = acc[:cut]
+                if cut < piece:
+                    q_refs[1][begin + cut - q_rows : end - q_rows, :] = acc[cut:]
 
     flat = [b for chunk in chunks for b in chunk]
-    outs = [((rows, width), BF16), ((rows, 2 * width), BF16)]
-    return call(body, outs, [*flat, w3, col_sums])
+    outs = [((min(q_rows, rows), width), BF16), ((rows - q_rows, width), BF16)][:n_q]
+    outs.append(((rows, 2 * width), BF16))
+    *queries, kv = call(body, outs, [*flat, w3, col_sums])
+    return queries, kv
 
 
 def project_begin(chunks, steps, w3):
@@ -218,15 +225,18 @@
     return call(body, outs, [*flat, w3])
 
 
-def project_end(lasts, last, begun, w3, col_sums, kinds):
+def project_end(lasts, last, begun, w3, col_sums, kinds, ahead=()):
     n_chunk = len(lasts)
     piece, feats = lasts[0].shape
     width = w3.shape[2]
-    rows = piece * n_chunk
+    skip = sum(a.shape[0] for a in ahead)
+    rows = piece * n_chunk + skip
     n_begun = w3.shape[1] // feats - 1
 
     def body(*refs):
-        w_ref, acc_ref, mom_ref, sum_ref, out_ref = refs[n_chunk:]
+        w_ref, acc_ref, mom_ref, sum_ref, *ahead_refs, out_ref = refs[n_chunk:]
+        for a in ahead_refs:
+            out_ref[:skip, :] = a[...]
         for c in range(n_chunk):
             at = pl.ds(c * piece, piece)
             held = mom_ref[at, :]
@@ -237,10 +247,11 @@
                 cols = slice(i * width, (i + 1) * width)
                 acc = acc_ref[at, cols] + project_sum([refs[c]], [last], w_ref, i)
                 acc = (acc - mean * sum_ref[0:1, cols]) * inv
-                out_ref[at, k * width : (k + 1) * width] = acc.astype(BF16)
+                to = pl.ds(skip + c * piece, piece)
+                out_ref[to, k * width : (k + 1) * width] = acc.astype(BF16)
 
     outs = [((rows, len(kinds) * width), BF16)]
-    return call(body, outs, [*lasts, w3, *begun, col_sums])[0]
+    return call(body, outs, [*lasts, w3, *begun, col_sums, *ahead])[0]
 
 
 class Slots:
@@ -251,12 +262,12 @@
         self.tail = [seg_len - o - RATE * n for o, n in zip(self.offset, self.count)]
         self.early = [max(0, (early_rows - o) // RATE) for o in self.offset]
         self.late = [n - e for n, e in zip(self.count, self.early)]
-        most = max(
+        most = (
             max(e + o for e, o in zip(self.early, self.offset)),
             max(l + t for l, t in zip(self.late, self.tail)),
         )
-        self.rows = -(-most // 8) * 8
-        self.pitch = -(-most // 16) * 16
+        self.rows = [-(-m // 8) * 8 for m in most]
+        self.pitch = [-(-m // 16) * 16 for m in most]
         self.joints = [b for b in range(RATE - 1) if self.tail[b] > 0]
 
 
@@ -269,7 +280,7 @@
 
 def write_slots(slots, late, sources, w_ref, outs):
     weight = filter_rows(w_ref)
-    n = slots.rows
+    n = slots.rows[late]
     main = sources[-1]
     base = slots.early_rows if late else 0
     counts = slots.late if late else slots.early
@@ -311,7 +322,7 @@
     def body(*refs):
         write_slots(slots, n_in == 2, refs[:n_in], refs[n_in], refs[n_in + 1 :])
 
-    outs = [((slots.rows, 2 * weight.shape[2]), BF16)] * RATE
+    outs = [((slots.rows[n_in == 2], 2 * weight.shape[2]), BF16)] * RATE
     return call(body, outs, [*sources, weight])
 
 
@@ -330,9 +341,9 @@
     return jnp.where(valid & (seg >= BACK), 0.0, NEG).astype(F32)
 
 
-def attend_begin(slots, q, own, memory, early):
+def attend_begin(slots, q, q_start, own, memory, early):
     rows, width = q.shape
-    n, pitch = slots.rows, slots.pitch
+    n, pitch = slots.rows[0], slots.pitch[0]
     n_comp = -(-RATE * pitch // 128) * 128
     heads = width // DH
 
@@ -347,9 +358,18 @@
             comp_ref[a * pitch : a * pitch + n, :] = early_refs[a][...]
         comp_bias = slot_bias(seg, n_comp, [(a * pitch, slots.early[a]) for a in range(RATE)])
         mem_bias = jnp.where(seg >= 1, 0.0, NEG).astype(F32)
-        q_row = lax.broadcasted_iota(jnp.int32, (rows, rows), 0)
-        k_row = lax.broadcasted_iota(jnp.int32, (rows, rows), 1)
-        causal = k_row <= q_row
+        seen = []
+        k_start = 0
+        for o in own_refs:
+            n_keys = min(o.shape[0], q_start + rows - k_start)
+            mask = None
+            if k_start + n_keys - 1 > q_start:
+                q_row = lax.broadcasted_iota(jnp.int32, (rows, n_keys), 0) + q_start
+                k_row = lax.broadcasted_iota(jnp.int32, (rows, n_keys), 1) + k_start
+                mask = k_row <= q_row
+            if n_keys > 0:
+                seen.append((o, n_keys, mask))
+            k_start += o.shape[0]
         lane = lax.broadcasted_iota(jnp.int32, (rows, 128), 1)
         stats = jnp.zeros((rows, 128), F32)
         for h in range(heads):
@@ -360,10 +380,9 @@
                 (score(q, comp_ref[:, kc]) + comp_bias, comp_ref, vc),
                 (score(q, mem_ref[:, kc]) + mem_bias, mem_ref, vc),
             ]
-            for o in own_refs[:-1]:
-                pieces.append((score(q, o[:, kc]), o, vc))
-            o = own_refs[-1]
-            pieces.append((jnp.where(causal, score(q, o[:, kc]), NEG), o, vc))
+            for o, n_keys, mask in seen:
+                s = score(q, o[:n_keys, kc])
+                pieces.append((s if mask is None else jnp.where(mask, s, NEG), o, vc))
             top, norm, mixed = gathered(pieces, None)
             mix_ref[:, kc] = mixed
             stats = jnp.where(lane == 2 * h, top, stats)
@@ -387,7 +406,7 @@
     for s, v, cols in pieces:
         p = jnp.exp2((s - top) * SCALE)
         total = jnp.sum(p, axis=1, keepdims=True)
-        part = jnp.dot(p.astype(BF16), v[:, cols], preferred_element_type=F32)
+        part = jnp.dot(p.astype(BF16), v[: s.shape[1], cols], preferred_element_type=F32)
         norm = total if norm is None else norm + total
         mixed = part if mixed is None else mixed + part
     return top, norm, mixed
@@ -422,7 +441,7 @@
 
 def attend_end(slots, q, begun, heads_of, late, weight):
     rows, width = q.shape
-    n, pitch = slots.rows, slots.pitch
+    n, pitch = slots.rows[1], slots.pitch[1]
     n_comp = -(-(RATE * pitch + 16) // 128) * 128
     heads = width // DH
 
@@ -578,7 +597,9 @@
         for chunk in first:
             chunk.append(spread(chunk, t))
     w_full = gather_rows(w_out, xored)
-    q0, kv0 = project(first, w_vmem, col_sums)
+    half = seg_len // 2
+    queries, kv0 = project(first, w_vmem, col_sums, half)
+    q0, ahead = queries[0], queries[1:]
     early_parts = compress(slots, [kv0], weight)
     mem0 = passed_along(kv0, 1)
     early = [passed_along(p, BACK - a) for a, p in enumerate(early_parts)]
@@ -594,11 +615,11 @@
     mem1 = passed_along(kv1, 1)
     late_parts = compress(slots, [kv0, kv1], weight)
     late = [passed_along(p, BACK - a) for a, p in enumerate(late_parts)]
-    q1 = project_end(lasts, final, begun, w_vmem, col_sums, (0,))
+    q1 = project_end(lasts, final, begun, w_vmem, col_sums, (0,), ahead)
 
     rings = []
-    for q, own in ((q0, [kv0]), (q1, [kv0, kv1])):
-        part = attend_begin(slots, q, own, mem0, early)
+    for h, (q, own) in enumerate(((q0, [kv0]), (q1, [kv0, kv1]))):
+        part = attend_begin(slots, q, h * half, own, mem0, early)
         part = attend_more(q, part, mem1)
         ctx = attend_end(slots, q, part, early, late, weight)
         rings.append([ctx])
@@ -608,9 +629,7 @@
     result = None
     for h, ring in enumerate(rings):
         part = output_begin([ring[t] for t in steps], steps, w_full, xored)
-        result = output_end(
-            h * early_rows, seg_len, final, ring[final], part, w_full, xored, result,
-        )
+        result = output_end(h * half, seg_len, final, ring[final], part, w_full, xored, result)
     return result[None]
 
 

time: 96.8 us -> 92.5 us (0.956)
  starting transfers between devices: 44.2 us -> 38.7 us
    ppermute x18, waiting for transfers between devices: 12.8 us -> 20 us  [spread(): return lax.ppermute(block, 'head', list(zip(order, towards)))]
    ppermute x8, waiting for transfers between devices: 19.7 us -> 13.4 us  [passed_along(): return lax.ppermute(block, 'seg', route)]
    ppermute x18, starting transfers between devices: 34.4 us -> 28.3 us  [spread(): return lax.ppermute(block, 'head', list(zip(order, towards)))]
  transfers between devices with their start and end apart: 29 -> 29, of which waited for: 12 -> 14; matrix products, arithmetic and copies ran while one was open for 0% -> 0% of each run, Pallas kernels for 17% -> 18%
where the time goes in v4:
time: 92.5 us; the launch traced here: 92.3 us
  starting transfers between devices  38.7 us (42%)
  waiting for transfers between devices  33.4 us (36%)
  Pallas kernels  18.9 us (20%)
    ppermute x18, starting transfers between devices, spread(): return lax.ppermute(block, 'head', list(zip(order, towards)))  28.3 us
    ppermute x18, waiting for transfers between devices, spread(): return lax.ppermute(block, 'head', list(zip(order, towards)))  20 us
    pallas_call x19, Pallas kernels, call(): pl.pallas_call(body, out_shape=tuple((jax.ShapeDtypeStruct(s, d) for s, d...  14.7 us
    ppermute x8, waiting for transfers between devices, passed_along(): return lax.ppermute(block, 'seg', route)  13.4 us
    ppermute x8, starting transfers between devices, passed_along(): return lax.ppermute(block, 'seg', route)  7.25 us
    ppermute x3, starting transfers between devices, gather_rows(): other = lax.ppermute(block, 'seg', [(i, i ^ step) for i in range(size)])  3.15 us
    pallas_call x1, Pallas kernels, fetch_weights(): pl.pallas_call(body, out_shape=(jax.ShapeDtypeStruct(w3.shape, w3.dtype),...  2.26 us
    pallas_call x2, Pallas kernels, output_end(): pl.pallas_call(body, out_shape=jax.ShapeDtypeStruct((n_rows, columns), BF...  1.92 us
  transfers between devices with their start and end apart: 29, of which 14 were waited for; matrix products, arithmetic and copies ran while one was open for 0% of the time, Pallas kernels for 18%

profile of v4, /device:TPU:0, one launch (start us, length us, event | category | flops | bytes accessed | tf_op | source)
XLA Modules:
  0.0 92.3 jit_solution(12217176558005652029)
XLA Ops:
  1.0 3.1 %collective-permute-start.6 = (bf16[160,512]{1,0:T(8,128)(2,1)S(1)}, bf16[160,512]{1,0:T(8,128)(2,1)S(1)}, u32[]{:S(2)}, u32[]{:S(2)}) collective-permute-start(bf16[160,512]{1,0:T(8,128)(2,1)S(1)} %get-tuple-element.36.refs_0_), channel_id=1, source_target_pairs={{0,1},{1,3},{3,2},{2,0},{4,5},{5,7},{7,6},{6,4},{8,9},{9,11},{11,1... | collective-permute-start | bytes 491528 | tf_op jit(solution)/shard_map/ppermute | solution.py:49
  4.1 2.6 %collective-permute-start.9 = (bf16[160,512]{1,0:T(8,128)(2,1)S(1)}, bf16[160,512]{1,0:T(8,128)(2,1)S(1)}, u32[]{:S(2)}, u32[]{:S(2)}) collective-permute-start(bf16[160,512]{1,0:T(8,128)(2,1)S(1)} %get-tuple-element.37.refs_4_), channel_id=1, source_target_pairs={{0,1},{1,3},{3,2},{2,0},{4,5},{5,7},{7,6},{6,4},{8,9},{9,11},{11,1... | collective-permute-start | bytes 491528 | tf_op jit(solution)/shard_map/ppermute | solution.py:49
  7.2 3.0 %collective-permute-done.6.refs_1_ = bf16[160,512]{1,0:T(8,128)(2,1)S(1)} collective-permute-done((bf16[160,512]{1,0:T(8,128)(2,1)S(1)}, bf16[160,512]{1,0:T(8,128)(2,1)S(1)}, u32[]{:S(2)}, u32[]{:S(2)}) %collective-permute-start.6) | collective-permute-done | bytes 163872 | tf_op jit(solution)/shard_map/ppermute | solution.py:49
  10.2 1.1 %collective-permute-start.8 = (bf16[160,512]{1,0:T(8,128)(2,1)S(1)}, bf16[160,512]{1,0:T(8,128)(2,1)S(1)}, u32[]{:S(2)}, u32[]{:S(2)}) collective-permute-start(bf16[160,512]{1,0:T(8,128)(2,1)S(1)} %collective-permute-done.6.refs_1_), channel_id=1, source_target_pairs={{0,1},{1,3},{3,2},{2,0},{4,5},{5,7},{7,6},{6,4},{8,9},{9,11},{11,1... | collective-permute-start | bytes 491528 | tf_op jit(solution)/shard_map/ppermute | solution.py:49
  11.3 3.1 %collective-permute-done.9.refs_5_ = bf16[160,512]{1,0:T(8,128)(2,1)S(1)} collective-permute-done((bf16[160,512]{1,0:T(8,128)(2,1)S(1)}, bf16[160,512]{1,0:T(8,128)(2,1)S(1)}, u32[]{:S(2)}, u32[]{:S(2)}) %collective-permute-start.9) | collective-permute-done | bytes 163872 | tf_op jit(solution)/shard_map/ppermute | solution.py:49
  14.5 7.4 %collective-permute-start.11 = (bf16[160,512]{1,0:T(8,128)(2,1)S(1)}, bf16[160,512]{1,0:T(8,128)(2,1)S(1)}, u32[]{:S(2)}, u32[]{:S(2)}) collective-permute-start(bf16[160,512]{1,0:T(8,128)(2,1)S(1)} %collective-permute-done.9.refs_5_), channel_id=1, source_target_pairs={{0,1},{1,3},{3,2},{2,0},{4,5},{5,7},{7,6},{6,4},{8,9},{9,11},{11,1... | collective-permute-start | bytes 491528 | tf_op jit(solution)/shard_map/ppermute | solution.py:49
  22.8 1.6 %collective-permute-start.24 = (bf16[256,512]{1,0:T(8,128)(2,1)S(1)}, bf16[256,512]{1,0:T(8,128)(2,1)S(1)}, u32[]{:S(2)}, u32[]{:S(2)}) collective-permute-start(bf16[256,512]{1,0:T(8,128)(2,1)S(1)} %shard_map.57.one_ref), channel_id=1, source_target_pairs={{0,8},{4,12},{8,0},{12,4},{16,24},{20,28},{24,16},{28,20},{1,9},{5... | collective-permute-start | bytes 786440 | tf_op jit(solution)/shard_map/ppermute | solution.py:563
  25.3 3.4 %collective-permute-start.2 = (bf16[96,512]{1,0:T(8,128)(2,1)S(1)}, bf16[96,512]{1,0:T(8,128)(2,1)S(1)}, u32[]{:S(2)}, u32[]{:S(2)}) collective-permute-start(bf16[96,512]{1,0:T(8,128)(2,1)S(1)} %get-tuple-element.30.refs_0_), channel_id=1, source_target_pairs={{0,1},{1,3},{3,2},{2,0},{4,5},{5,7},{7,6},{6,4},{8,9},{9,11},{11,1... | collective-permute-start | bytes 294920 | tf_op jit(solution)/shard_map/ppermute | solution.py:49
  28.9 2.3 %fetch.1 = (bf16[3,2048,256]{2,1,0:T(8,128)(2,1)S(1)}, f32[8,768]{1,0:T(8,128)S(1)}) custom-call(bf16[3,2048,256]{2,1,0:T(8,128)(2,1)} %bitcast.3), custom_call_target="tpu_custom_call" | custom-call | tf_op jit(solution)/shard_map/fetch/pallas_call | solution.py:155
  31.1 1.6 %shard_map.49 = (bf16[256,256]{1,0:T(8,128)(2,1)S(1)}, bf16[64,256]{1,0:T(8,128)(2,1)S(1)}, bf16[320,512]{1,0:T(8,128)(2,1)S(1)}) custom-call(bf16[160,512]{1,0:T(8,128)(2,1)S(1)} %get-tuple-element.36.refs_0_, bf16[160,512]{1,0:T(8,128)(2,1)S(1)} %collective-permute-done.6.refs_1_, bf16[160,512]{1,0:T(8,128)(2,1)S(1)} %collective-permute-done.7.refs_2_, ...), custom_call_target="tpu_custom_call" | custom-call | tf_op jit(solution)/shard_map/pallas_call | solution.py:73
  35.5 1.6 %collective-permute-start.13 = (bf16[112,512]{1,0:T(8,128)(2,1)S(1)}, bf16[112,512]{1,0:T(8,128)(2,1)S(1)}, u32[]{:S(2)}, u32[]{:S(2)}) collective-permute-start(bf16[112,512]{1,0:T(8,128)(2,1)S(1)} %get-tuple-element.40), channel_id=1, source_target_pairs={{0,16},{4,20},{8,24},{12,28},{16,0},{20,4},{24,8},{28,12},{1,17},{... | collective-permute-start | bytes 344072 | tf_op jit(solution)/shard_map/ppermute | solution.py:55
  37.1 2.4 %collective-permute-done.3.refs_2_ = bf16[96,512]{1,0:T(8,128)(2,1)S(1)} collective-permute-done((bf16[96,512]{1,0:T(8,128)(2,1)S(1)}, bf16[96,512]{1,0:T(8,128)(2,1)S(1)}, u32[]{:S(2)}, u32[]{:S(2)}) %collective-permute-start.3) | collective-permute-done | bytes 98336 | tf_op jit(solution)/shard_map/ppermute | solution.py:49
  39.5 2.0 %collective-permute-start = (bf16[96,512]{1,0:T(8,128)(2,1)S(1)}, bf16[96,512]{1,0:T(8,128)(2,1)S(1)}, u32[]{:S(2)}, u32[]{:S(2)}) collective-permute-start(bf16[96,512]{1,0:T(8,128)(2,1)S(1)} %get-tuple-element.30.refs_0_), channel_id=1, source_target_pairs={{1,0},{3,1},{2,3},{0,2},{5,4},{7,5},{6,7},{4,6},{9,8},{11,9},{10,1... | collective-permute-start | bytes 294920 | tf_op jit(solution)/shard_map/ppermute | solution.py:49
  41.5 1.6 %collective-permute-start.25 = (bf16[512,512]{1,0:T(8,128)(2,1)S(1)}, bf16[512,512]{1,0:T(8,128)(2,1)S(1)}, u32[]{:S(2)}, u32[]{:S(2)}) collective-permute-start(bf16[512,512]{1,0:T(8,128)(2,1)S(1)} %shard_map.58.one_ref), channel_id=1, source_target_pairs={{0,16},{4,20},{8,24},{12,28},{16,0},{20,4},{24,8},{28,12},{1,17},{... | collective-permute-start | bytes 1572872 | tf_op jit(solution)/shard_map/ppermute | solution.py:563
  47.1 2.7 %collective-permute-start.14 = (bf16[112,512]{1,0:T(8,128)(2,1)S(1)}, bf16[112,512]{1,0:T(8,128)(2,1)S(1)}, u32[]{:S(2)}, u32[]{:S(2)}) collective-permute-start(bf16[112,512]{1,0:T(8,128)(2,1)S(1)} %get-tuple-element.41), channel_id=1, source_target_pairs={{0,12},{4,16},{8,20},{12,24},{16,28},{20,0},{24,4},{28,8},{1,13},{... | collective-permute-start | bytes 344072 | tf_op jit(solution)/shard_map/ppermute | solution.py:55
  50.9 11.3 %collective-permute-done.14.refs_4_.refs_1_.refs_3_ = bf16[112,512]{1,0:T(8,128)(2,1)S(1)} collective-permute-done((bf16[112,512]{1,0:T(8,128)(2,1)S(1)}, bf16[112,512]{1,0:T(8,128)(2,1)S(1)}, u32[]{:S(2)}, u32[]{:S(2)}) %collective-permute-start.14) | collective-permute-done | bytes 114720 | tf_op jit(solution)/shard_map/ppermute | solution.py:55
  62.2 1.5 %collective-permute-start.17 = (bf16[72,512]{1,0:T(8,128)(2,1)S(1)}, bf16[72,512]{1,0:T(8,128)(2,1)S(1)}, u32[]{:S(2)}, u32[]{:S(2)}) collective-permute-start(bf16[72,512]{1,0:T(8,128)(2,1)S(1)} %get-tuple-element.47), channel_id=1, source_target_pairs={{0,16},{4,20},{8,24},{12,28},{16,0},{20,4},{24,8},{28,12},{1,17},{... | collective-permute-start | bytes 221192 | tf_op jit(solution)/shard_map/ppermute | solution.py:55
  65.0 1.5 %shard_map.53 = (f32[256,256]{1,0:T(8,128)S(1)}, f32[256,128]{1,0:T(8,128)S(1)}) custom-call(bf16[256,256]{1,0:T(8,128)(2,1)S(1)} %shard_map.50.q_ref, bf16[320,512]{1,0:T(8,128)(2,1)S(1)} %get-tuple-element.39.refs_0_, bf16[192,512]{1,0:T(8,128)(2,1)S(1)} %shard_map.51.refs_1_, bf16[320,512]{1,0:T(8,128)(2,1)S(1)} %collective-permute-done.12.refs_2_.refs_1_, ...), custom_call_target="tpu_custom_call" | custom-call | tf_op jit(solution)/shard_map/pallas_call | solution.py:73
  67.5 1.2 %collective-permute-done.17.refs_3_ = bf16[72,512]{1,0:T(8,128)(2,1)S(1)} collective-permute-done((bf16[72,512]{1,0:T(8,128)(2,1)S(1)}, bf16[72,512]{1,0:T(8,128)(2,1)S(1)}, u32[]{:S(2)}, u32[]{:S(2)}) %collective-permute-start.17) | collective-permute-done | bytes 73760 | tf_op jit(solution)/shard_map/ppermute | solution.py:55
  70.9 1.1 %shard_map.61 = (f32[256,256]{1,0:T(8,128)S(1)}, f32[256,128]{1,0:T(8,128)S(1)}) custom-call(bf16[256,256]{1,0:T(8,128)(2,1)S(1)} %get-tuple-element.50.q_ref, bf16[320,512]{1,0:T(8,128)(2,1)S(1)} %get-tuple-element.39.refs_0_, bf16[320,512]{1,0:T(8,128)(2,1)S(1)} %collective-permute-done.12.refs_2_.refs_1_, ...), custom_call_target="tpu_custom_call" | custom-call | tf_op jit(solution)/shard_map/pallas_call | solution.py:73
  74.0 1.9 %collective-permute-start.27 = (bf16[256,256]{1,0:T(8,128)(2,1)S(1)}, bf16[256,256]{1,0:T(8,128)(2,1)S(1)}, u32[]{:S(2)}, u32[]{:S(2)}) collective-permute-start(bf16[256,256]{1,0:T(8,128)(2,1)S(1)} %shard_map.63.refs_0_), channel_id=1, source_target_pairs={{0,1},{1,3},{3,2},{2,0},{4,5},{5,7},{7,6},{6,4},{8,9},{9,11},{11,1... | collective-permute-start | bytes 393224 | tf_op jit(solution)/shard_map/ppermute | solution.py:49
  77.7 3.6 %collective-permute-done.27.refs_1_ = bf16[256,256]{1,0:T(8,128)(2,1)S(1)} collective-permute-done((bf16[256,256]{1,0:T(8,128)(2,1)S(1)}, bf16[256,256]{1,0:T(8,128)(2,1)S(1)}, u32[]{:S(2)}, u32[]{:S(2)}) %collective-permute-start.27) | collective-permute-done | bytes 131104 | tf_op jit(solution)/shard_map/ppermute | solution.py:49
  82.1 2.1 %collective-permute-start.26 = (bf16[256,256]{1,0:T(8,128)(2,1)S(1)}, bf16[256,256]{1,0:T(8,128)(2,1)S(1)}, u32[]{:S(2)}, u32[]{:S(2)}) collective-permute-start(bf16[256,256]{1,0:T(8,128)(2,1)S(1)} %shard_map.63.refs_0_), channel_id=1, source_target_pairs={{1,0},{3,1},{2,3},{0,2},{5,4},{7,5},{6,7},{4,6},{9,8},{11,9},{10,1... | collective-permute-start | bytes 393224 | tf_op jit(solution)/shard_map/ppermute | solution.py:49
  85.7 3.1 %collective-permute-done.28.refs_2_ = bf16[256,256]{1,0:T(8,128)(2,1)S(1)} collective-permute-done((bf16[256,256]{1,0:T(8,128)(2,1)S(1)}, bf16[256,256]{1,0:T(8,128)(2,1)S(1)}, u32[]{:S(2)}, u32[]{:S(2)}) %collective-permute-start.28) | collective-permute-done | bytes 131104 | tf_op jit(solution)/shard_map/ppermute | solution.py:49
  (60 shorter events, 25.3 us)
Async XLA Ops:
  1.0 9.2 %collective-permute-start.6 = (bf16[160,512]{1,0:T(8,128)(2,1)S(1)}, bf16[160,512]{1,0:T(8,128)(2,1)S(1)}, u32[]{:S(2)}, u32[]{:S(2)}) collective-permute-start(bf16[160,512]{1,0:T(8,128)(2,1)S(1)} %get-tuple-element.36.refs_0_), channel_id=1, source_target_pairs={{0,1},{1,3},{3,2},{2,0},{4,5},{5,7},{7,6},{6,4},{8,9},{9,11},{11,1... | collective-permute-start | bytes 491528 | tf_op jit(solution)/shard_map/ppermute | solution.py:49
  4.1 10.4 %collective-permute-start.9 = (bf16[160,512]{1,0:T(8,128)(2,1)S(1)}, bf16[160,512]{1,0:T(8,128)(2,1)S(1)}, u32[]{:S(2)}, u32[]{:S(2)}) collective-permute-start(bf16[160,512]{1,0:T(8,128)(2,1)S(1)} %get-tuple-element.37.refs_4_), channel_id=1, source_target_pairs={{0,1},{1,3},{3,2},{2,0},{4,5},{5,7},{7,6},{6,4},{8,9},{9,11},{11,1... | collective-permute-start | bytes 491528 | tf_op jit(solution)/shard_map/ppermute | solution.py:49
  6.7 15.2 %collective-permute-start.23 = (bf16[128,512]{1,0:T(8,128)(2,1)}, bf16[128,512]{1,0:T(8,128)(2,1)S(1)}, u32[]{:S(2)}, u32[]{:S(2)}) collective-permute-start(bf16[128,512]{1,0:T(8,128)(2,1)} %one_ref.1), channel_id=1, source_target_pairs={{0,4},{4,0},{8,12},{12,8},{16,20},{20,16},{24,28},{28,24},{1,5},{5... | collective-permute-start | bytes 393224 | tf_op jit(solution)/shard_map/ppermute | solution.py:563
  6.7 18.6 %collective-permute-start.7 = (bf16[160,512]{1,0:T(8,128)(2,1)S(1)}, bf16[160,512]{1,0:T(8,128)(2,1)S(1)}, u32[]{:S(2)}, u32[]{:S(2)}) collective-permute-start(bf16[160,512]{1,0:T(8,128)(2,1)S(1)} %get-tuple-element.36.refs_0_), channel_id=1, source_target_pairs={{1,0},{3,1},{2,3},{0,2},{5,4},{7,5},{6,7},{4,6},{9,8},{11,9},{10,1... | collective-permute-start | bytes 491528 | tf_op jit(solution)/shard_map/ppermute | solution.py:49
  7.1 21.7 %collective-permute-start.10 = (bf16[160,512]{1,0:T(8,128)(2,1)S(1)}, bf16[160,512]{1,0:T(8,128)(2,1)S(1)}, u32[]{:S(2)}, u32[]{:S(2)}) collective-permute-start(bf16[160,512]{1,0:T(8,128)(2,1)S(1)} %get-tuple-element.37.refs_4_), channel_id=1, source_target_pairs={{1,0},{3,1},{2,3},{0,2},{5,4},{7,5},{6,7},{4,6},{9,8},{11,9},{10,1... | collective-permute-start | bytes 491528 | tf_op jit(solution)/shard_map/ppermute | solution.py:49
  10.2 20.9 %collective-permute-start.8 = (bf16[160,512]{1,0:T(8,128)(2,1)S(1)}, bf16[160,512]{1,0:T(8,128)(2,1)S(1)}, u32[]{:S(2)}, u32[]{:S(2)}) collective-permute-start(bf16[160,512]{1,0:T(8,128)(2,1)S(1)} %collective-permute-done.6.refs_1_), channel_id=1, source_target_pairs={{0,1},{1,3},{3,2},{2,0},{4,5},{5,7},{7,6},{6,4},{8,9},{9,11},{11,1... | collective-permute-start | bytes 491528 | tf_op jit(solution)/shard_map/ppermute | solution.py:49
  14.5 16.6 %collective-permute-start.11 = (bf16[160,512]{1,0:T(8,128)(2,1)S(1)}, bf16[160,512]{1,0:T(8,128)(2,1)S(1)}, u32[]{:S(2)}, u32[]{:S(2)}) collective-permute-start(bf16[160,512]{1,0:T(8,128)(2,1)S(1)} %collective-permute-done.9.refs_5_), channel_id=1, source_target_pairs={{0,1},{1,3},{3,2},{2,0},{4,5},{5,7},{7,6},{6,4},{8,9},{9,11},{11,1... | collective-permute-start | bytes 491528 | tf_op jit(solution)/shard_map/ppermute | solution.py:49
  22.8 18.6 %collective-permute-start.24 = (bf16[256,512]{1,0:T(8,128)(2,1)S(1)}, bf16[256,512]{1,0:T(8,128)(2,1)S(1)}, u32[]{:S(2)}, u32[]{:S(2)}) collective-permute-start(bf16[256,512]{1,0:T(8,128)(2,1)S(1)} %shard_map.57.one_ref), channel_id=1, source_target_pairs={{0,8},{4,12},{8,0},{12,4},{16,24},{20,28},{24,16},{28,20},{1,9},{5... | collective-permute-start | bytes 786440 | tf_op jit(solution)/shard_map/ppermute | solution.py:563
  25.3 7.5 %collective-permute-start.2 = (bf16[96,512]{1,0:T(8,128)(2,1)S(1)}, bf16[96,512]{1,0:T(8,128)(2,1)S(1)}, u32[]{:S(2)}, u32[]{:S(2)}) collective-permute-start(bf16[96,512]{1,0:T(8,128)(2,1)S(1)} %get-tuple-element.30.refs_0_), channel_id=1, source_target_pairs={{0,1},{1,3},{3,2},{2,0},{4,5},{5,7},{7,6},{6,4},{8,9},{9,11},{11,1... | collective-permute-start | bytes 294920 | tf_op jit(solution)/shard_map/ppermute | solution.py:49
  32.8 30.9 %collective-permute-start.12 = (bf16[320,512]{1,0:T(8,128)(2,1)S(1)}, bf16[320,512]{1,0:T(8,128)(2,1)S(1)}, u32[]{:S(2)}, u32[]{:S(2)}) collective-permute-start(bf16[320,512]{1,0:T(8,128)(2,1)S(1)} %get-tuple-element.39.refs_0_), channel_id=1, source_target_pairs={{0,4},{4,8},{8,12},{12,16},{16,20},{20,24},{24,28},{28,0},{1,5},{5... | collective-permute-start | bytes 983048 | tf_op jit(solution)/shard_map/ppermute | solution.py:55
  32.8 6.6 %collective-permute-start.3 = (bf16[96,512]{1,0:T(8,128)(2,1)S(1)}, bf16[96,512]{1,0:T(8,128)(2,1)S(1)}, u32[]{:S(2)}, u32[]{:S(2)}) collective-permute-start(bf16[96,512]{1,0:T(8,128)(2,1)S(1)} %collective-permute-done.2.refs_1_), channel_id=1, source_target_pairs={{0,1},{1,3},{3,2},{2,0},{4,5},{5,7},{7,6},{6,4},{8,9},{9,11},{11,1... | collective-permute-start | bytes 294920 | tf_op jit(solution)/shard_map/ppermute | solution.py:49
  34.3 7.2 %collective-permute-start.5 = (bf16[96,512]{1,0:T(8,128)(2,1)S(1)}, bf16[96,512]{1,0:T(8,128)(2,1)S(1)}, u32[]{:S(2)}, u32[]{:S(2)}) collective-permute-start(bf16[96,512]{1,0:T(8,128)(2,1)S(1)} %collective-permute-done.4.refs_4_), channel_id=1, source_target_pairs={{0,1},{1,3},{3,2},{2,0},{4,5},{5,7},{7,6},{6,4},{8,9},{9,11},{11,1... | collective-permute-start | bytes 294920 | tf_op jit(solution)/shard_map/ppermute | solution.py:49
  35.5 14.3 %collective-permute-start.13 = (bf16[112,512]{1,0:T(8,128)(2,1)S(1)}, bf16[112,512]{1,0:T(8,128)(2,1)S(1)}, u32[]{:S(2)}, u32[]{:S(2)}) collective-permute-start(bf16[112,512]{1,0:T(8,128)(2,1)S(1)} %get-tuple-element.40), channel_id=1, source_target_pairs={{0,16},{4,20},{8,24},{12,28},{16,0},{20,4},{24,8},{28,12},{1,17},{... | collective-permute-start | bytes 344072 | tf_op jit(solution)/shard_map/ppermute | solution.py:55
  41.5 43.6 %collective-permute-start.25 = (bf16[512,512]{1,0:T(8,128)(2,1)S(1)}, bf16[512,512]{1,0:T(8,128)(2,1)S(1)}, u32[]{:S(2)}, u32[]{:S(2)}) collective-permute-start(bf16[512,512]{1,0:T(8,128)(2,1)S(1)} %shard_map.58.one_ref), channel_id=1, source_target_pairs={{0,16},{4,20},{8,24},{12,28},{16,0},{20,4},{24,8},{28,12},{1,17},{... | collective-permute-start | bytes 1572872 | tf_op jit(solution)/shard_map/ppermute | solution.py:563
  47.0 19.5 %collective-permute-start.16 = (bf16[192,512]{1,0:T(8,128)(2,1)S(1)}, bf16[192,512]{1,0:T(8,128)(2,1)S(1)}, u32[]{:S(2)}, u32[]{:S(2)}) collective-permute-start(bf16[192,512]{1,0:T(8,128)(2,1)S(1)} %shard_map.51.refs_1_), channel_id=1, source_target_pairs={{0,4},{4,8},{8,12},{12,16},{16,20},{20,24},{24,28},{28,0},{1,5},{5... | collective-permute-start | bytes 589832 | tf_op jit(solution)/shard_map/ppermute | solution.py:55
  47.1 15.1 %collective-permute-start.14 = (bf16[112,512]{1,0:T(8,128)(2,1)S(1)}, bf16[112,512]{1,0:T(8,128)(2,1)S(1)}, u32[]{:S(2)}, u32[]{:S(2)}) collective-permute-start(bf16[112,512]{1,0:T(8,128)(2,1)S(1)} %get-tuple-element.41), channel_id=1, source_target_pairs={{0,12},{4,16},{8,20},{12,24},{16,28},{20,0},{24,4},{28,8},{1,13},{... | collective-permute-start | bytes 344072 | tf_op jit(solution)/shard_map/ppermute | solution.py:55
  49.8 13.9 %collective-permute-start.15 = (bf16[112,512]{1,0:T(8,128)(2,1)S(1)}, bf16[112,512]{1,0:T(8,128)(2,1)S(1)}, u32[]{:S(2)}, u32[]{:S(2)}) collective-permute-start(bf16[112,512]{1,0:T(8,128)(2,1)S(1)} %get-tuple-element.42), channel_id=1, source_target_pairs={{0,8},{4,12},{8,16},{12,20},{16,24},{20,28},{24,0},{28,4},{1,9},{5... | collective-permute-start | bytes 344072 | tf_op jit(solution)/shard_map/ppermute | solution.py:55
  62.2 6.5 %collective-permute-start.17 = (bf16[72,512]{1,0:T(8,128)(2,1)S(1)}, bf16[72,512]{1,0:T(8,128)(2,1)S(1)}, u32[]{:S(2)}, u32[]{:S(2)}) collective-permute-start(bf16[72,512]{1,0:T(8,128)(2,1)S(1)} %get-tuple-element.47), channel_id=1, source_target_pairs={{0,16},{4,20},{8,24},{12,28},{16,0},{20,4},{24,8},{28,12},{1,17},{... | collective-permute-start | bytes 221192 | tf_op jit(solution)/shard_map/ppermute | solution.py:55
  70.6 6.1 %collective-permute-start.21 = (bf16[256,256]{1,0:T(8,128)(2,1)S(1)}, bf16[256,256]{1,0:T(8,128)(2,1)S(1)}, u32[]{:S(2)}, u32[]{:S(2)}) collective-permute-start(bf16[256,256]{1,0:T(8,128)(2,1)S(1)} %shard_map.56.refs_0_), channel_id=1, source_target_pairs={{0,1},{1,3},{3,2},{2,0},{4,5},{5,7},{7,6},{6,4},{8,9},{9,11},{11,1... | collective-permute-start | bytes 393224 | tf_op jit(solution)/shard_map/ppermute | solution.py:49
  74.0 7.2 %collective-permute-start.27 = (bf16[256,256]{1,0:T(8,128)(2,1)S(1)}, bf16[256,256]{1,0:T(8,128)(2,1)S(1)}, u32[]{:S(2)}, u32[]{:S(2)}) collective-permute-start(bf16[256,256]{1,0:T(8,128)(2,1)S(1)} %shard_map.63.refs_0_), channel_id=1, source_target_pairs={{0,1},{1,3},{3,2},{2,0},{4,5},{5,7},{7,6},{6,4},{8,9},{9,11},{11,1... | collective-permute-start | bytes 393224 | tf_op jit(solution)/shard_map/ppermute | solution.py:49
  76.7 8.4 %collective-permute-start.22 = (bf16[256,256]{1,0:T(8,128)(2,1)S(1)}, bf16[256,256]{1,0:T(8,128)(2,1)S(1)}, u32[]{:S(2)}, u32[]{:S(2)}) collective-permute-start(bf16[256,256]{1,0:T(8,128)(2,1)S(1)} %collective-permute-done.21.refs_1_), channel_id=1, source_target_pairs={{0,1},{1,3},{3,2},{2,0},{4,5},{5,7},{7,6},{6,4},{8,9},{9,11},{11,1... | collective-permute-start | bytes 393224 | tf_op jit(solution)/shard_map/ppermute | solution.py:49
  81.3 7.6 %collective-permute-start.28 = (bf16[256,256]{1,0:T(8,128)(2,1)S(1)}, bf16[256,256]{1,0:T(8,128)(2,1)S(1)}, u32[]{:S(2)}, u32[]{:S(2)}) collective-permute-start(bf16[256,256]{1,0:T(8,128)(2,1)S(1)} %collective-permute-done.27.refs_1_), channel_id=1, source_target_pairs={{0,1},{1,3},{3,2},{2,0},{4,5},{5,7},{7,6},{6,4},{8,9},{9,11},{11,1... | collective-permute-start | bytes 393224 | tf_op jit(solution)/shard_map/ppermute | solution.py:49
  82.1 7.7 %collective-permute-start.26 = (bf16[256,256]{1,0:T(8,128)(2,1)S(1)}, bf16[256,256]{1,0:T(8,128)(2,1)S(1)}, u32[]{:S(2)}, u32[]{:S(2)}) collective-permute-start(bf16[256,256]{1,0:T(8,128)(2,1)S(1)} %shard_map.63.refs_0_), channel_id=1, source_target_pairs={{1,0},{3,1},{2,3},{0,2},{5,4},{7,5},{6,7},{4,6},{9,8},{11,9},{10,1... | collective-permute-start | bytes 393224 | tf_op jit(solution)/shard_map/ppermute | solution.py:49
  84.2 7.0 %collective-permute-start.20 = (bf16[256,256]{1,0:T(8,128)(2,1)S(1)}, bf16[256,256]{1,0:T(8,128)(2,1)S(1)}, u32[]{:S(2)}, u32[]{:S(2)}) collective-permute-start(bf16[256,256]{1,0:T(8,128)(2,1)S(1)} %shard_map.56.refs_0_), channel_id=1, source_target_pairs={{1,0},{3,1},{2,3},{0,2},{5,4},{7,5},{6,7},{4,6},{9,8},{11,9},{10,1... | collective-permute-start | bytes 393224 | tf_op jit(solution)/shard_map/ppermute | solution.py:49
  (7 other events, 34.8 us)
